TPU v7x, 256 devices: a whole 4x4x8 slice. The times are simulated.
256 devices in a mesh: panel: 8 (over z), rows: 32 (over y, x, core).
Axes of the slice: x: 4, y: 4, z: 8, core: 2. Of those that a mesh axis runs over, the one named last changes fastest.
Arguments:
- rhs_diag: bfloat16 [8, 8192, 128], P(None, 'rows'), may hold values from -6 to 6
- rhs_tall: bfloat16 [8, 16384, 128], P('panel', 'rows'), may hold values from -6 to 6
- diag_inverse: bfloat16 [8, 1024, 1024], P('panel'), may hold values from -0.1875 to 0.1875
- coupling: bfloat16 [8, 8192, 1024], P('panel', 'rows'), may hold values from -0.09375 to 0.09375
- tall_blocks: bfloat16 [8, 128, 128, 1024], P('panel', 'rows'), may hold values from -0.125 to 0.125
- sparsity: int32 [128, 8], P('rows', 'panel'), may hold values 0 or 1
Outputs:
- solution: float32 [8, 8, 1024, 128], P('panel', None, 'rows')
- tall_residual: float32 [8, 16384, 128], P('panel', 'rows')
All inputs are finite; a program needn't handle non-finite values. No bound on the sum of `sparsity` on one device may be relied on, other than what follows from the above.
Results may differ from a plain program's by a relative error of at most 0.0085.
Values may be sent and summed in bfloat16 or wider, within the bound.
No kernel may reach another device: no remote copies, remote signals or barrier semaphores. Data moves between devices by JAX's collectives and lax.ppermute only.
A program may use at most 64 MiB of HBM per device.

v0:
```python
import jax
import jax.numpy as jnp
from jax import lax
from jax.sharding import PartitionSpec as P


def shifted(block, axis, distance):
    devices = range(lax.axis_size(axis))
    route = [(i - distance, i) for i in devices if i - distance in devices]
    return lax.ppermute(block, axis, route)


def per_device(rhs_diag, rhs_tall, diag_inverse, coupling, tall_blocks, sparsity):
    panel_index = lax.axis_index("panel")
    rows_index = lax.axis_index("rows")
    panel_count = lax.axis_size("panel")
    rows_count = lax.axis_size("rows")
    batches, rows_here, columns = rhs_diag.shape
    panel_width = diag_inverse.shape[1]
    slice_rows = panel_width // rows_count
    blocks_here = tall_blocks.shape[1]
    block_rows = tall_blocks.shape[2]
    tall_rows = blocks_here * block_rows
    rows_panel = rows_index * rows_here // panel_width
    offset = jnp.clip(
        rows_index * rows_here - panel_index * panel_width, 0, panel_width - rows_here
    )
    inverse_cols = lax.dynamic_slice_in_dim(diag_inverse[0], offset, rows_here, 1)
    owner = rows_panel == panel_index
    is_later = rows_panel > panel_index
    coupling_here = coupling[0]
    tall_matrix = tall_blocks[0].reshape(tall_rows, panel_width)
    block_mask = jnp.repeat(sparsity[:, 0].astype(jnp.float32), block_rows)[:, None]

    def advance(tick_number, state_now):
        incoming, solutions, stored = state_now
        batch_now = tick_number - panel_index
        active = (batch_now >= 0) & (batch_now < batches)
        batch_safe = jnp.clip(batch_now, 0, batches - 1)
        rhs_now = lax.dynamic_index_in_dim(rhs_diag, batch_safe, 0, keepdims=False).astype(
            jnp.float32
        )
        reduced = (rhs_now - incoming).astype(jnp.bfloat16)
        partial_value = jnp.dot(inverse_cols, reduced, preferred_element_type=jnp.float32)
        partial_value = jnp.where(owner, partial_value, jnp.float32(0.0))
        summed_all = lax.psum(partial_value, "rows")
        own_rows = lax.dynamic_slice_in_dim(summed_all, rows_index * slice_rows, slice_rows, 0)
        solved = summed_all.astype(jnp.bfloat16)
        previous = lax.dynamic_index_in_dim(solutions, batch_safe, 0, keepdims=False)
        solutions = lax.dynamic_update_index_in_dim(
            solutions, jnp.where(active, own_rows, previous), batch_safe, 0
        )
        update = jnp.dot(coupling_here, solved, preferred_element_type=jnp.float32)
        outgoing = incoming + jnp.where(is_later, update, jnp.float32(0.0))
        earlier = lax.dynamic_index_in_dim(stored, batch_safe, 0, keepdims=False)
        stored = lax.dynamic_update_index_in_dim(
            stored, jnp.where(active, solved, earlier), batch_safe, 0
        )
        incoming = shifted(outgoing, "panel", 1)
        return (incoming, solutions, stored)

    stored = jnp.zeros((batches, panel_width, columns), jnp.bfloat16)
    initial = (
        jnp.zeros((rows_here, columns), jnp.float32),
        jnp.zeros((batches, slice_rows, columns), jnp.float32),
        stored,
    )
    tick_count = batches + panel_count - 1
    incoming, solutions, stored = lax.fori_loop(0, tick_count, advance, initial)
    tall_terms = (
        jnp.einsum("rw,bws->brs", tall_matrix, stored, preferred_element_type=jnp.float32)
        * block_mask
    )
    summed = lax.psum_scatter(tall_terms, "panel", scatter_dimension=0, tiled=True)
    tall_residual = rhs_tall.astype(jnp.float32) - summed
    return (solutions[None], tall_residual)


def solution(mesh):
    placed = (
        P(None, "rows", None),
        P("panel", "rows", None),
        P("panel", None, None),
        P("panel", "rows", None),
        P("panel", "rows", None, None),
        P("rows", "panel"),
    )
    return jax.shard_map(
        per_device,
        mesh=mesh,
        in_specs=placed,
        out_specs=(P("panel", None, "rows", None), P("panel", "rows", None)),
        check_vma=False,
    )
```

profile of v0, /device:TPU:1, one launch (start us, length us, event | category | flops | bytes accessed | tf_op | source)
XLA Modules:
  0.0 1985.4 jit_solution(4910491097746578890)
XLA Ops:
  9.9 1.6 broadcast_in_dim.57
  12.2 1920.9 %while.19 = (s32[]{:T(128)}, f32[256,128]{0,1:T(8,128)S(1)}, f32[8,32,128]{2,1,0:T(8,128)}, bf16[8,1024,128]{1,2,0:T(8,128)(2,1)}, pred[]{:T(512)}, /*index=5*/p...) while((s32[]{:T(128)}, f32[256,128]{0,1:T(8,128)S(1)}, ...), condition=%wide.region_2.3_spmd, body=%wide.region_0.2_spmd.sunk | while | flops 135041024 | bytes 8307022 | solution.py:69
  16.7 116.9 %all-reduce.2.cloned.1.call-done = f32[1024,128]{0,1:T(8,128)} async-done(((f32[1024,128]{0,1:T(8,128)}), f32[1024,128]{0,1:T(8,128)}) %all-reduce.2.cloned.1.call-update) | async-done | bytes 524304 | tf_op jit(solution)/shard_map/while/body/eval_jaxpr/psum | solution.py:46
  133.6 2.0 fusion.24
  135.6 3.2 collective-permute-start
  138.8 1.8 bitcast_dynamic-update-slice_fusion.2
  146.8 114.9 %all-reduce.2.cloned.1.call-done = f32[1024,128]{0,1:T(8,128)} async-done(((f32[1024,128]{0,1:T(8,128)}), f32[1024,128]{0,1:T(8,128)}) %all-reduce.2.cloned.1.call-update) | async-done | bytes 524304 | tf_op jit(solution)/shard_map/while/body/eval_jaxpr/psum | solution.py:46
  261.7 2.0 fusion.24
  263.7 3.2 collective-permute-start
  266.9 1.8 bitcast_dynamic-update-slice_fusion.2
  274.9 114.9 %all-reduce.2.cloned.1.call-done = f32[1024,128]{0,1:T(8,128)} async-done(((f32[1024,128]{0,1:T(8,128)}), f32[1024,128]{0,1:T(8,128)}) %all-reduce.2.cloned.1.call-update) | async-done | bytes 524304 | tf_op jit(solution)/shard_map/while/body/eval_jaxpr/psum | solution.py:46
  389.8 2.0 fusion.24
  391.8 3.2 collective-permute-start
  395.0 1.8 bitcast_dynamic-update-slice_fusion.2
  403.0 114.5 %all-reduce.2.cloned.1.call-done = f32[1024,128]{0,1:T(8,128)} async-done(((f32[1024,128]{0,1:T(8,128)}), f32[1024,128]{0,1:T(8,128)}) %all-reduce.2.cloned.1.call-update) | async-done | bytes 524304 | tf_op jit(solution)/shard_map/while/body/eval_jaxpr/psum | solution.py:46
  517.5 2.0 fusion.24
  519.5 3.2 collective-permute-start
  522.7 1.8 bitcast_dynamic-update-slice_fusion.2
  530.7 114.6 %all-reduce.2.cloned.1.call-done = f32[1024,128]{0,1:T(8,128)} async-done(((f32[1024,128]{0,1:T(8,128)}), f32[1024,128]{0,1:T(8,128)}) %all-reduce.2.cloned.1.call-update) | async-done | bytes 524304 | tf_op jit(solution)/shard_map/while/body/eval_jaxpr/psum | solution.py:46
  645.3 2.0 fusion.24
  647.3 3.2 collective-permute-start
  650.5 1.8 bitcast_dynamic-update-slice_fusion.2
  658.5 114.5 %all-reduce.2.cloned.1.call-done = f32[1024,128]{0,1:T(8,128)} async-done(((f32[1024,128]{0,1:T(8,128)}), f32[1024,128]{0,1:T(8,128)}) %all-reduce.2.cloned.1.call-update) | async-done | bytes 524304 | tf_op jit(solution)/shard_map/while/body/eval_jaxpr/psum | solution.py:46
  773.0 2.0 fusion.24
  775.0 3.2 collective-permute-start
  778.2 1.8 bitcast_dynamic-update-slice_fusion.2
  786.2 114.9 %all-reduce.2.cloned.1.call-done = f32[1024,128]{0,1:T(8,128)} async-done(((f32[1024,128]{0,1:T(8,128)}), f32[1024,128]{0,1:T(8,128)}) %all-reduce.2.cloned.1.call-update) | async-done | bytes 524304 | tf_op jit(solution)/shard_map/while/body/eval_jaxpr/psum | solution.py:46
  901.1 2.0 fusion.24
  903.1 3.2 collective-permute-start
  906.3 1.8 bitcast_dynamic-update-slice_fusion.2
  914.3 114.8 %all-reduce.2.cloned.1.call-done = f32[1024,128]{0,1:T(8,128)} async-done(((f32[1024,128]{0,1:T(8,128)}), f32[1024,128]{0,1:T(8,128)}) %all-reduce.2.cloned.1.call-update) | async-done | bytes 524304 | tf_op jit(solution)/shard_map/while/body/eval_jaxpr/psum | solution.py:46
  1029.1 2.0 fusion.24
  1031.1 3.2 collective-permute-start
  1034.3 1.8 bitcast_dynamic-update-slice_fusion.2
  1042.3 114.9 %all-reduce.2.cloned.1.call-done = f32[1024,128]{0,1:T(8,128)} async-done(((f32[1024,128]{0,1:T(8,128)}), f32[1024,128]{0,1:T(8,128)}) %all-reduce.2.cloned.1.call-update) | async-done | bytes 524304 | tf_op jit(solution)/shard_map/while/body/eval_jaxpr/psum | solution.py:46
  1157.2 2.0 fusion.24
  1159.2 3.2 collective-permute-start
  1162.4 1.8 bitcast_dynamic-update-slice_fusion.2
  1170.4 114.6 %all-reduce.2.cloned.1.call-done = f32[1024,128]{0,1:T(8,128)} async-done(((f32[1024,128]{0,1:T(8,128)}), f32[1024,128]{0,1:T(8,128)}) %all-reduce.2.cloned.1.call-update) | async-done | bytes 524304 | tf_op jit(solution)/shard_map/while/body/eval_jaxpr/psum | solution.py:46
  1284.9 2.0 fusion.24
  1287.0 3.2 collective-permute-start
  1290.2 1.8 bitcast_dynamic-update-slice_fusion.2
  1298.2 114.9 %all-reduce.2.cloned.1.call-done = f32[1024,128]{0,1:T(8,128)} async-done(((f32[1024,128]{0,1:T(8,128)}), f32[1024,128]{0,1:T(8,128)}) %all-reduce.2.cloned.1.call-update) | async-done | bytes 524304 | tf_op jit(solution)/shard_map/while/body/eval_jaxpr/psum | solution.py:46
  1413.0 2.0 fusion.24
  1415.1 3.2 collective-permute-start
  1418.3 1.8 bitcast_dynamic-update-slice_fusion.2
  1426.2 114.6 %all-reduce.2.cloned.1.call-done = f32[1024,128]{0,1:T(8,128)} async-done(((f32[1024,128]{0,1:T(8,128)}), f32[1024,128]{0,1:T(8,128)}) %all-reduce.2.cloned.1.call-update) | async-done | bytes 524304 | tf_op jit(solution)/shard_map/while/body/eval_jaxpr/psum | solution.py:46
  1540.8 2.0 fusion.24
  1542.9 3.2 collective-permute-start
  1546.0 1.8 bitcast_dynamic-update-slice_fusion.2
  1554.0 114.8 %all-reduce.2.cloned.1.call-done = f32[1024,128]{0,1:T(8,128)} async-done(((f32[1024,128]{0,1:T(8,128)}), f32[1024,128]{0,1:T(8,128)}) %all-reduce.2.cloned.1.call-update) | async-done | bytes 524304 | tf_op jit(solution)/shard_map/while/body/eval_jaxpr/psum | solution.py:46
  1668.9 2.0 fusion.24
  1670.9 3.2 collective-permute-start
  1674.1 1.8 bitcast_dynamic-update-slice_fusion.2
  1682.1 114.5 %all-reduce.2.cloned.1.call-done = f32[1024,128]{0,1:T(8,128)} async-done(((f32[1024,128]{0,1:T(8,128)}), f32[1024,128]{0,1:T(8,128)}) %all-reduce.2.cloned.1.call-update) | async-done | bytes 524304 | tf_op jit(solution)/shard_map/while/body/eval_jaxpr/psum | solution.py:46
  1796.6 2.0 fusion.24
  1798.6 3.2 collective-permute-start
  1801.8 1.8 bitcast_dynamic-update-slice_fusion.2
  1809.8 114.6 %all-reduce.2.cloned.1.call-done = f32[1024,128]{0,1:T(8,128)} async-done(((f32[1024,128]{0,1:T(8,128)}), f32[1024,128]{0,1:T(8,128)}) %all-reduce.2.cloned.1.call-update) | async-done | bytes 524304 | tf_op jit(solution)/shard_map/while/body/eval_jaxpr/psum | solution.py:46
  1924.4 2.0 fusion.24
  1926.4 3.2 collective-permute-start
  1929.6 1.8 bitcast_dynamic-update-slice_fusion.2
  1933.1 4.5 multiply_bitcast_fusion
  1938.5 37.9 %reduce-scatter.2.cloned.1.call-done = f32[1,512,128]{1,2,0:T(8,128)} async-done(((f32[8,512,128]{1,2,0:T(8,128)}), f32[1,512,128]{1,2,0:T(8,128)}) %reduce-scatter.2.cloned.1.call-update) | async-done | bytes 262160 | tf_op jit(solution)/shard_map/reduce_scatter | solution.py:74
  (226 shorter events, 97.2 us)
Async XLA Ops:
  8.0 1.6 copy-start
  8.0 4.1 copy-start.1
  12.2 121.4 %all-reduce.2.cloned.1.call-start = ((), (), s32[]{:S(2)}) async-start(), calls=%async_computation.2 | async-start | bytes 1048576 | tf_op jit(solution)/shard_map/while/body/eval_jaxpr/psum | solution.py:46
  133.6 7.0 copy-start.2
  135.6 6.6 collective-permute-start
  142.3 119.4 %all-reduce.2.cloned.1.call-start = ((), (), s32[]{:S(2)}) async-start(), calls=%async_computation.2 | async-start | bytes 1048576 | tf_op jit(solution)/shard_map/while/body/eval_jaxpr/psum | solution.py:46
  261.7 7.0 copy-start.2
  263.7 6.6 collective-permute-start
  270.3 119.4 %all-reduce.2.cloned.1.call-start = ((), (), s32[]{:S(2)}) async-start(), calls=%async_computation.2 | async-start | bytes 1048576 | tf_op jit(solution)/shard_map/while/body/eval_jaxpr/psum | solution.py:46
  389.8 7.0 copy-start.2
  391.8 6.6 collective-permute-start
  398.4 119.1 %all-reduce.2.cloned.1.call-start = ((), (), s32[]{:S(2)}) async-start(), calls=%async_computation.2 | async-start | bytes 1048576 | tf_op jit(solution)/shard_map/while/body/eval_jaxpr/psum | solution.py:46
  517.5 7.0 copy-start.2
  519.5 6.6 collective-permute-start
  526.2 119.1 %all-reduce.2.cloned.1.call-start = ((), (), s32[]{:S(2)}) async-start(), calls=%async_computation.2 | async-start | bytes 1048576 | tf_op jit(solution)/shard_map/while/body/eval_jaxpr/psum | solution.py:46
  645.3 7.1 copy-start.2
  647.3 6.6 collective-permute-start
  653.9 119.1 %all-reduce.2.cloned.1.call-start = ((), (), s32[]{:S(2)}) async-start(), calls=%async_computation.2 | async-start | bytes 1048576 | tf_op jit(solution)/shard_map/while/body/eval_jaxpr/psum | solution.py:46
  773.0 7.0 copy-start.2
  775.0 6.6 collective-permute-start
  781.7 119.4 %all-reduce.2.cloned.1.call-start = ((), (), s32[]{:S(2)}) async-start(), calls=%async_computation.2 | async-start | bytes 1048576 | tf_op jit(solution)/shard_map/while/body/eval_jaxpr/psum | solution.py:46
  901.1 7.0 copy-start.2
  903.1 6.6 collective-permute-start
  909.7 119.4 %all-reduce.2.cloned.1.call-start = ((), (), s32[]{:S(2)}) async-start(), calls=%async_computation.2 | async-start | bytes 1048576 | tf_op jit(solution)/shard_map/while/body/eval_jaxpr/psum | solution.py:46
  1029.1 7.0 copy-start.2
  1031.1 6.6 collective-permute-start
  1037.8 119.4 %all-reduce.2.cloned.1.call-start = ((), (), s32[]{:S(2)}) async-start(), calls=%async_computation.2 | async-start | bytes 1048576 | tf_op jit(solution)/shard_map/while/body/eval_jaxpr/psum | solution.py:46
  1157.2 7.0 copy-start.2
  1159.2 6.6 collective-permute-start
  1165.8 119.1 %all-reduce.2.cloned.1.call-start = ((), (), s32[]{:S(2)}) async-start(), calls=%async_computation.2 | async-start | bytes 1048576 | tf_op jit(solution)/shard_map/while/body/eval_jaxpr/psum | solution.py:46
  1284.9 7.0 copy-start.2
  1287.0 6.6 collective-permute-start
  1293.6 119.4 %all-reduce.2.cloned.1.call-start = ((), (), s32[]{:S(2)}) async-start(), calls=%async_computation.2 | async-start | bytes 1048576 | tf_op jit(solution)/shard_map/while/body/eval_jaxpr/psum | solution.py:46
  1413.0 7.0 copy-start.2
  1415.1 6.6 collective-permute-start
  1421.7 119.1 %all-reduce.2.cloned.1.call-start = ((), (), s32[]{:S(2)}) async-start(), calls=%async_computation.2 | async-start | bytes 1048576 | tf_op jit(solution)/shard_map/while/body/eval_jaxpr/psum | solution.py:46
  1540.8 7.0 copy-start.2
  1542.9 6.6 collective-permute-start
  1549.5 119.4 %all-reduce.2.cloned.1.call-start = ((), (), s32[]{:S(2)}) async-start(), calls=%async_computation.2 | async-start | bytes 1048576 | tf_op jit(solution)/shard_map/while/body/eval_jaxpr/psum | solution.py:46
  1668.9 7.0 copy-start.2
  1670.9 6.6 collective-permute-start
  1677.5 119.1 %all-reduce.2.cloned.1.call-start = ((), (), s32[]{:S(2)}) async-start(), calls=%async_computation.2 | async-start | bytes 1048576 | tf_op jit(solution)/shard_map/while/body/eval_jaxpr/psum | solution.py:46
  1796.6 7.0 copy-start.2
  1798.6 6.6 collective-permute-start
  1805.3 119.1 %all-reduce.2.cloned.1.call-start = ((), (), s32[]{:S(2)}) async-start(), calls=%async_computation.2 | async-start | bytes 1048576 | tf_op jit(solution)/shard_map/while/body/eval_jaxpr/psum | solution.py:46
  1924.4 7.0 copy-start.2
  1926.4 6.6 collective-permute-start
  1933.1 43.4 %reduce-scatter.2.cloned.1.call-start = ((), (), s32[]{:S(2)}) async-start(), calls=%async_computation.1 | async-start | bytes 2359296 | tf_op jit(solution)/shard_map/reduce_scatter | solution.py:74
  1937.5 0.9 copy-start.3
Sparse Core Ops, SparseCore 0:
  16.2 117.3 all-reduce.1
  146.3 115.3 all-reduce.1
  274.4 115.3 all-reduce.1
  402.1 115.3 all-reduce.1
  529.9 115.3 all-reduce.1
  657.6 115.3 all-reduce.1
  785.7 115.3 all-reduce.1
  913.7 115.3 all-reduce.1
  1041.8 115.3 all-reduce.1
  1169.5 115.3 all-reduce.1
  1297.6 115.3 all-reduce.1
  1425.4 115.3 all-reduce.1
  1553.5 115.3 all-reduce.1
  1681.2 115.3 all-reduce.1
  1809.0 115.3 all-reduce.1
Sparse Core Ops, SparseCore 1:
  1937.6 38.8 reduce-scatter.1
where the time goes:
time: 1990 us
  waiting for transfers between devices  1760 us (88%)
  local copies, waits for them, and re-layouts  66.1 us (3%)
  matrix products  51.9 us (3%)
  starting transfers between devices  47.6 us (2%)
  other arithmetic  42.9 us (2%)
    psum x15, waiting for transfers between devices, advance(): summed_all = lax.psum(partial_value, 'rows')  1720 us
    ppermute x15, starting transfers between devices, shifted(): return lax.ppermute(block, axis, route)  47.6 us
  transfers between devices with their start and end apart: 31, of which 16 were waited for; matrix products, arithmetic and copies ran while one was open for 4% of the time, Pallas kernels for 0%

commit v1 on v0

v1 whole, which is shorter than its diff:
```python
import jax
import jax.numpy as jnp
from jax import lax
from jax.sharding import Mesh
from jax.sharding import PartitionSpec as P

F32 = jnp.float32
BF16 = jnp.bfloat16
ROWS = ("chip", "core")


def times(left, weight):
    return lax.dot_general(
        left, weight, (((1,), (1,)), ((), ())), preferred_element_type=F32
    )


def per_device(rhs_diag, rhs_tall, diag_inverse, coupling, tall_blocks, sparsity):
    z = lax.axis_index("panel")
    rows_index = lax.axis_index(ROWS)
    core = lax.axis_index("core")
    panels = lax.axis_size("panel")
    chips = lax.axis_size("chip")
    groups = lax.axis_size(ROWS)
    batches, rows_here, columns = rhs_diag.shape
    width = diag_inverse.shape[1]
    owners = width // rows_here
    share = batches * columns // groups
    parts = columns // share
    slice_rows = width // groups

    whole = lax.all_gather(coupling[0], ROWS).reshape(panels, width, width)

    pieces = rhs_diag.reshape(batches, rows_here, parts, share)
    pieces = pieces.transpose(0, 2, 3, 1).reshape(groups, share, rows_here)
    pieces = lax.all_to_all(pieces, ROWS, 0, 0, tiled=True)
    own = lax.dynamic_slice_in_dim(pieces, owners * z, owners, 0)
    own_rhs = own.transpose(1, 0, 2).reshape(share, width).astype(F32)

    inverse = diag_inverse[0]
    following = lax.dynamic_index_in_dim(
        whole, jnp.minimum(z + 1, panels - 1), 0, keepdims=False
    )

    def weight_of(index):
        return lax.dynamic_index_in_dim(
            whole, jnp.clip(index, 0, panels - 1), 0, keepdims=False
        )

    zero = jnp.zeros((share, width), F32)
    solved = jnp.zeros((share, width), BF16)
    near = zero
    even, odd = [zero, zero], [zero]
    for k in range(panels):
        reduced = (own_rhs - (near + even[k])).astype(BF16)
        fresh = times(reduced, inverse).astype(BF16)
        solved = jnp.where(z == k, fresh, solved)
        if k == panels - 1:
            break
        into_odd = odd[k]
        into_even = even[k + 1]
        near = lax.ppermute(times(fresh, following) + into_odd, "panel", [(k, k + 1)])
        senders = range(max(0, 2 * k - panels + 2), min(k, panels - 3) + 1)
        if k < panels - 2:
            far_odd = into_odd + times(solved, weight_of(2 * k + 1 - z))
            far_even = into_even + times(solved, weight_of(2 * k + 2 - z))
            both = jnp.stack([far_odd, far_even]).astype(BF16)
            both = lax.ppermute(both, "panel", [(s, s + 2) for s in senders])
            odd.append(both[0].astype(F32))
            even.append(both[1].astype(F32))
    mine = lax.all_to_all(
        jnp.broadcast_to(solved[None], (chips, share, width)), "chip", 0, 0, tiled=True
    )
    other = lax.ppermute(mine, "core", [(0, 1), (1, 0)])
    first = jnp.where(core == 0, mine, other)
    second = jnp.where(core == 0, other, mine)
    full = jnp.stack([first, second], 1).reshape(batches, columns, width)

    own_rows = lax.dynamic_slice_in_dim(full, rows_index * slice_rows, slice_rows, 2)
    solution_rows = own_rows.transpose(0, 2, 1).astype(F32)

    blocks, block_rows = tall_blocks.shape[1], tall_blocks.shape[2]
    tall = tall_blocks[0].reshape(blocks * block_rows, width)
    mask = jnp.repeat(sparsity[:, 0].astype(F32), block_rows)[:, None]
    terms = jnp.einsum("rw,bsw->brs", tall, full, preferred_element_type=F32) * mask
    summed = lax.psum_scatter(terms, "panel", scatter_dimension=0, tiled=True)
    return solution_rows[None], rhs_tall.astype(F32) - summed


def solution(mesh):
    panels, rows = mesh.devices.shape
    split = Mesh(mesh.devices.reshape(panels, rows // 2, 2), ("panel", "chip", "core"))
    placed = (
        P(None, ROWS, None),
        P("panel", ROWS, None),
        P("panel", None, None),
        P("panel", ROWS, None),
        P("panel", ROWS, None, None),
        P(ROWS, "panel"),
    )
    return jax.shard_map(
        per_device,
        mesh=split,
        in_specs=placed,
        out_specs=(P("panel", None, ROWS, None), P("panel", ROWS, None)),
        check_vma=False,
    )
```

time: 1990 us -> 287 us (0.14)
  waiting for transfers between devices: 1760 us -> 141 us
  local copies, waits for them, and re-layouts: 66.1 us -> 6.27 us
  other arithmetic: 42.9 us -> 3.79 us
    psum x15 -> x0, waiting for transfers between devices: 1720 us -> none  [advance(): summed_all = lax.psum(partial_value, 'rows')]
    all_gather x0 -> x1, waiting for transfers between devices: none -> 61.5 us  [per_device(): whole = lax.all_gather(coupling[0], ROWS).reshape(panels, width, width)]
    dynamic_slice x76 -> x0, local copies, waits for them, and re-layouts: 50.8 us -> none  [the longest x30 21.8 us: advance(): lax.dynamic_index_in_dim(solutions, batch_safe, 0, keepdims=False)]
    dynamic_update_slice x15 -> x0, other arithmetic: 27.3 us -> none  [advance(): lax.dynamic_update_index_in_dim(stored, jnp.where(active, solved, earlier...]
    reduce_scatter x1, waiting for transfers between devices: 37.9 us -> 59.2 us  [per_device(): summed = lax.psum_scatter(terms, 'panel', scatter_dimension=0, tiled=True)]
    ppermute x15 -> x14, starting transfers between devices: 47.6 us -> 37.7 us  [the longest x6 25.1 us: per_device(): both = lax.ppermute(both, 'panel', [(s, s + 2) for s in senders])]
    dot_general x31 -> x28, matrix products: 51.9 us -> 52.3 us  [the longest x27 49.8 us: times(): lax.dot_general(left, weight, (((1,), (1,)), ((), ())), preferred_element...]
  transfers between devices with their start and end apart: 31 -> 17, of which waited for: 16 -> 8; matrix products, arithmetic and copies ran while one was open for 4% -> 9% of each run, Pallas kernels for 0% -> 0%
where the time goes in v1:
time: 287 us; the launch traced here: 282 us
  waiting for transfers between devices  141 us (49%)
  matrix products  52.3 us (18%)
  starting transfers between devices  46.3 us (16%)
  blocking collectives  17.5 us (6%)
  between operations  14.5 us (5%)
  local copies, waits for them, and re-layouts  6.27 us (2%)
  other arithmetic  3.79 us (1%)
    all_gather x1, waiting for transfers between devices, per_device(): whole = lax.all_gather(coupling[0], ROWS).reshape(panels, width, width)  61.5 us
    reduce_scatter x1, waiting for transfers between devices, per_device(): summed = lax.psum_scatter(terms, 'panel', scatter_dimension=0, tiled=True)  59.2 us
    dot_general x27, matrix products, times(): lax.dot_general(left, weight, (((1,), (1,)), ((), ())), preferred_element...  49.8 us
    ppermute x6, starting transfers between devices, per_device(): both = lax.ppermute(both, 'panel', [(s, s + 2) for s in senders])  25.1 us
    all_to_all x1, blocking collectives, per_device(): lax.all_to_all(jnp.broadcast_to(solved[None], (chips, share, width)), 'ch...  17.5 us
    all_to_all x1, waiting for transfers between devices, per_device(): pieces = lax.all_to_all(pieces, ROWS, 0, 0, tiled=True)  11.5 us
    all_to_all x1, starting transfers between devices, per_device(): pieces = lax.all_to_all(pieces, ROWS, 0, 0, tiled=True)  8.59 us
    ppermute x7, starting transfers between devices, per_device(): lax.ppermute(times(fresh, following) + into_odd, 'panel', [(k, k + 1)])  7.2 us
  transfers between devices with their start and end apart: 17, of which 8 were waited for; matrix products, arithmetic and copies ran while one was open for 9% of the time, Pallas kernels for 0%

profile of v1, /device:TPU:1, one launch (start us, length us, event | category | flops | bytes accessed | tf_op | source)
XLA Modules:
  0.0 282.2 jit_solution(6874435012670674414)
XLA Ops:
  7.2 0.7 all-gather.2.cloned.1.call-update
  7.9 2.1 copy.19
  10.0 8.6 %all-to-all-start = ((bf16[32,32,256]{2,1,0:T(8,128)(2,1)}), bf16[32,32,256]{2,1,0:T(8,128)(2,1)S(1)}, u32[]{:S(2)}, u32[]{:S(2)}) async-start(bf16[32,32,256]{2,1,0:T(8,128)(2,1)} %bitcast.2), calls=%async_computation | async-start | bytes 1048576 | tf_op jit(solution)/shard_map/all_to_all | solution.py:36
  18.6 11.5 %all-to-all-done = bf16[32,32,256]{2,1,0:T(8,128)(2,1)S(1)} async-done(((bf16[32,32,256]{2,1,0:T(8,128)(2,1)}), bf16[32,32,256]{2,1,0:T(8,128)(2,1)S(1)}, u32[]{:S(2)}, u32[]{:S(2)}) %all-to-all-start) | async-done | bytes 524320 | tf_op jit(solution)/shard_map/all_to_all | solution.py:36
  30.1 0.7 fusion.147
  30.9 61.5 %all-gather.2.cloned.1.call-done = bf16[32,256,1024]{2,1,0:T(8,128)(2,1)} async-done(((bf16[1,256,1024]{2,1,0:T(8,128)(2,1)}), bf16[32,256,1024]{2,1,0:T(8,128)(2,1)}) %all-gather.2.cloned.1.call-update) | async-done | bytes 16777232 | tf_op jit(solution)/shard_map/all_gather | solution.py:32
  92.3 2.3 fusion.36
  94.6 3.2 %collective-permute-start = (f32[32,1024]{1,0:T(8,128)S(1)}, f32[32,1024]{1,0:T(8,128)S(1)}, u32[]{:S(2)}, u32[]{:S(2)}) collective-permute-start(f32[32,1024]{1,0:T(8,128)S(1)} %fusion.36), channel_id=1, source_target_pairs={{0,32},{1,33},{2,34},{3,35},{4,36},{5,37},{6,38},{7,39},{8,40},{9,... | collective-permute-start | bytes 393224 | tf_op jit(solution)/shard_map/ppermute | solution.py:62
  97.8 2.3 fusion.201
  100.1 2.3 fusion.204
  102.5 1.7 collective-permute-start.1
  104.2 0.7 broadcast_select_fusion.4
  104.9 1.9 collective-permute-done.1
  106.8 2.3 fusion.66
  109.1 0.7 collective-permute-start.2
  109.8 2.3 fusion.171
  112.1 2.3 fusion.174
  114.4 5.6 %collective-permute-start.3 = (bf16[2,32,1024]{2,1,0:T(8,128)(2,1)S(1)}, bf16[2,32,1024]{2,1,0:T(8,128)(2,1)S(1)}, u32[]{:S(2)}, u32[]{:S(2)}) collective-permute-start(bf16[2,32,1024]{2,1,0:T(8,128)(2,1)S(1)} %pad_maximum_fusion.2), channel_id=1, source_target_pairs={{0,64},{32,96},{1,65},{33,97},{2,66},{34,98},{3,67},{35,99},{4,68}... | collective-permute-start | bytes 393224 | tf_op jit(solution)/shard_map/ppermute | solution.py:68
  120.1 0.7 fusion.153
  120.8 1.2 collective-permute-done.3
  122.0 2.3 fusion.69
  124.3 0.7 collective-permute-start.4
  125.0 0.7 broadcast_select_fusion.2
  125.8 2.3 fusion.177
  128.1 2.3 fusion.180
  130.4 11.6 %collective-permute-start.5 = (bf16[2,32,1024]{2,1,0:T(8,128)(2,1)S(1)}, bf16[2,32,1024]{2,1,0:T(8,128)(2,1)S(1)}, u32[]{:S(2)}, u32[]{:S(2)}) collective-permute-start(bf16[2,32,1024]{2,1,0:T(8,128)(2,1)S(1)} %pad_maximum_fusion.3), channel_id=1, source_target_pairs={{0,64},{32,96},{64,128},{1,65},{33,97},{65,129},{2,66},{34,98},{66... | collective-permute-start | bytes 393224 | tf_op jit(solution)/shard_map/ppermute | solution.py:68
  142.0 1.9 collective-permute-done.5
  143.9 2.3 fusion.72
  146.2 0.7 collective-permute-start.6
  146.9 2.3 fusion.183
  149.2 2.3 fusion.186
  151.6 4.8 %collective-permute-start.7 = (bf16[2,32,1024]{2,1,0:T(8,128)(2,1)S(1)}, bf16[2,32,1024]{2,1,0:T(8,128)(2,1)S(1)}, u32[]{:S(2)}, u32[]{:S(2)}) collective-permute-start(bf16[2,32,1024]{2,1,0:T(8,128)(2,1)S(1)} %pad_maximum_fusion.4), channel_id=1, source_target_pairs={{0,64},{32,96},{64,128},{96,160},{1,65},{33,97},{65,129},{97,161},... | collective-permute-start | bytes 393224 | tf_op jit(solution)/shard_map/ppermute | solution.py:68
  156.4 0.7 fusion.159
  157.1 1.2 collective-permute-done.7
  158.3 2.3 fusion.75
  160.6 0.7 collective-permute-start.8
  161.3 0.7 broadcast_select_fusion
  162.0 2.3 fusion.189
  164.3 2.3 fusion.192
  166.7 0.8 collective-permute-start.9
  167.6 2.3 fusion.78
  169.9 0.7 collective-permute-start.10
  170.6 2.3 fusion.195
  172.9 2.3 fusion.198
  175.2 0.7 collective-permute-start.11
  175.9 0.7 fusion.165
  176.7 2.3 convert_add_fusion.6
  179.0 0.7 collective-permute-start.12
  179.7 0.7 fusion.207
  180.4 0.1 broadcast_in_dim.19
  180.6 17.5 %all_to_all.10 = bf16[16,32,1024]{2,1,0:T(8,128)(2,1)S(1)} all-to-all(bf16[16,32,1024]{2,1,0:T(8,128)(2,1)S(1)} %broadcast_in_dim.19), channel_id=1, replica_groups=mesh['panel'=8,'chip'=16,'core'=2] {'chip'}, dimensions={0} | all-to-all | bytes 2097152 | tf_op jit(solution)/shard_map/all_to_all | solution.py:71
  198.1 5.3 %collective-permute-start.13 = (bf16[16,32,1024]{2,1,0:T(8,128)(2,1)S(1)}, bf16[16,32,1024]{2,1,0:T(8,128)(2,1)}, u32[]{:S(2)}, u32[]{:S(2)}) collective-permute-start(bf16[16,32,1024]{2,1,0:T(8,128)(2,1)S(1)} %all_to_all.10), channel_id=1, source_target_pairs={{0,1},{1,0},{2,3},{3,2},{4,5},{5,4},{6,7},{7,6},{8,9},{9,8},{10,11... | collective-permute-start | bytes 3145736 | tf_op jit(solution)/shard_map/ppermute | solution.py:74
  203.5 2.3 collective-permute-done.13
  205.8 1.4 select_bitcast_fusion.1
  207.2 0.2 pad_maximum_fusion
  207.4 1.3 copy-done.1
  208.7 2.6 multiply_bitcast_fusion
  211.4 0.9 copy-done.2
  212.2 0.1 copy.22
  212.4 1.1 convert_bitcast_fusion
  213.5 0.8 copy.23
  214.3 59.2 %reduce-scatter.2.cloned.1.call-done = f32[1,512,128]{1,2,0:T(8,128)} async-done(((f32[8,512,128]{1,2,0:T(8,128)}), f32[1,512,128]{1,2,0:T(8,128)}) %reduce-scatter.2.cloned.1.call-update) | async-done | bytes 262160 | tf_op jit(solution)/shard_map/reduce_scatter | solution.py:86
  273.5 1.0 convert_subtract_fusion.7
  274.5 0.8 copy.24
  (30 shorter events, 0.4 us)
Async XLA Ops:
  7.2 23.0 %copy-start = (bf16[1,1024,1024]{2,1,0:T(8,128)(2,1)S(1)}, bf16[1,1024,1024]{2,1,0:T(8,128)(2,1)}, u32[]{:S(2)}) copy-start(bf16[1,1024,1024]{2,1,0:T(8,128)(2,1)} %param.8) | copy-start | bytes 6291460
  7.2 85.1 %all-gather.2.cloned.1.call-start = ((), (), s32[]{:S(2)}) async-start(), calls=%async_computation.3 | async-start | bytes 17301504 | tf_op jit(solution)/shard_map/all_gather | solution.py:32
  10.0 20.1 %all-to-all-start = ((bf16[32,32,256]{2,1,0:T(8,128)(2,1)}), bf16[32,32,256]{2,1,0:T(8,128)(2,1)S(1)}, u32[]{:S(2)}, u32[]{:S(2)}) async-start(bf16[32,32,256]{2,1,0:T(8,128)(2,1)} %bitcast.2), calls=%async_computation | async-start | bytes 1048576 | tf_op jit(solution)/shard_map/all_to_all | solution.py:36
  18.6 255.0 %reduce-scatter.2.cloned.1.call-start = ((), (), s32[]{:S(2)}) async-start(), calls=%async_computation.4 | async-start | bytes 2359296 | tf_op jit(solution)/shard_map/reduce_scatter | solution.py:86
  94.6 9.5 %collective-permute-start = (f32[32,1024]{1,0:T(8,128)S(1)}, f32[32,1024]{1,0:T(8,128)S(1)}, u32[]{:S(2)}, u32[]{:S(2)}) collective-permute-start(f32[32,1024]{1,0:T(8,128)S(1)} %fusion.36), channel_id=1, source_target_pairs={{0,32},{1,33},{2,34},{3,35},{4,36},{5,37},{6,38},{7,39},{8,40},{9,... | collective-permute-start | bytes 393224 | tf_op jit(solution)/shard_map/ppermute | solution.py:62
  102.5 4.3 %collective-permute-start.1 = (bf16[2,32,1024]{2,1,0:T(8,128)(2,1)S(1)}, bf16[2,32,1024]{2,1,0:T(8,128)(2,1)S(1)}, u32[]{:S(2)}, u32[]{:S(2)}) collective-permute-start(bf16[2,32,1024]{2,1,0:T(8,128)(2,1)S(1)} %pad_maximum_fusion.1), channel_id=1, source_target_pairs={{0,64},{1,65},{2,66},{3,67},{4,68},{5,69},{6,70},{7,71},{8,72},{9,... | collective-permute-start | bytes 393224 | tf_op jit(solution)/shard_map/ppermute | solution.py:68
  109.1 11.0 %collective-permute-start.2 = (f32[32,1024]{1,0:T(8,128)S(1)}, f32[32,1024]{1,0:T(8,128)S(1)}, u32[]{:S(2)}, u32[]{:S(2)}) collective-permute-start(f32[32,1024]{1,0:T(8,128)S(1)} %fusion.66), channel_id=1, source_target_pairs={{32,64},{33,65},{34,66},{35,67},{36,68},{37,69},{38,70},{39,71},{4... | collective-permute-start | bytes 393224 | tf_op jit(solution)/shard_map/ppermute | solution.py:62
  114.4 7.6 %collective-permute-start.3 = (bf16[2,32,1024]{2,1,0:T(8,128)(2,1)S(1)}, bf16[2,32,1024]{2,1,0:T(8,128)(2,1)S(1)}, u32[]{:S(2)}, u32[]{:S(2)}) collective-permute-start(bf16[2,32,1024]{2,1,0:T(8,128)(2,1)S(1)} %pad_maximum_fusion.2), channel_id=1, source_target_pairs={{0,64},{32,96},{1,65},{33,97},{2,66},{34,98},{3,67},{35,99},{4,68}... | collective-permute-start | bytes 393224 | tf_op jit(solution)/shard_map/ppermute | solution.py:68
  124.3 0.7 collective-permute-start.4
  130.4 13.5 %collective-permute-start.5 = (bf16[2,32,1024]{2,1,0:T(8,128)(2,1)S(1)}, bf16[2,32,1024]{2,1,0:T(8,128)(2,1)S(1)}, u32[]{:S(2)}, u32[]{:S(2)}) collective-permute-start(bf16[2,32,1024]{2,1,0:T(8,128)(2,1)S(1)} %pad_maximum_fusion.3), channel_id=1, source_target_pairs={{0,64},{32,96},{64,128},{1,65},{33,97},{65,129},{2,66},{34,98},{66... | collective-permute-start | bytes 393224 | tf_op jit(solution)/shard_map/ppermute | solution.py:68
  146.2 10.1 %collective-permute-start.6 = (f32[32,1024]{1,0:T(8,128)S(1)}, f32[32,1024]{1,0:T(8,128)S(1)}, u32[]{:S(2)}, u32[]{:S(2)}) collective-permute-start(f32[32,1024]{1,0:T(8,128)S(1)} %fusion.72), channel_id=1, source_target_pairs={{96,128},{97,129},{98,130},{99,131},{100,132},{101,133},{102,134},... | collective-permute-start | bytes 393224 | tf_op jit(solution)/shard_map/ppermute | solution.py:62
  151.6 6.7 %collective-permute-start.7 = (bf16[2,32,1024]{2,1,0:T(8,128)(2,1)S(1)}, bf16[2,32,1024]{2,1,0:T(8,128)(2,1)S(1)}, u32[]{:S(2)}, u32[]{:S(2)}) collective-permute-start(bf16[2,32,1024]{2,1,0:T(8,128)(2,1)S(1)} %pad_maximum_fusion.4), channel_id=1, source_target_pairs={{0,64},{32,96},{64,128},{96,160},{1,65},{33,97},{65,129},{97,161},... | collective-permute-start | bytes 393224 | tf_op jit(solution)/shard_map/ppermute | solution.py:68
  160.6 0.7 collective-permute-start.8
  166.7 0.9 collective-permute-start.9
  169.9 6.0 %collective-permute-start.10 = (f32[32,1024]{1,0:T(8,128)S(1)}, f32[32,1024]{1,0:T(8,128)S(1)}, u32[]{:S(2)}, u32[]{:S(2)}) collective-permute-start(f32[32,1024]{1,0:T(8,128)S(1)} %fusion.78), channel_id=1, source_target_pairs={{160,192},{161,193},{162,194},{163,195},{164,196},{165,197},{166,1... | collective-permute-start | bytes 393224 | tf_op jit(solution)/shard_map/ppermute | solution.py:62
  175.2 1.4 collective-permute-start.11
  179.0 0.7 collective-permute-start.12
  180.4 23.0 %copy-start.4 = (s32[4,1]{0,1:T(1,128)S(1)}, s32[4,1]{0,1:T(1,128)}, u32[]{:S(2)}) copy-start(s32[4,1]{0,1:T(1,128)} %param.11) | copy-start | bytes 52
  198.1 7.7 %collective-permute-start.13 = (bf16[16,32,1024]{2,1,0:T(8,128)(2,1)S(1)}, bf16[16,32,1024]{2,1,0:T(8,128)(2,1)}, u32[]{:S(2)}, u32[]{:S(2)}) collective-permute-start(bf16[16,32,1024]{2,1,0:T(8,128)(2,1)S(1)} %all_to_all.10), channel_id=1, source_target_pairs={{0,1},{1,0},{2,3},{3,2},{4,5},{5,4},{6,7},{7,6},{8,9},{9,8},{10,11... | collective-permute-start | bytes 3145736 | tf_op jit(solution)/shard_map/ppermute | solution.py:74
  207.2 1.6 copy-start.3
  207.4 1.3 copy-start.1
  211.3 0.9 copy-start.2
Sparse Core Ops, SparseCore 0:
  10.6 81.7 all-gather.1
  211.5 61.9 reduce-scatter.1

commit v2 on v1

--- a/solution.py
+++ b/solution.py
@@ -1,18 +1,88 @@
 import jax
 import jax.numpy as jnp
 from jax import lax
+from jax.experimental import pallas as pl
+from jax.experimental.pallas import tpu as pltpu
 from jax.sharding import Mesh
 from jax.sharding import PartitionSpec as P
 
 F32 = jnp.float32
 BF16 = jnp.bfloat16
 ROWS = ("chip", "core")
+FAR_SENDS = {
+    1: ((3, (0, 1)), (6, (0, 1))),
+    2: ((4, (0, 1, 2)), (5, (0, 1, 2)), (7, (0,))),
+    3: ((3, (2, 3)), (4, (3,))),
+    4: ((3, (4,)),),
+}
 
 
 def times(left, weight):
     return lax.dot_general(
         left, weight, (((1,), (1,)), ((), ())), preferred_element_type=F32
     )
+
+
+def later_body(
+    place_ref, solved_ref, whole_ref, kept_ref, out_ref, weights, products, loaded, stored
+):
+    z = place_ref[0]
+    count, panels = weights.shape[0], whole_ref.shape[0]
+
+    def load(i):
+        return pltpu.make_async_copy(whole_ref.at[z + 3 + i], weights.at[i], loaded.at[i])
+
+    def store(i):
+        return pltpu.make_async_copy(products.at[i], out_ref.at[i], stored.at[i])
+
+    @pl.when(place_ref[1] == 1)
+    def _():
+        for i in range(count):
+
+            @pl.when(z + 3 + i < panels)
+            def _():
+                load(i).start()
+
+        for i in range(count):
+
+            @pl.when(z + 3 + i < panels)
+            def _():
+                load(i).wait()
+                products[i] = times(solved_ref[...], weights[i])
+                store(i).start()
+
+        for i in range(count):
+
+            @pl.when(z + 3 + i < panels)
+            def _():
+                store(i).wait()
+
+
+def later_products(z, turn, solved, whole, kept):
+    count, share, width = kept.shape
+    return pl.pallas_call(
+        later_body,
+        grid_spec=pltpu.PrefetchScalarGridSpec(
+            num_scalar_prefetch=1,
+            grid=(1,),
+            in_specs=[
+                pl.BlockSpec((share, width), lambda i, p: (0, 0)),
+                pl.BlockSpec(memory_space=pl.ANY),
+                pl.BlockSpec(memory_space=pl.ANY),
+            ],
+            out_specs=pl.BlockSpec(memory_space=pl.ANY),
+            scratch_shapes=[
+                pltpu.VMEM((count, width, width), BF16),
+                pltpu.VMEM((count, share, width), F32),
+                pltpu.SemaphoreType.DMA((count,)),
+                pltpu.SemaphoreType.DMA((count,)),
+            ],
+        ),
+        out_shape=jax.ShapeDtypeStruct(kept.shape, F32),
+        input_output_aliases={3: 0},
+        compiler_params=pltpu.CompilerParams(vmem_limit_bytes=16 * 2**20),
+        name="later_products",
+    )(jnp.stack([z, turn.astype(jnp.int32)]), solved, whole, kept)
 
 
 def per_device(rhs_diag, rhs_tall, diag_inverse, coupling, tall_blocks, sparsity):
@@ -38,36 +108,36 @@
     own_rhs = own.transpose(1, 0, 2).reshape(share, width).astype(F32)
 
     inverse = diag_inverse[0]
-    following = lax.dynamic_index_in_dim(
-        whole, jnp.minimum(z + 1, panels - 1), 0, keepdims=False
-    )
+    def ahead(distance):
+        index = jnp.minimum(z + distance, panels - 1)
+        return lax.dynamic_index_in_dim(whole, index, 0, keepdims=False)
 
-    def weight_of(index):
-        return lax.dynamic_index_in_dim(
-            whole, jnp.clip(index, 0, panels - 1), 0, keepdims=False
-        )
+    following, second = lax.optimization_barrier((ahead(1), ahead(2)))
 
-    zero = jnp.zeros((share, width), F32)
     solved = jnp.zeros((share, width), BF16)
-    near = zero
-    even, odd = [zero, zero], [zero]
+    kept = jnp.zeros((panels - 3, share, width), F32)
+    arrivals = [[] for _ in range(panels)]
+
+    def send(value, senders, distance):
+        moved = lax.ppermute(value, "panel", [(s, s + distance) for s in senders])
+        for s in senders:
+            arrivals[s + distance].append(moved)
+
     for k in range(panels):
-        reduced = (own_rhs - (near + even[k])).astype(BF16)
-        fresh = times(reduced, inverse).astype(BF16)
+        earlier = sum(arrivals[k], jnp.zeros((share, width), F32))
+        fresh = times((own_rhs - earlier).astype(BF16), inverse).astype(BF16)
         solved = jnp.where(z == k, fresh, solved)
         if k == panels - 1:
             break
-        into_odd = odd[k]
-        into_even = even[k + 1]
-        near = lax.ppermute(times(fresh, following) + into_odd, "panel", [(k, k + 1)])
-        senders = range(max(0, 2 * k - panels + 2), min(k, panels - 3) + 1)
+        near = times(fresh, following)
+        near, fresh = lax.optimization_barrier((near, fresh))
+        send(near, [k], 1)
         if k < panels - 2:
-            far_odd = into_odd + times(solved, weight_of(2 * k + 1 - z))
-            far_even = into_even + times(solved, weight_of(2 * k + 2 - z))
-            both = jnp.stack([far_odd, far_even]).astype(BF16)
-            both = lax.ppermute(both, "panel", [(s, s + 2) for s in senders])
-            odd.append(both[0].astype(F32))
-            even.append(both[1].astype(F32))
+            send(times(fresh, second), [k], 2)
+        if k < panels - 3:
+            kept = later_products(z, z == k, fresh, whole, kept)
+        for distance, senders in FAR_SENDS.get(k, ()):
+            send(kept[distance - 3], senders, distance)
     mine = lax.all_to_all(
         jnp.broadcast_to(solved[None], (chips, share, width)), "chip", 0, 0, tiled=True
     )

time: 287 us -> 247 us (0.86)
  matrix products: 52.3 us -> 21 us
  waiting for transfers between devices: 141 us -> 126 us
  starting transfers between devices: 46.3 us -> 31.9 us
  local copies, waits for them, and re-layouts: 6.27 us -> 15.5 us
  Pallas kernels: 0 us -> 8.52 us
  blocking collectives: 17.5 us -> 20.8 us
    dot_general x27 -> x21, matrix products: 49.8 us -> 16.8 us  [times(): lax.dot_general(left, weight, (((1,), (1,)), ((), ())), preferred_element...]
    ppermute x13 -> x21, starting transfers between devices: 32.3 us -> 21.4 us  [send(): moved = lax.ppermute(value, 'panel', [(s, s + distance) for s in senders])]
    reduce_scatter x1, waiting for transfers between devices: 59.2 us -> 49.7 us  [per_device(): summed = lax.psum_scatter(terms, 'panel', scatter_dimension=0, tiled=True)]
    pallas_call x0 -> x5, Pallas kernels: none -> 8.52 us  [later_products(): pl.pallas_call(later_body, grid_spec=pltpu.PrefetchScalarGridSpec(num_sca...]
    ppermute x13 -> x21, waiting for transfers between devices: 6.23 us -> 0.46 us  [send(): moved = lax.ppermute(value, 'panel', [(s, s + distance) for s in senders])]
    squeeze x0 -> x5, local copies, waits for them, and re-layouts: none -> 4.71 us  [the longest x1 2.66 us: ahead(): return lax.dynamic_index_in_dim(whole, index, 0, keepdims=False)]
    unnamed x15 -> x17, local copies, waits for them, and re-layouts: 6.08 us -> 10.5 us
    ppermute x1, starting transfers between devices: 5.32 us -> 1.88 us  [per_device(): other = lax.ppermute(mine, 'core', [(0, 1), (1, 0)])]
  transfers between devices with their start and end apart: 17 -> 25, of which waited for: 8 -> 5; matrix products, arithmetic and copies ran while one was open for 9% -> 9% of each run, Pallas kernels for 0% -> 4%
where the time goes in v2:
time: 247 us; the launch traced here: 243 us
  waiting for transfers between devices  126 us (51%)
  starting transfers between devices  31.9 us (13%)
  matrix products  21 us (9%)
  blocking collectives  20.8 us (8%)
  local copies, waits for them, and re-layouts  15.5 us (6%)
  between operations  14.5 us (6%)
  Pallas kernels  8.52 us (3%)
  other arithmetic  5.2 us (2%)
    all_gather x1, waiting for transfers between devices, per_device(): whole = lax.all_gather(coupling[0], ROWS).reshape(panels, width, width)  61.5 us
    reduce_scatter x1, waiting for transfers between devices, per_device(): summed = lax.psum_scatter(terms, 'panel', scatter_dimension=0, tiled=True)  49.7 us
    ppermute x21, starting transfers between devices, send(): moved = lax.ppermute(value, 'panel', [(s, s + distance) for s in senders])  21.4 us
    all_to_all x1, blocking collectives, per_device(): lax.all_to_all(jnp.broadcast_to(solved[None], (chips, share, width)), 'ch...  20.8 us
    dot_general x21, matrix products, times(): lax.dot_general(left, weight, (((1,), (1,)), ((), ())), preferred_element...  16.8 us
    all_to_all x1, waiting for transfers between devices, per_device(): pieces = lax.all_to_all(pieces, ROWS, 0, 0, tiled=True)  11.2 us
    unnamed x17, local copies, waits for them, and re-layouts  10.5 us
    all_to_all x1, starting transfers between devices, per_device(): pieces = lax.all_to_all(pieces, ROWS, 0, 0, tiled=True)  8.59 us
  transfers between devices with their start and end apart: 25, of which 5 were waited for; matrix products, arithmetic and copies ran while one was open for 9% of the time, Pallas kernels for 4%

profile of v2, /device:TPU:1, one launch (start us, length us, event | category | flops | bytes accessed | tf_op | source)
XLA Modules:
  0.0 243.4 jit_solution(13775655328050407323)
XLA Ops:
  7.2 0.7 all-gather.2.cloned.1.call-update
  7.9 2.0 copy.24
  10.0 8.6 %all-to-all-start = ((bf16[32,32,256]{2,1,0:T(8,128)(2,1)}), bf16[32,32,256]{2,1,0:T(8,128)(2,1)S(1)}, u32[]{:S(2)}, u32[]{:S(2)}) async-start(bf16[32,32,256]{2,1,0:T(8,128)(2,1)} %bitcast.2), calls=%async_computation | async-start | bytes 1048576 | tf_op jit(solution)/shard_map/all_to_all | solution.py:106
  18.9 11.2 %all-to-all-done = bf16[32,32,256]{2,1,0:T(8,128)(2,1)S(1)} async-done(((bf16[32,32,256]{2,1,0:T(8,128)(2,1)}), bf16[32,32,256]{2,1,0:T(8,128)(2,1)S(1)}, u32[]{:S(2)}, u32[]{:S(2)}) %all-to-all-start) | async-done | bytes 524320 | tf_op jit(solution)/shard_map/all_to_all | solution.py:106
  30.1 0.7 fusion.16.solved_ref
  30.9 61.5 %all-gather.2.cloned.1.call-done = bf16[32,256,1024]{2,1,0:T(8,128)(2,1)} async-done(((bf16[1,256,1024]{2,1,0:T(8,128)(2,1)}), bf16[32,256,1024]{2,1,0:T(8,128)(2,1)}) %all-gather.2.cloned.1.call-update) | async-done | bytes 16777232 | tf_op jit(solution)/shard_map/all_gather | solution.py:102
  92.3 2.7 %dynamic-slice_bitcast_fusion = (bf16[1024,1024]{1,0:T(8,128)(2,1)S(1)}, bf16[1024,1024]{1,0:T(8,128)(2,1)S(1)}) fusion(bf16[8,1024,1024]{2,1,0:T(8,128)(2,1)} %bitcast.120, s32[]{:T(128)S(6)} %select_n.79, s32[]{:T(128)S(6)} %select_n.78), kind=kLoop, calls=%fused_computation.18 | loop fusion | bytes 8388616 | tf_op jit(solution)/shard_map/jit(dynamic_index_in_dim)/squeeze | solution.py:113
  95.0 0.7 fusion.57
  95.7 3.2 %collective-permute-start = (f32[32,1024]{1,0:T(8,128)S(1)}, f32[32,1024]{1,0:T(8,128)S(1)}, u32[]{:S(2)}, u32[]{:S(2)}) collective-permute-start(f32[32,1024]{1,0:T(8,128)S(1)} %fusion.57), channel_id=1, source_target_pairs={{0,32},{1,33},{2,34},{3,35},{4,36},{5,37},{6,38},{7,39},{8,40},{9,... | collective-permute-start | bytes 393224 | tf_op jit(solution)/shard_map/ppermute | solution.py:122
  98.9 0.7 fusion.59
  99.6 1.7 collective-permute-start.2
  101.4 5.8 %copy-done.1 = bf16[32,256,1024]{2,1,0:T(8,128)(2,1)S(1)} copy-done((bf16[32,256,1024]{2,1,0:T(8,128)(2,1)S(1)}, bf16[32,256,1024]{2,1,0:T(8,128)(2,1)}, u32[]{:S(2)}) %copy-start.1) | copy-done | bytes 16777240
  107.1 5.7 %later_products.5.kept_ref = f32[5,32,1024]{2,1,0:T(8,128)S(1)} custom-call(s32[2]{0:T(128)S(1)} %get-tuple-element.50.place_ref, bf16[32,1024]{1,0:T(8,128)(2,1)S(1)} %fusion.16.solved_ref, bf16[8,1024,1024]{2,1,0:T(8,128)(2,1)S(1)} %bitcast.121, f32[5,32,1024]{2,1,0:T(8,128)S(1)} %broadcast_in_dim.21.kept_ref), custom_call_target="tpu_custom_call", output_to_operand_aliasing={{}: (3, {})} | custom-call | tf_op jit(solution)/shard_map/later_products/pallas_call | solution.py:63
  112.9 0.7 fusion.19.solved_ref
  113.6 0.7 fusion.58
  114.3 0.7 collective-permute-start.3
  115.0 0.7 fusion.61
  115.7 0.7 collective-permute-start.6
  117.1 1.3 collective-permute-start.7
  118.4 1.3 collective-permute-start.1
  119.7 0.7 fusion.22.solved_ref
  120.5 0.7 fusion.60
  121.2 0.7 collective-permute-start.8
  121.9 0.7 fusion.63
  122.6 0.8 later_products.7.kept_ref
  123.4 0.7 slice_bitcast_fusion.5
  124.1 1.3 collective-permute-start.11
  125.4 0.7 collective-permute-start.10
  126.1 1.3 collective-permute-start.4
  127.4 0.7 fusion.25.solved_ref
  128.1 0.7 fusion.62
  128.9 0.7 collective-permute-start.12
  129.6 0.7 fusion.65
  130.9 0.7 slice_bitcast_fusion.3
  132.3 0.7 collective-permute-start.14
  133.0 0.7 fusion.28.solved_ref
  133.7 0.7 fusion.64
  134.4 0.7 collective-permute-start.16
  135.1 0.7 fusion.68
  137.6 1.3 collective-permute-start.5
  138.9 0.7 collective-permute-start.9
  139.6 0.7 collective-permute-start.18
  140.2 0.7 fusion.31
  141.0 0.7 fusion.66
  141.7 0.7 collective-permute-start.19
  142.4 0.7 fusion.67
  143.1 0.7 collective-permute-start.13
  143.8 0.7 collective-permute-start.17
  144.5 0.7 fusion.34
  145.2 1.4 fusion.69
  146.6 1.3 collective-permute-start.20
  148.0 1.7 fusion.40
  149.8 20.8 %all_to_all.10 = bf16[16,32,1024]{2,1,0:T(8,128)(2,1)S(1)} all-to-all(bf16[16,32,1024]{2,1,0:T(8,128)(2,1)S(1)} %broadcast_in_dim.23), channel_id=1, replica_groups=mesh['panel'=8,'chip'=16,'core'=2] {'chip'}, dimensions={0} | all-to-all | bytes 2097152 | tf_op jit(solution)/shard_map/all_to_all | solution.py:141
  170.6 1.9 collective-permute-start.21
  172.6 2.3 collective-permute-done.21
  174.9 1.4 select_bitcast_fusion.1
  176.3 1.5 pad_maximum_fusion
  177.8 4.2 %multiply_bitcast_fusion = f32[8,512,128]{1,2,0:T(8,128)} fusion(bf16[8,128,1024]{2,1,0:T(8,128)(2,1)} %bitcast.25, bf16[512,1024,1]{1,0,2:T(8,128)(2,1)S(1)} %bitcast.134, f32[512]{0:T(512)S(1)} %broadcast_bitcast_fusion), kind=kOutput, calls=%fused_computation.17 | convolution fusion | flops 1074266112 | bytes 5244928 | tf_op jit(solution)/shard_map/rw,bsw->brs/dot_general | solution.py:155
  182.1 0.9 copy-done.3
  183.1 1.1 convert_bitcast_fusion
  184.2 0.8 copy.28
  185.0 49.7 %reduce-scatter.2.cloned.1.call-done = f32[1,512,128]{1,2,0:T(8,128)} async-done(((f32[8,512,128]{1,2,0:T(8,128)}), f32[1,512,128]{1,2,0:T(8,128)}) %reduce-scatter.2.cloned.1.call-update) | async-done | bytes 262160 | tf_op jit(solution)/shard_map/reduce_scatter | solution.py:156
  234.8 1.0 convert_subtract_fusion.7
  235.7 0.8 copy.29
  (50 shorter events, 4.5 us)
Async XLA Ops:
  7.2 23.0 %copy-start = (bf16[1,1024,1024]{2,1,0:T(8,128)(2,1)S(1)}, bf16[1,1024,1024]{2,1,0:T(8,128)(2,1)}, u32[]{:S(2)}) copy-start(bf16[1,1024,1024]{2,1,0:T(8,128)(2,1)} %param.8) | copy-start | bytes 6291460
  7.2 85.1 %all-gather.2.cloned.1.call-start = ((), (), s32[]{:S(2)}) async-start(), calls=%async_computation.3 | async-start | bytes 17301504 | tf_op jit(solution)/shard_map/all_gather | solution.py:102
  10.0 20.1 %all-to-all-start = ((bf16[32,32,256]{2,1,0:T(8,128)(2,1)}), bf16[32,32,256]{2,1,0:T(8,128)(2,1)S(1)}, u32[]{:S(2)}, u32[]{:S(2)}) async-start(bf16[32,32,256]{2,1,0:T(8,128)(2,1)} %bitcast.2), calls=%async_computation | async-start | bytes 1048576 | tf_op jit(solution)/shard_map/all_to_all | solution.py:106
  18.6 216.2 %reduce-scatter.2.cloned.1.call-start = ((), (), s32[]{:S(2)}) async-start(), calls=%async_computation.4 | async-start | bytes 2359296 | tf_op jit(solution)/shard_map/reduce_scatter | solution.py:156
  95.7 17.2 %collective-permute-start = (f32[32,1024]{1,0:T(8,128)S(1)}, f32[32,1024]{1,0:T(8,128)S(1)}, u32[]{:S(2)}, u32[]{:S(2)}) collective-permute-start(f32[32,1024]{1,0:T(8,128)S(1)} %fusion.57), channel_id=1, source_target_pairs={{0,32},{1,33},{2,34},{3,35},{4,36},{5,37},{6,38},{7,39},{8,40},{9,... | collective-permute-start | bytes 393224 | tf_op jit(solution)/shard_map/ppermute | solution.py:122
  99.6 20.1 %collective-permute-start.2 = (f32[32,1024]{1,0:T(8,128)S(1)}, f32[32,1024]{1,0:T(8,128)S(1)}, u32[]{:S(2)}, u32[]{:S(2)}) collective-permute-start(f32[32,1024]{1,0:T(8,128)S(1)} %fusion.59), channel_id=1, source_target_pairs={{0,64},{1,65},{2,66},{3,67},{4,68},{5,69},{6,70},{7,71},{8,72},{9,... | collective-permute-start | bytes 393224 | tf_op jit(solution)/shard_map/ppermute | solution.py:122
  101.4 5.8 %copy-start.1 = (bf16[32,256,1024]{2,1,0:T(8,128)(2,1)S(1)}, bf16[32,256,1024]{2,1,0:T(8,128)(2,1)}, u32[]{:S(2)}) copy-start(bf16[32,256,1024]{2,1,0:T(8,128)(2,1)} %all-gather.2.cloned.1.call-done) | copy-start | bytes 50331652
  107.1 9.3 %copy-start.2 = (bf16[32,256,1024]{2,1,0:T(8,128)(2,1)S(1)}, bf16[32,256,1024]{2,1,0:T(8,128)(2,1)}, u32[]{:S(2)}) copy-start(bf16[32,256,1024]{2,1,0:T(8,128)(2,1)} %all-gather.2.cloned.1.call-done) | copy-start | bytes 50331652
  114.3 5.4 %collective-permute-start.3 = (f32[32,1024]{1,0:T(8,128)S(1)}, f32[32,1024]{1,0:T(8,128)S(1)}, u32[]{:S(2)}, u32[]{:S(2)}) collective-permute-start(f32[32,1024]{1,0:T(8,128)S(1)} %fusion.58), channel_id=1, source_target_pairs={{32,64},{33,65},{34,66},{35,67},{36,68},{37,69},{38,70},{39,71},{4... | collective-permute-start | bytes 393224 | tf_op jit(solution)/shard_map/ppermute | solution.py:122
  115.7 9.7 %collective-permute-start.6 = (f32[32,1024]{1,0:T(8,128)S(1)}, f32[32,1024]{1,0:T(8,128)S(1)}, u32[]{:S(2)}, u32[]{:S(2)}) collective-permute-start(f32[32,1024]{1,0:T(8,128)S(1)} %fusion.61), channel_id=1, source_target_pairs={{32,96},{33,97},{34,98},{35,99},{36,100},{37,101},{38,102},{39,103... | collective-permute-start | bytes 393224 | tf_op jit(solution)/shard_map/ppermute | solution.py:122
  117.1 9.0 %collective-permute-start.7 = (f32[32,1024]{1,0:T(8,128)S(1)}, f32[32,1024]{1,0:T(8,128)S(1)}, u32[]{:S(2)}, u32[]{:S(2)}) collective-permute-start(f32[32,1024]{1,0:T(8,128)S(1)} %get-tuple-element.48), channel_id=1, source_target_pairs={{0,96},{32,128},{1,97},{33,129},{2,98},{34,130},{3,99},{35,131},{4... | collective-permute-start | bytes 393224 | tf_op jit(solution)/shard_map/ppermute | solution.py:122
  118.4 24.7 %collective-permute-start.1 = (f32[32,1024]{1,0:T(8,128)S(1)}, f32[32,1024]{1,0:T(8,128)S(1)}, u32[]{:S(2)}, u32[]{:S(2)}) collective-permute-start(f32[32,1024]{1,0:T(8,128)S(1)} %get-tuple-element.47), channel_id=1, source_target_pairs={{0,192},{32,224},{1,193},{33,225},{2,194},{34,226},{3,195},{35,227... | collective-permute-start | bytes 393224 | tf_op jit(solution)/shard_map/ppermute | solution.py:122
  121.2 6.2 %collective-permute-start.8 = (f32[32,1024]{1,0:T(8,128)S(1)}, f32[32,1024]{1,0:T(8,128)S(1)}, u32[]{:S(2)}, u32[]{:S(2)}) collective-permute-start(f32[32,1024]{1,0:T(8,128)S(1)} %fusion.60), channel_id=1, source_target_pairs={{64,96},{65,97},{66,98},{67,99},{68,100},{69,101},{70,102},{71,103... | collective-permute-start | bytes 393224 | tf_op jit(solution)/shard_map/ppermute | solution.py:122
  124.1 7.5 %collective-permute-start.11 = (f32[32,1024]{1,0:T(8,128)S(1)}, f32[32,1024]{1,0:T(8,128)S(1)}, u32[]{:S(2)}, u32[]{:S(2)}) collective-permute-start(f32[32,1024]{1,0:T(8,128)S(1)} %get-tuple-element.43), channel_id=1, source_target_pairs={{0,128},{32,160},{64,192},{1,129},{33,161},{65,193},{2,130},{34,16... | collective-permute-start | bytes 393224 | tf_op jit(solution)/shard_map/ppermute | solution.py:122
  125.4 6.9 %collective-permute-start.10 = (f32[32,1024]{1,0:T(8,128)S(1)}, f32[32,1024]{1,0:T(8,128)S(1)}, u32[]{:S(2)}, u32[]{:S(2)}) collective-permute-start(f32[32,1024]{1,0:T(8,128)S(1)} %fusion.63), channel_id=1, source_target_pairs={{64,128},{65,129},{66,130},{67,131},{68,132},{69,133},{70,134},{71... | collective-permute-start | bytes 393224 | tf_op jit(solution)/shard_map/ppermute | solution.py:122
  126.1 11.5 %collective-permute-start.4 = (f32[32,1024]{1,0:T(8,128)S(1)}, f32[32,1024]{1,0:T(8,128)S(1)}, u32[]{:S(2)}, u32[]{:S(2)}) collective-permute-start(f32[32,1024]{1,0:T(8,128)S(1)} %get-tuple-element.44), channel_id=1, source_target_pairs={{0,160},{32,192},{64,224},{1,161},{33,193},{65,225},{2,162},{34,19... | collective-permute-start | bytes 393224 | tf_op jit(solution)/shard_map/ppermute | solution.py:122
  128.9 4.1 %collective-permute-start.12 = (f32[32,1024]{1,0:T(8,128)S(1)}, f32[32,1024]{1,0:T(8,128)S(1)}, u32[]{:S(2)}, u32[]{:S(2)}) collective-permute-start(f32[32,1024]{1,0:T(8,128)S(1)} %fusion.62), channel_id=1, source_target_pairs={{96,128},{97,129},{98,130},{99,131},{100,132},{101,133},{102,134},... | collective-permute-start | bytes 393224 | tf_op jit(solution)/shard_map/ppermute | solution.py:122
  131.6 7.2 %collective-permute-start.15 = (f32[32,1024]{1,0:T(8,128)S(1)}, f32[32,1024]{1,0:T(8,128)S(1)}, u32[]{:S(2)}, u32[]{:S(2)}) collective-permute-start(f32[32,1024]{1,0:T(8,128)S(1)} %get-tuple-element.46), channel_id=1, source_target_pairs={{64,160},{96,192},{65,161},{97,193},{66,162},{98,194},{67,163},{99... | collective-permute-start | bytes 393224 | tf_op jit(solution)/shard_map/ppermute | solution.py:122
  132.3 7.3 %collective-permute-start.14 = (f32[32,1024]{1,0:T(8,128)S(1)}, f32[32,1024]{1,0:T(8,128)S(1)}, u32[]{:S(2)}, u32[]{:S(2)}) collective-permute-start(f32[32,1024]{1,0:T(8,128)S(1)} %fusion.65), channel_id=1, source_target_pairs={{96,160},{97,161},{98,162},{99,163},{100,164},{101,165},{102,166},... | collective-permute-start | bytes 393224 | tf_op jit(solution)/shard_map/ppermute | solution.py:122
  134.4 5.8 %collective-permute-start.16 = (f32[32,1024]{1,0:T(8,128)S(1)}, f32[32,1024]{1,0:T(8,128)S(1)}, u32[]{:S(2)}, u32[]{:S(2)}) collective-permute-start(f32[32,1024]{1,0:T(8,128)S(1)} %fusion.64), channel_id=1, source_target_pairs={{128,160},{129,161},{130,162},{131,163},{132,164},{133,165},{134,1... | collective-permute-start | bytes 393224 | tf_op jit(solution)/shard_map/ppermute | solution.py:122
  137.6 10.4 %collective-permute-start.5 = (f32[32,1024]{1,0:T(8,128)}, f32[32,1024]{1,0:T(8,128)S(1)}, u32[]{:S(2)}, u32[]{:S(2)}) collective-permute-start(f32[32,1024]{1,0:T(8,128)} %get-tuple-element.42), channel_id=1, source_target_pairs={{0,224},{1,225},{2,226},{3,227},{4,228},{5,229},{6,230},{7,231},{8... | collective-permute-start | bytes 393224 | tf_op jit(solution)/shard_map/ppermute | solution.py:122
  138.9 9.1 %collective-permute-start.9 = (f32[32,1024]{1,0:T(8,128)}, f32[32,1024]{1,0:T(8,128)S(1)}, u32[]{:S(2)}, u32[]{:S(2)}) collective-permute-start(f32[32,1024]{1,0:T(8,128)} %get-tuple-element.45), channel_id=1, source_target_pairs={{96,224},{97,225},{98,226},{99,227},{100,228},{101,229},{102,230},... | collective-permute-start | bytes 393224 | tf_op jit(solution)/shard_map/ppermute | solution.py:122
  139.6 4.2 %collective-permute-start.18 = (f32[32,1024]{1,0:T(8,128)S(1)}, f32[32,1024]{1,0:T(8,128)S(1)}, u32[]{:S(2)}, u32[]{:S(2)}) collective-permute-start(f32[32,1024]{1,0:T(8,128)S(1)} %fusion.68), channel_id=1, source_target_pairs={{128,192},{129,193},{130,194},{131,195},{132,196},{133,197},{134,1... | collective-permute-start | bytes 393224 | tf_op jit(solution)/shard_map/ppermute | solution.py:122
  141.7 2.8 %collective-permute-start.19 = (f32[32,1024]{1,0:T(8,128)S(1)}, f32[32,1024]{1,0:T(8,128)S(1)}, u32[]{:S(2)}, u32[]{:S(2)}) collective-permute-start(f32[32,1024]{1,0:T(8,128)S(1)} %fusion.66), channel_id=1, source_target_pairs={{160,192},{161,193},{162,194},{163,195},{164,196},{165,197},{166,1... | collective-permute-start | bytes 393224 | tf_op jit(solution)/shard_map/ppermute | solution.py:122
  143.1 4.8 %collective-permute-start.13 = (f32[32,1024]{1,0:T(8,128)}, f32[32,1024]{1,0:T(8,128)S(1)}, u32[]{:S(2)}, u32[]{:S(2)}) collective-permute-start(f32[32,1024]{1,0:T(8,128)} %slice_bitcast_fusion.1), channel_id=1, source_target_pairs={{128,224},{129,225},{130,226},{131,227},{132,228},{133,229},{134,2... | collective-permute-start | bytes 393224 | tf_op jit(solution)/shard_map/ppermute | solution.py:122
  143.8 4.2 %collective-permute-start.17 = (f32[32,1024]{1,0:T(8,128)S(1)}, f32[32,1024]{1,0:T(8,128)S(1)}, u32[]{:S(2)}, u32[]{:S(2)}) collective-permute-start(f32[32,1024]{1,0:T(8,128)S(1)} %fusion.67), channel_id=1, source_target_pairs={{160,224},{161,225},{162,226},{163,227},{164,228},{165,229},{166,2... | collective-permute-start | bytes 393224 | tf_op jit(solution)/shard_map/ppermute | solution.py:122
  146.6 1.3 collective-permute-start.20
  149.6 22.8 %copy-start.5 = (s32[4,1]{0,1:T(1,128)S(1)}, s32[4,1]{0,1:T(1,128)}, u32[]{:S(2)}) copy-start(s32[4,1]{0,1:T(1,128)} %param.11) | copy-start | bytes 52
  170.6 4.3 %collective-permute-start.21 = (bf16[16,32,1024]{2,1,0:T(8,128)(2,1)S(1)}, bf16[16,32,1024]{2,1,0:T(8,128)(2,1)}, u32[]{:S(2)}, u32[]{:S(2)}) collective-permute-start(bf16[16,32,1024]{2,1,0:T(8,128)(2,1)S(1)} %all_to_all.10), channel_id=1, source_target_pairs={{0,1},{1,0},{2,3},{3,2},{4,5},{5,4},{6,7},{7,6},{8,9},{9,8},{10,11... | collective-permute-start | bytes 3145736 | tf_op jit(solution)/shard_map/ppermute | solution.py:144
  176.3 1.6 copy-start.4
  182.1 0.9 copy-start.3
Sparse Core Ops, SparseCore 0:
  10.6 81.7 all-gather.1
  182.2 52.5 reduce-scatter.1

commit v3 on v2

--- a/solution.py
+++ b/solution.py
@@ -10,10 +10,11 @@
 BF16 = jnp.bfloat16
 ROWS = ("chip", "core")
 FAR_SENDS = {
-    1: ((3, (0, 1)), (6, (0, 1))),
-    2: ((4, (0, 1, 2)), (5, (0, 1, 2)), (7, (0,))),
-    3: ((3, (2, 3)), (4, (3,))),
-    4: ((3, (4,)),),
+    1: ((3, (0, 1)),),
+    2: ((4, (0, 1, 2)),),
+    3: ((3, (2, 3)), (5, (0, 1, 2))),
+    4: ((4, (3,)), (6, (0, 1))),
+    5: ((3, (4,)), (7, (0,))),
 }
 
 
@@ -37,25 +38,16 @@
 
     @pl.when(place_ref[1] == 1)
     def _():
-        for i in range(count):
+        valid = jnp.minimum(count, panels - 3 - z)
+        lax.fori_loop(0, valid, lambda i, _: load(i).start(), None)
 
-            @pl.when(z + 3 + i < panels)
-            def _():
-                load(i).start()
+        def multiply(i, _):
+            load(i).wait()
+            products[i] = times(solved_ref[...], weights[i]).astype(BF16)
+            store(i).start()
 
-        for i in range(count):
-
-            @pl.when(z + 3 + i < panels)
-            def _():
-                load(i).wait()
-                products[i] = times(solved_ref[...], weights[i])
-                store(i).start()
-
-        for i in range(count):
-
-            @pl.when(z + 3 + i < panels)
-            def _():
-                store(i).wait()
+        lax.fori_loop(0, valid, multiply, None)
+        lax.fori_loop(0, valid, lambda i, _: store(i).wait(), None)
 
 
 def later_products(z, turn, solved, whole, kept):
@@ -73,12 +65,12 @@
             out_specs=pl.BlockSpec(memory_space=pl.ANY),
             scratch_shapes=[
                 pltpu.VMEM((count, width, width), BF16),
-                pltpu.VMEM((count, share, width), F32),
+                pltpu.VMEM((count, share, width), BF16),
                 pltpu.SemaphoreType.DMA((count,)),
                 pltpu.SemaphoreType.DMA((count,)),
             ],
         ),
-        out_shape=jax.ShapeDtypeStruct(kept.shape, F32),
+        out_shape=jax.ShapeDtypeStruct(kept.shape, BF16),
         input_output_aliases={3: 0},
         compiler_params=pltpu.CompilerParams(vmem_limit_bytes=16 * 2**20),
         name="later_products",
@@ -115,13 +107,13 @@
     following, second = lax.optimization_barrier((ahead(1), ahead(2)))
 
     solved = jnp.zeros((share, width), BF16)
-    kept = jnp.zeros((panels - 3, share, width), F32)
+    kept = jnp.zeros((panels - 3, share, width), BF16)
     arrivals = [[] for _ in range(panels)]
 
     def send(value, senders, distance):
         moved = lax.ppermute(value, "panel", [(s, s + distance) for s in senders])
         for s in senders:
-            arrivals[s + distance].append(moved)
+            arrivals[s + distance].append(moved.astype(F32))
 
     for k in range(panels):
         earlier = sum(arrivals[k], jnp.zeros((share, width), F32))
@@ -129,11 +121,11 @@
         solved = jnp.where(z == k, fresh, solved)
         if k == panels - 1:
             break
-        near = times(fresh, following)
+        near = times(fresh, following).astype(BF16)
         near, fresh = lax.optimization_barrier((near, fresh))
         send(near, [k], 1)
         if k < panels - 2:
-            send(times(fresh, second), [k], 2)
+            send(times(fresh, second).astype(BF16), [k], 2)
         if k < panels - 3:
             kept = later_products(z, z == k, fresh, whole, kept)
         for distance, senders in FAR_SENDS.get(k, ()):
@@ -142,9 +134,9 @@
         jnp.broadcast_to(solved[None], (chips, share, width)), "chip", 0, 0, tiled=True
     )
     other = lax.ppermute(mine, "core", [(0, 1), (1, 0)])
-    first = jnp.where(core == 0, mine, other)
-    second = jnp.where(core == 0, other, mine)
-    full = jnp.stack([first, second], 1).reshape(batches, columns, width)
+    sources = lax.broadcasted_iota(jnp.int32, (1, 2, 1, 1), 1)
+    full = jnp.where(sources == core, mine[:, None], other[:, None])
+    full = full.reshape(batches, columns, width)
 
     own_rows = lax.dynamic_slice_in_dim(full, rows_index * slice_rows, slice_rows, 2)
     solution_rows = own_rows.transpose(0, 2, 1).astype(F32)
@@ -152,9 +144,18 @@
     blocks, block_rows = tall_blocks.shape[1], tall_blocks.shape[2]
     tall = tall_blocks[0].reshape(blocks * block_rows, width)
     mask = jnp.repeat(sparsity[:, 0].astype(F32), block_rows)[:, None]
-    terms = jnp.einsum("rw,bsw->brs", tall, full, preferred_element_type=F32) * mask
-    summed = lax.psum_scatter(terms, "panel", scatter_dimension=0, tiled=True)
-    return solution_rows[None], rhs_tall.astype(F32) - summed
+
+    def product(batch):
+        term = times(tall, lax.dynamic_index_in_dim(full, batch, 0, keepdims=False))
+        return term * mask
+
+    summed = jnp.zeros((blocks * block_rows, columns), F32)
+    for distance in sorted(range(1, panels), key=lambda d: abs(2 * d - panels)):
+        term = product(lax.rem(z + distance, panels)).astype(BF16)
+        route = [(s, (s + distance) % panels) for s in range(panels)]
+        summed = summed + lax.ppermute(term, "panel", route).astype(F32)
+    summed = summed + product(z)
+    return solution_rows[None], rhs_tall.astype(F32) - summed[None]
 
 
 def solution(mesh):

time: 247 us -> 219 us (0.89); the launches traced: 243 us -> 218 us
  waiting for transfers between devices: 126 us -> 81.3 us
  starting transfers between devices: 31.9 us -> 50.2 us
  other arithmetic: 5.2 us -> 2.41 us
  matrix products: 21 us -> 23.7 us
    reduce_scatter x1 -> x0, waiting for transfers between devices: 49.7 us -> none  [per_device(): summed = lax.psum_scatter(terms, 'panel', scatter_dimension=0, tiled=True)]
    ppermute x0 -> x7, starting transfers between devices: none -> 14.4 us  [per_device(): summed = summed + lax.ppermute(term, 'panel', route).astype(F32)]
    dot_general x21 -> x29, matrix products: 16.8 us -> 23.7 us  [times(): lax.dot_general(left, weight, (((1,), (1,)), ((), ())), preferred_element...]
    ppermute x0 -> x7, waiting for transfers between devices: none -> 5.69 us  [per_device(): summed = summed + lax.ppermute(term, 'panel', route).astype(F32)]
    dot_general x1 -> x0, matrix products: 4.23 us -> none  [per_device(): jnp.einsum('rw,bsw->brs', tall, full, preferred_element_type=F32) * mask]
    ppermute x21, starting transfers between devices: 21.4 us -> 24.8 us  [send(): moved = lax.ppermute(value, 'panel', [(s, s + distance) for s in senders])]
    another operation x2 -> x0, other arithmetic: 2.9 us -> none  [per_device(): full = jnp.stack([first, second], 1).reshape(batches, columns, width)]
    unnamed x17 -> x21, local copies, waits for them, and re-layouts: 10.5 us -> 12.5 us
  transfers between devices with their start and end apart: 25 -> 31, of which waited for: 5 -> 7; matrix products, arithmetic and copies ran while one was open for 9% -> 13% of each run, Pallas kernels for 4% -> 4%
where the time goes in v3:
time: 219 us; the launch traced here: 218 us
  waiting for transfers between devices  81.3 us (37%)
  starting transfers between devices  50.2 us (23%)
  matrix products  23.7 us (11%)
  blocking collectives  20.3 us (9%)
  local copies, waits for them, and re-layouts  17.4 us (8%)
  between operations  14.6 us (7%)
  Pallas kernels  7.95 us (4%)
  other arithmetic  2.41 us (1%)
    all_gather x1, waiting for transfers between devices, per_device(): whole = lax.all_gather(coupling[0], ROWS).reshape(panels, width, width)  61.4 us
    ppermute x21, starting transfers between devices, send(): moved = lax.ppermute(value, 'panel', [(s, s + distance) for s in senders])  24.8 us
    dot_general x29, matrix products, times(): lax.dot_general(left, weight, (((1,), (1,)), ((), ())), preferred_element...  23.7 us
    all_to_all x1, blocking collectives, per_device(): lax.all_to_all(jnp.broadcast_to(solved[None], (chips, share, width)), 'ch...  20.3 us
    ppermute x7, starting transfers between devices, per_device(): summed = summed + lax.ppermute(term, 'panel', route).astype(F32)  14.4 us
    unnamed x21, local copies, waits for them, and re-layouts  12.5 us
    all_to_all x1, waiting for transfers between devices, per_device(): pieces = lax.all_to_all(pieces, ROWS, 0, 0, tiled=True)  11.3 us
    all_to_all x1, starting transfers between devices, per_device(): pieces = lax.all_to_all(pieces, ROWS, 0, 0, tiled=True)  8.59 us
  transfers between devices with their start and end apart: 31, of which 7 were waited for; matrix products, arithmetic and copies ran while one was open for 13% of the time, Pallas kernels for 4%

profile of v3, /device:TPU:1, one launch (start us, length us, event | category | flops | bytes accessed | tf_op | source)
XLA Modules:
  0.0 217.9 jit_solution(17909066174880716602)
XLA Ops:
  7.2 0.7 all-gather.2.cloned.1.call-update
  7.9 2.1 copy.21
  10.0 8.6 %all-to-all-start = ((bf16[32,32,256]{2,1,0:T(8,128)(2,1)}), bf16[32,32,256]{2,1,0:T(8,128)(2,1)S(1)}, u32[]{:S(2)}, u32[]{:S(2)}) async-start(bf16[32,32,256]{2,1,0:T(8,128)(2,1)} %bitcast.2), calls=%async_computation | async-start | bytes 1048576 | tf_op jit(solution)/shard_map/all_to_all | solution.py:98
  18.8 11.3 %all-to-all-done = bf16[32,32,256]{2,1,0:T(8,128)(2,1)S(1)} async-done(((bf16[32,32,256]{2,1,0:T(8,128)(2,1)}), bf16[32,32,256]{2,1,0:T(8,128)(2,1)S(1)}, u32[]{:S(2)}, u32[]{:S(2)}) %all-to-all-start) | async-done | bytes 524320 | tf_op jit(solution)/shard_map/all_to_all | solution.py:98
  30.1 0.7 fusion.31.solved_ref
  30.9 61.4 %all-gather.2.cloned.1.call-done = bf16[32,256,1024]{2,1,0:T(8,128)(2,1)} async-done(((bf16[1,256,1024]{2,1,0:T(8,128)(2,1)}), bf16[32,256,1024]{2,1,0:T(8,128)(2,1)}) %all-gather.2.cloned.1.call-update) | async-done | bytes 16777232 | tf_op jit(solution)/shard_map/all_gather | solution.py:94
  92.3 2.7 %dynamic-slice_bitcast_fusion = (bf16[1024,1024]{1,0:T(8,128)(2,1)S(1)}, bf16[1024,1024]{1,0:T(8,128)(2,1)S(1)}) fusion(bf16[8,1024,1024]{2,1,0:T(8,128)(2,1)} %bitcast.163, s32[]{:T(128)S(6)} %select_n.96, s32[]{:T(128)S(6)} %select_n.95), kind=kLoop, calls=%fused_computation.16 | loop fusion | bytes 8388616 | tf_op jit(solution)/shard_map/jit(dynamic_index_in_dim)/squeeze | solution.py:105
  95.0 0.7 convolution_convert_fusion.12
  95.7 3.2 %collective-permute-start = (bf16[32,1024]{1,0:T(8,128)(2,1)S(1)}, bf16[32,1024]{1,0:T(8,128)(2,1)S(1)}, u32[]{:S(2)}, u32[]{:S(2)}) collective-permute-start(bf16[32,1024]{1,0:T(8,128)(2,1)S(1)} %convolution_convert_fusion.12), channel_id=1, source_target_pairs={{0,32},{1,33},{2,34},{3,35},{4,36},{5,37},{6,38},{7,39},{8,40},{9,... | collective-permute-start | bytes 196616 | tf_op jit(solution)/shard_map/ppermute | solution.py:114
  98.9 0.7 convolution_convert_fusion.9
  99.6 1.7 collective-permute-start.3
  101.3 5.8 %copy-done.1 = bf16[32,256,1024]{2,1,0:T(8,128)(2,1)S(1)} copy-done((bf16[32,256,1024]{2,1,0:T(8,128)(2,1)S(1)}, bf16[32,256,1024]{2,1,0:T(8,128)(2,1)}, u32[]{:S(2)}) %copy-start.1) | copy-done | bytes 16777240
  107.1 5.4 %later_products.5.kept_ref = bf16[5,32,1024]{2,1,0:T(8,128)(2,1)S(1)} custom-call(s32[2]{0:T(128)S(1)} %get-tuple-element.48.place_ref, bf16[32,1024]{1,0:T(8,128)(2,1)S(1)} %fusion.31.solved_ref, bf16[8,1024,1024]{2,1,0:T(8,128)(2,1)S(1)} %bitcast.164, bf16[5,32,1024]{2,1,0:T(8,128)(2,1)S(1)} %broadcast_in_dim.61.kept_ref), custom_call_target="tpu_custom_call", output_to_operand_aliasing={{}: (3, {})} | custom-call | tf_op jit(solution)/shard_map/later_products/pallas_call | solution.py:55
  112.5 0.7 fusion.34.solved_ref
  113.2 0.7 convolution_convert_fusion.11
  114.0 0.7 convolution_convert_fusion.10
  114.7 0.7 collective-permute-start.1
  116.7 1.3 collective-permute-start.2
  118.0 0.7 fusion.37.solved_ref
  118.7 0.7 convolution_convert_fusion.8
  120.2 0.7 convolution_convert_fusion.6
  122.2 1.3 collective-permute-start.8
  123.5 0.7 fusion.40.solved_ref
  124.3 0.7 convolution_convert_fusion.7
  125.0 0.7 convolution_convert_fusion.4
  128.4 1.3 collective-permute-start.6
  129.8 0.7 fusion.43.solved_ref
  130.5 0.7 convolution_convert_fusion.5
  131.2 0.7 collective-permute-start.14
  131.9 0.7 convolution_convert_fusion.1
  134.0 5.2 %collective-permute-start.11 = (bf16[32,1024]{1,0:T(8,128)(2,1)S(1)}, bf16[32,1024]{1,0:T(8,128)(2,1)S(1)}, u32[]{:S(2)}, u32[]{:S(2)}) collective-permute-start(bf16[32,1024]{1,0:T(8,128)(2,1)S(1)} %get-tuple-element.43), channel_id=1, source_target_pairs={{0,192},{32,224},{1,193},{33,225},{2,194},{34,226},{3,195},{35,227... | collective-permute-start | bytes 196616 | tf_op jit(solution)/shard_map/ppermute | solution.py:114
  139.9 0.8 collective-permute-start.16
  140.7 0.7 fusion.46
  141.5 0.7 convolution_convert_fusion.3
  142.9 0.7 convolution_convert_fusion.2
  143.6 1.3 collective-permute-start.17
  145.6 0.7 fusion.49
  146.3 0.7 convolution_convert_fusion
  147.1 0.7 collective-permute-start.20
  147.8 0.7 fusion.55
  148.7 20.3 %all_to_all.10 = bf16[16,32,1024]{2,1,0:T(8,128)(2,1)S(1)} all-to-all(bf16[16,32,1024]{2,1,0:T(8,128)(2,1)S(1)} %broadcast_in_dim.63), channel_id=1, replica_groups=mesh['panel'=8,'chip'=16,'core'=2] {'chip'}, dimensions={0} | all-to-all | bytes 2097152 | tf_op jit(solution)/shard_map/all_to_all | solution.py:133
  169.0 2.4 %collective-permute-start.21 = (bf16[16,32,1024]{2,1,0:T(8,128)(2,1)S(1)}, bf16[16,32,1024]{2,1,0:T(8,128)(2,1)}, u32[]{:S(2)}, u32[]{:S(2)}) collective-permute-start(bf16[16,32,1024]{2,1,0:T(8,128)(2,1)S(1)} %all_to_all.10), channel_id=1, source_target_pairs={{0,1},{1,0},{2,3},{3,2},{4,5},{5,4},{6,7},{7,6},{8,9},{9,8},{10,11... | collective-permute-start | bytes 3145736 | tf_op jit(solution)/shard_map/ppermute | solution.py:136
  171.6 2.2 collective-permute-done.21
  173.8 1.5 broadcast_in_dim.66
  175.9 0.9 copy-done.3
  177.3 4.6 %collective-permute-start.22 = (bf16[512,128]{0,1:T(8,128)(2,1)S(1)}, bf16[512,128]{0,1:T(8,128)(2,1)S(1)}, u32[]{:S(2)}, u32[]{:S(2)}) collective-permute-start(bf16[512,128]{0,1:T(8,128)(2,1)S(1)} %fusion.30), channel_id=1, source_target_pairs={{0,128},{32,160},{64,192},{96,224},{128,0},{160,32},{192,64},{224,... | collective-permute-start | bytes 393224 | tf_op jit(solution)/shard_map/ppermute | solution.py:156
  182.4 4.6 %collective-permute-start.23 = (bf16[512,128]{0,1:T(8,128)(2,1)S(1)}, bf16[512,128]{0,1:T(8,128)(2,1)S(1)}, u32[]{:S(2)}, u32[]{:S(2)}) collective-permute-start(bf16[512,128]{0,1:T(8,128)(2,1)S(1)} %fusion.29), channel_id=1, source_target_pairs={{0,96},{32,128},{64,160},{96,192},{128,224},{160,0},{192,32},{224,... | collective-permute-start | bytes 393224 | tf_op jit(solution)/shard_map/ppermute | solution.py:156
  187.0 1.1 fusion.28
  188.1 1.1 fusion.27
  189.3 2.8 %collective-permute-start.25 = (bf16[512,128]{0,1:T(8,128)(2,1)}, bf16[512,128]{0,1:T(8,128)(2,1)}, u32[]{:S(2)}, u32[]{:S(2)}) collective-permute-start(bf16[512,128]{0,1:T(8,128)(2,1)} %fusion.27), channel_id=1, source_target_pairs={{0,64},{32,96},{64,128},{96,160},{128,192},{160,224},{192,0},{224,... | collective-permute-start | bytes 393224 | tf_op jit(solution)/shard_map/ppermute | solution.py:156
  192.1 1.2 fusion.26
  193.2 0.8 collective-permute-start.26
  194.0 1.1 fusion.25
  195.1 1.1 fusion.24
  196.6 1.0 collective-permute-done.23
  197.6 1.4 collective-permute-start.28
  199.0 1.0 copy.23
  200.0 1.9 convert_bitcast_fusion
  201.9 1.9 copy.24
  203.8 1.0 collective-permute-done.26
  204.7 1.9 collective-permute-done.27
  206.6 1.8 collective-permute-done.28
  208.4 1.8 bitcast_subtract_fusion
  210.3 0.8 copy.25
  (75 shorter events, 11.9 us)
Async XLA Ops:
  7.2 23.0 %copy-start = (bf16[1,1024,1024]{2,1,0:T(8,128)(2,1)S(1)}, bf16[1,1024,1024]{2,1,0:T(8,128)(2,1)}, u32[]{:S(2)}) copy-start(bf16[1,1024,1024]{2,1,0:T(8,128)(2,1)} %param.8) | copy-start | bytes 6291460
  7.2 85.1 %all-gather.2.cloned.1.call-start = ((), (), s32[]{:S(2)}) async-start(), calls=%async_computation.2 | async-start | bytes 17301504 | tf_op jit(solution)/shard_map/all_gather | solution.py:94
  10.0 20.1 %all-to-all-start = ((bf16[32,32,256]{2,1,0:T(8,128)(2,1)}), bf16[32,32,256]{2,1,0:T(8,128)(2,1)S(1)}, u32[]{:S(2)}, u32[]{:S(2)}) async-start(bf16[32,32,256]{2,1,0:T(8,128)(2,1)} %bitcast.2), calls=%async_computation | async-start | bytes 1048576 | tf_op jit(solution)/shard_map/all_to_all | solution.py:98
  95.7 16.8 %collective-permute-start = (bf16[32,1024]{1,0:T(8,128)(2,1)S(1)}, bf16[32,1024]{1,0:T(8,128)(2,1)S(1)}, u32[]{:S(2)}, u32[]{:S(2)}) collective-permute-start(bf16[32,1024]{1,0:T(8,128)(2,1)S(1)} %convolution_convert_fusion.12), channel_id=1, source_target_pairs={{0,32},{1,33},{2,34},{3,35},{4,36},{5,37},{6,38},{7,39},{8,40},{9,... | collective-permute-start | bytes 196616 | tf_op jit(solution)/shard_map/ppermute | solution.py:114
  99.6 18.4 %collective-permute-start.3 = (bf16[32,1024]{1,0:T(8,128)(2,1)S(1)}, bf16[32,1024]{1,0:T(8,128)(2,1)S(1)}, u32[]{:S(2)}, u32[]{:S(2)}) collective-permute-start(bf16[32,1024]{1,0:T(8,128)(2,1)S(1)} %convolution_convert_fusion.9), channel_id=1, source_target_pairs={{0,64},{1,65},{2,66},{3,67},{4,68},{5,69},{6,70},{7,71},{8,72},{9,... | collective-permute-start | bytes 196616 | tf_op jit(solution)/shard_map/ppermute | solution.py:114
  101.3 5.8 %copy-start.1 = (bf16[32,256,1024]{2,1,0:T(8,128)(2,1)S(1)}, bf16[32,256,1024]{2,1,0:T(8,128)(2,1)}, u32[]{:S(2)}) copy-start(bf16[32,256,1024]{2,1,0:T(8,128)(2,1)} %all-gather.2.cloned.1.call-done) | copy-start | bytes 50331652
  107.1 8.9 %copy-start.2 = (bf16[32,256,1024]{2,1,0:T(8,128)(2,1)S(1)}, bf16[32,256,1024]{2,1,0:T(8,128)(2,1)}, u32[]{:S(2)}) copy-start(bf16[32,256,1024]{2,1,0:T(8,128)(2,1)} %all-gather.2.cloned.1.call-done) | copy-start | bytes 50331652
  114.7 8.8 %collective-permute-start.1 = (bf16[32,1024]{1,0:T(8,128)(2,1)S(1)}, bf16[32,1024]{1,0:T(8,128)(2,1)S(1)}, u32[]{:S(2)}, u32[]{:S(2)}) collective-permute-start(bf16[32,1024]{1,0:T(8,128)(2,1)S(1)} %convolution_convert_fusion.10), channel_id=1, source_target_pairs={{32,96},{33,97},{34,98},{35,99},{36,100},{37,101},{38,102},{39,103... | collective-permute-start | bytes 196616 | tf_op jit(solution)/shard_map/ppermute | solution.py:114
  115.4 2.7 %collective-permute-start.4 = (bf16[32,1024]{1,0:T(8,128)(2,1)S(1)}, bf16[32,1024]{1,0:T(8,128)(2,1)S(1)}, u32[]{:S(2)}, u32[]{:S(2)}) collective-permute-start(bf16[32,1024]{1,0:T(8,128)(2,1)S(1)} %convolution_convert_fusion.11), channel_id=1, source_target_pairs={{32,64},{33,65},{34,66},{35,67},{36,68},{37,69},{38,70},{39,71},{4... | collective-permute-start | bytes 196616 | tf_op jit(solution)/shard_map/ppermute | solution.py:114
  116.7 6.8 %collective-permute-start.2 = (bf16[32,1024]{1,0:T(8,128)(2,1)S(1)}, bf16[32,1024]{1,0:T(8,128)(2,1)S(1)}, u32[]{:S(2)}, u32[]{:S(2)}) collective-permute-start(bf16[32,1024]{1,0:T(8,128)(2,1)S(1)} %slice_bitcast_fusion.7), channel_id=1, source_target_pairs={{0,96},{32,128},{1,97},{33,129},{2,98},{34,130},{3,99},{35,131},{4... | collective-permute-start | bytes 196616 | tf_op jit(solution)/shard_map/ppermute | solution.py:114
  119.5 4.1 %collective-permute-start.5 = (bf16[32,1024]{1,0:T(8,128)(2,1)S(1)}, bf16[32,1024]{1,0:T(8,128)(2,1)S(1)}, u32[]{:S(2)}, u32[]{:S(2)}) collective-permute-start(bf16[32,1024]{1,0:T(8,128)(2,1)S(1)} %convolution_convert_fusion.8), channel_id=1, source_target_pairs={{64,96},{65,97},{66,98},{67,99},{68,100},{69,101},{70,102},{71,103... | collective-permute-start | bytes 196616 | tf_op jit(solution)/shard_map/ppermute | solution.py:114
  120.9 7.6 %collective-permute-start.7 = (bf16[32,1024]{1,0:T(8,128)(2,1)S(1)}, bf16[32,1024]{1,0:T(8,128)(2,1)S(1)}, u32[]{:S(2)}, u32[]{:S(2)}) collective-permute-start(bf16[32,1024]{1,0:T(8,128)(2,1)S(1)} %convolution_convert_fusion.6), channel_id=1, source_target_pairs={{64,128},{65,129},{66,130},{67,131},{68,132},{69,133},{70,134},{71... | collective-permute-start | bytes 196616 | tf_op jit(solution)/shard_map/ppermute | solution.py:114
  122.2 7.5 %collective-permute-start.8 = (bf16[32,1024]{1,0:T(8,128)(2,1)S(1)}, bf16[32,1024]{1,0:T(8,128)(2,1)S(1)}, u32[]{:S(2)}, u32[]{:S(2)}) collective-permute-start(bf16[32,1024]{1,0:T(8,128)(2,1)S(1)} %slice_bitcast_fusion.5), channel_id=1, source_target_pairs={{0,128},{32,160},{64,192},{1,129},{33,161},{65,193},{2,130},{34,16... | collective-permute-start | bytes 196616 | tf_op jit(solution)/shard_map/ppermute | solution.py:114
  125.7 8.2 %collective-permute-start.12 = (bf16[32,1024]{1,0:T(8,128)(2,1)S(1)}, bf16[32,1024]{1,0:T(8,128)(2,1)S(1)}, u32[]{:S(2)}, u32[]{:S(2)}) collective-permute-start(bf16[32,1024]{1,0:T(8,128)(2,1)S(1)} %convolution_convert_fusion.4), channel_id=1, source_target_pairs={{96,160},{97,161},{98,162},{99,163},{100,164},{101,165},{102,166},... | collective-permute-start | bytes 196616 | tf_op jit(solution)/shard_map/ppermute | solution.py:114
  126.4 3.3 %collective-permute-start.9 = (bf16[32,1024]{1,0:T(8,128)(2,1)S(1)}, bf16[32,1024]{1,0:T(8,128)(2,1)S(1)}, u32[]{:S(2)}, u32[]{:S(2)}) collective-permute-start(bf16[32,1024]{1,0:T(8,128)(2,1)S(1)} %convolution_convert_fusion.7), channel_id=1, source_target_pairs={{96,128},{97,129},{98,130},{99,131},{100,132},{101,133},{102,134},... | collective-permute-start | bytes 196616 | tf_op jit(solution)/shard_map/ppermute | solution.py:114
  127.7 11.4 %collective-permute-start.13 = (bf16[32,1024]{1,0:T(8,128)(2,1)S(1)}, bf16[32,1024]{1,0:T(8,128)(2,1)S(1)}, u32[]{:S(2)}, u32[]{:S(2)}) collective-permute-start(bf16[32,1024]{1,0:T(8,128)(2,1)S(1)} %get-tuple-element.44), channel_id=1, source_target_pairs={{64,160},{96,192},{65,161},{97,193},{66,162},{98,194},{67,163},{99... | collective-permute-start | bytes 196616 | tf_op jit(solution)/shard_map/ppermute | solution.py:114
  128.4 11.4 %collective-permute-start.6 = (bf16[32,1024]{1,0:T(8,128)(2,1)S(1)}, bf16[32,1024]{1,0:T(8,128)(2,1)S(1)}, u32[]{:S(2)}, u32[]{:S(2)}) collective-permute-start(bf16[32,1024]{1,0:T(8,128)(2,1)S(1)} %get-tuple-element.45), channel_id=1, source_target_pairs={{0,160},{32,192},{64,224},{1,161},{33,193},{65,225},{2,162},{34,19... | collective-permute-start | bytes 196616 | tf_op jit(solution)/shard_map/ppermute | solution.py:114
  131.2 9.5 %collective-permute-start.14 = (bf16[32,1024]{1,0:T(8,128)(2,1)S(1)}, bf16[32,1024]{1,0:T(8,128)(2,1)S(1)}, u32[]{:S(2)}, u32[]{:S(2)}) collective-permute-start(bf16[32,1024]{1,0:T(8,128)(2,1)S(1)} %convolution_convert_fusion.5), channel_id=1, source_target_pairs={{128,160},{129,161},{130,162},{131,163},{132,164},{133,165},{134,1... | collective-permute-start | bytes 196616 | tf_op jit(solution)/shard_map/ppermute | solution.py:114
  132.6 11.0 %collective-permute-start.18 = (bf16[32,1024]{1,0:T(8,128)(2,1)S(1)}, bf16[32,1024]{1,0:T(8,128)(2,1)S(1)}, u32[]{:S(2)}, u32[]{:S(2)}) collective-permute-start(bf16[32,1024]{1,0:T(8,128)(2,1)S(1)} %convolution_convert_fusion.1), channel_id=1, source_target_pairs={{128,192},{129,193},{130,194},{131,195},{132,196},{133,197},{134,1... | collective-permute-start | bytes 196616 | tf_op jit(solution)/shard_map/ppermute | solution.py:114
  134.0 10.9 %collective-permute-start.11 = (bf16[32,1024]{1,0:T(8,128)(2,1)S(1)}, bf16[32,1024]{1,0:T(8,128)(2,1)S(1)}, u32[]{:S(2)}, u32[]{:S(2)}) collective-permute-start(bf16[32,1024]{1,0:T(8,128)(2,1)S(1)} %get-tuple-element.43), channel_id=1, source_target_pairs={{0,192},{32,224},{1,193},{33,225},{2,194},{34,226},{3,195},{35,227... | collective-permute-start | bytes 196616 | tf_op jit(solution)/shard_map/ppermute | solution.py:114
  139.2 8.5 %collective-permute-start.10 = (bf16[32,1024]{1,0:T(8,128)(2,1)S(1)}, bf16[32,1024]{1,0:T(8,128)(2,1)S(1)}, u32[]{:S(2)}, u32[]{:S(2)}) collective-permute-start(bf16[32,1024]{1,0:T(8,128)(2,1)S(1)} %get-tuple-element.40), channel_id=1, source_target_pairs={{96,224},{97,225},{98,226},{99,227},{100,228},{101,229},{102,230},... | collective-permute-start | bytes 196616 | tf_op jit(solution)/shard_map/ppermute | solution.py:114
  139.9 7.9 %collective-permute-start.16 = (bf16[32,1024]{1,0:T(8,128)(2,1)S(1)}, bf16[32,1024]{1,0:T(8,128)(2,1)S(1)}, u32[]{:S(2)}, u32[]{:S(2)}) collective-permute-start(bf16[32,1024]{1,0:T(8,128)(2,1)S(1)} %get-tuple-element.42), channel_id=1, source_target_pairs={{128,224},{129,225},{130,226},{131,227},{132,228},{133,229},{134,2... | collective-permute-start | bytes 196616 | tf_op jit(solution)/shard_map/ppermute | solution.py:114
  142.2 3.4 %collective-permute-start.19 = (bf16[32,1024]{1,0:T(8,128)(2,1)S(1)}, bf16[32,1024]{1,0:T(8,128)(2,1)S(1)}, u32[]{:S(2)}, u32[]{:S(2)}) collective-permute-start(bf16[32,1024]{1,0:T(8,128)(2,1)S(1)} %convolution_convert_fusion.3), channel_id=1, source_target_pairs={{160,192},{161,193},{162,194},{163,195},{164,196},{165,197},{166,1... | collective-permute-start | bytes 196616 | tf_op jit(solution)/shard_map/ppermute | solution.py:114
  143.6 4.2 %collective-permute-start.17 = (bf16[32,1024]{1,0:T(8,128)(2,1)S(1)}, bf16[32,1024]{1,0:T(8,128)(2,1)S(1)}, u32[]{:S(2)}, u32[]{:S(2)}) collective-permute-start(bf16[32,1024]{1,0:T(8,128)(2,1)S(1)} %get-tuple-element.41), channel_id=1, source_target_pairs={{0,224},{1,225},{2,226},{3,227},{4,228},{5,229},{6,230},{7,231},{8... | collective-permute-start | bytes 196616 | tf_op jit(solution)/shard_map/ppermute | solution.py:114
  144.9 2.9 %collective-permute-start.15 = (bf16[32,1024]{1,0:T(8,128)(2,1)S(1)}, bf16[32,1024]{1,0:T(8,128)(2,1)S(1)}, u32[]{:S(2)}, u32[]{:S(2)}) collective-permute-start(bf16[32,1024]{1,0:T(8,128)(2,1)S(1)} %convolution_convert_fusion.2), channel_id=1, source_target_pairs={{160,224},{161,225},{162,226},{163,227},{164,228},{165,229},{166,2... | collective-permute-start | bytes 196616 | tf_op jit(solution)/shard_map/ppermute | solution.py:114
  147.1 0.7 collective-permute-start.20
  148.5 23.0 %copy-start.7 = (s32[4,1]{0,1:T(1,128)S(1)}, s32[4,1]{0,1:T(1,128)}, u32[]{:S(2)}) copy-start(s32[4,1]{0,1:T(1,128)} %param.11) | copy-start | bytes 52
  169.0 4.8 %collective-permute-start.21 = (bf16[16,32,1024]{2,1,0:T(8,128)(2,1)S(1)}, bf16[16,32,1024]{2,1,0:T(8,128)(2,1)}, u32[]{:S(2)}, u32[]{:S(2)}) collective-permute-start(bf16[16,32,1024]{2,1,0:T(8,128)(2,1)S(1)} %all_to_all.10), channel_id=1, source_target_pairs={{0,1},{1,0},{2,3},{3,2},{4,5},{5,4},{6,7},{7,6},{8,9},{9,8},{10,11... | collective-permute-start | bytes 3145736 | tf_op jit(solution)/shard_map/ppermute | solution.py:136
  175.6 1.2 copy-start.3
  175.9 19.3 %copy-start.4 = (bf16[8,128,1024]{2,1,0:T(8,128)(2,1)}, bf16[8,128,1024]{2,1,0:T(8,128)(2,1)S(1)}, u32[]{:S(2)}) copy-start(bf16[8,128,1024]{2,1,0:T(8,128)(2,1)S(1)} %broadcast_select_fusion) | copy-start | bytes 6291460
  177.3 19.0 %collective-permute-start.22 = (bf16[512,128]{0,1:T(8,128)(2,1)S(1)}, bf16[512,128]{0,1:T(8,128)(2,1)S(1)}, u32[]{:S(2)}, u32[]{:S(2)}) collective-permute-start(bf16[512,128]{0,1:T(8,128)(2,1)S(1)} %fusion.30), channel_id=1, source_target_pairs={{0,128},{32,160},{64,192},{96,224},{128,0},{160,32},{192,64},{224,... | collective-permute-start | bytes 393224 | tf_op jit(solution)/shard_map/ppermute | solution.py:156
  182.4 15.3 %collective-permute-start.23 = (bf16[512,128]{0,1:T(8,128)(2,1)S(1)}, bf16[512,128]{0,1:T(8,128)(2,1)S(1)}, u32[]{:S(2)}, u32[]{:S(2)}) collective-permute-start(bf16[512,128]{0,1:T(8,128)(2,1)S(1)} %fusion.29), channel_id=1, source_target_pairs={{0,96},{32,128},{64,160},{96,192},{128,224},{160,0},{192,32},{224,... | collective-permute-start | bytes 393224 | tf_op jit(solution)/shard_map/ppermute | solution.py:156
  188.1 15.7 %collective-permute-start.24 = (bf16[512,128]{0,1:T(8,128)(2,1)}, bf16[512,128]{0,1:T(8,128)(2,1)}, u32[]{:S(2)}, u32[]{:S(2)}) collective-permute-start(bf16[512,128]{0,1:T(8,128)(2,1)} %fusion.28), channel_id=1, source_target_pairs={{0,160},{32,192},{64,224},{96,0},{128,32},{160,64},{192,96},{224,1... | collective-permute-start | bytes 393224 | tf_op jit(solution)/shard_map/ppermute | solution.py:156
  189.3 14.5 %collective-permute-start.25 = (bf16[512,128]{0,1:T(8,128)(2,1)}, bf16[512,128]{0,1:T(8,128)(2,1)}, u32[]{:S(2)}, u32[]{:S(2)}) collective-permute-start(bf16[512,128]{0,1:T(8,128)(2,1)} %fusion.27), channel_id=1, source_target_pairs={{0,64},{32,96},{64,128},{96,160},{128,192},{160,224},{192,0},{224,... | collective-permute-start | bytes 393224 | tf_op jit(solution)/shard_map/ppermute | solution.py:156
  193.2 11.5 %collective-permute-start.26 = (bf16[512,128]{0,1:T(8,128)(2,1)}, bf16[512,128]{0,1:T(8,128)(2,1)}, u32[]{:S(2)}, u32[]{:S(2)}) collective-permute-start(bf16[512,128]{0,1:T(8,128)(2,1)} %fusion.26), channel_id=1, source_target_pairs={{0,192},{32,224},{64,0},{96,32},{128,64},{160,96},{192,128},{224,1... | collective-permute-start | bytes 393224 | tf_op jit(solution)/shard_map/ppermute | solution.py:156
  196.3 10.3 %copy-start.5 = (bf16[512,128]{0,1:T(8,128)(2,1)}, bf16[512,128]{0,1:T(8,128)(2,1)S(1)}, u32[]{:S(2)}) copy-start(bf16[512,128]{0,1:T(8,128)(2,1)S(1)} %collective-permute-done.22) | copy-start | bytes 393220
  196.3 10.3 %collective-permute-start.27 = (bf16[512,128]{0,1:T(8,128)(2,1)}, bf16[512,128]{0,1:T(8,128)(2,1)}, u32[]{:S(2)}, u32[]{:S(2)}) collective-permute-start(bf16[512,128]{0,1:T(8,128)(2,1)} %fusion.25), channel_id=1, source_target_pairs={{0,32},{32,64},{64,96},{96,128},{128,160},{160,192},{192,224},{224... | collective-permute-start | bytes 393224 | tf_op jit(solution)/shard_map/ppermute | solution.py:156
  197.6 9.0 %copy-start.6 = (bf16[512,128]{0,1:T(8,128)(2,1)}, bf16[512,128]{0,1:T(8,128)(2,1)S(1)}, u32[]{:S(2)}) copy-start(bf16[512,128]{0,1:T(8,128)(2,1)S(1)} %collective-permute-done.23) | copy-start | bytes 393220
  197.6 10.8 %collective-permute-start.28 = (bf16[512,128]{0,1:T(8,128)(2,1)}, bf16[512,128]{0,1:T(8,128)(2,1)}, u32[]{:S(2)}, u32[]{:S(2)}) collective-permute-start(bf16[512,128]{0,1:T(8,128)(2,1)} %fusion.24), channel_id=1, source_target_pairs={{0,224},{32,0},{64,32},{96,64},{128,96},{160,128},{192,160},{224,1... | collective-permute-start | bytes 393224 | tf_op jit(solution)/shard_map/ppermute | solution.py:156
Sparse Core Ops, SparseCore 0:
  10.6 81.7 all-gather.1

commit v4 on v3

--- a/solution.py
+++ b/solution.py
@@ -10,11 +10,10 @@
 BF16 = jnp.bfloat16
 ROWS = ("chip", "core")
 FAR_SENDS = {
-    1: ((3, (0, 1)),),
-    2: ((4, (0, 1, 2)),),
-    3: ((3, (2, 3)), (5, (0, 1, 2))),
-    4: ((4, (3,)), (6, (0, 1))),
-    5: ((3, (4,)), (7, (0,))),
+    2: ((4, (0, 1)),),
+    3: ((5, (0, 1, 2)),),
+    4: ((4, (2, 3)), (6, (0, 1))),
+    5: ((7, (0,)),),
 }
 
 
@@ -31,14 +30,14 @@
     count, panels = weights.shape[0], whole_ref.shape[0]
 
     def load(i):
-        return pltpu.make_async_copy(whole_ref.at[z + 3 + i], weights.at[i], loaded.at[i])
+        return pltpu.make_async_copy(whole_ref.at[z + 4 + i], weights.at[i], loaded.at[i])
 
     def store(i):
         return pltpu.make_async_copy(products.at[i], out_ref.at[i], stored.at[i])
 
     @pl.when(place_ref[1] == 1)
     def _():
-        valid = jnp.minimum(count, panels - 3 - z)
+        valid = jnp.minimum(count, panels - 4 - z)
         lax.fori_loop(0, valid, lambda i, _: load(i).start(), None)
 
         def multiply(i, _):
@@ -72,7 +71,12 @@
         ),
         out_shape=jax.ShapeDtypeStruct(kept.shape, BF16),
         input_output_aliases={3: 0},
-        compiler_params=pltpu.CompilerParams(vmem_limit_bytes=16 * 2**20),
+        compiler_params=pltpu.CompilerParams(vmem_limit_bytes=48 * 2**20),
+        cost_estimate=pl.CostEstimate(
+            flops=2 * count * share * width * width,
+            bytes_accessed=2 * count * width * width,
+            transcendentals=0,
+        ),
         name="later_products",
     )(jnp.stack([z, turn.astype(jnp.int32)]), solved, whole, kept)
 
@@ -99,15 +103,24 @@
     own = lax.dynamic_slice_in_dim(pieces, owners * z, owners, 0)
     own_rhs = own.transpose(1, 0, 2).reshape(share, width).astype(F32)
 
+    def swap(value):
+        return lax.ppermute(value, "core", [(0, 1), (1, 0)])
+
+    tall = tall_blocks[0] * sparsity[:, 0].astype(BF16)[:, None, None]
+    tall = tall.reshape(-1, width)
+    tall_rows = tall.shape[0]
+    both_tall = jnp.concatenate([tall, swap(tall)])
+    own_rhs, both_tall = lax.optimization_barrier((own_rhs, both_tall))
+
     inverse = diag_inverse[0]
     def ahead(distance):
         index = jnp.minimum(z + distance, panels - 1)
         return lax.dynamic_index_in_dim(whole, index, 0, keepdims=False)
 
-    following, second = lax.optimization_barrier((ahead(1), ahead(2)))
+    following, second, third = lax.optimization_barrier((ahead(1), ahead(2), ahead(3)))
 
     solved = jnp.zeros((share, width), BF16)
-    kept = jnp.zeros((panels - 3, share, width), BF16)
+    kept = jnp.zeros((panels - 4, share, width), BF16)
     arrivals = [[] for _ in range(panels)]
 
     def send(value, senders, distance):
@@ -121,41 +134,52 @@
         solved = jnp.where(z == k, fresh, solved)
         if k == panels - 1:
             break
+        if k > 0:
+            fresh, previous = lax.optimization_barrier((fresh, previous))
         near = times(fresh, following).astype(BF16)
         near, fresh = lax.optimization_barrier((near, fresh))
         send(near, [k], 1)
         if k < panels - 2:
             send(times(fresh, second).astype(BF16), [k], 2)
         if k < panels - 3:
-            kept = later_products(z, z == k, fresh, whole, kept)
+            send(times(fresh, third).astype(BF16), [k], 3)
+        if 0 < k < panels - 3:
+            kept = later_products(z, z == k - 1, previous, whole, kept)
+        previous = fresh
         for distance, senders in FAR_SENDS.get(k, ()):
-            send(kept[distance - 3], senders, distance)
+            send(kept[distance - 4], senders, distance)
     mine = lax.all_to_all(
         jnp.broadcast_to(solved[None], (chips, share, width)), "chip", 0, 0, tiled=True
     )
-    other = lax.ppermute(mine, "core", [(0, 1), (1, 0)])
-    sources = lax.broadcasted_iota(jnp.int32, (1, 2, 1, 1), 1)
-    full = jnp.where(sources == core, mine[:, None], other[:, None])
-    full = full.reshape(batches, columns, width)
-
-    own_rows = lax.dynamic_slice_in_dim(full, rows_index * slice_rows, slice_rows, 2)
-    solution_rows = own_rows.transpose(0, 2, 1).astype(F32)
-
-    blocks, block_rows = tall_blocks.shape[1], tall_blocks.shape[2]
-    tall = tall_blocks[0].reshape(blocks * block_rows, width)
-    mask = jnp.repeat(sparsity[:, 0].astype(F32), block_rows)[:, None]
-
-    def product(batch):
-        term = times(tall, lax.dynamic_index_in_dim(full, batch, 0, keepdims=False))
-        return term * mask
-
-    summed = jnp.zeros((blocks * block_rows, columns), F32)
-    for distance in sorted(range(1, panels), key=lambda d: abs(2 * d - panels)):
-        term = product(lax.rem(z + distance, panels)).astype(BF16)
+    products = times(mine.reshape(-1, width), both_tall).astype(BF16)
+    products = products.reshape(batches, -1, 2 * tall_rows)
+
+    def part(batch):
+        return lax.dynamic_index_in_dim(products, batch, 0, keepdims=False)
+
+    summed = part(z).astype(F32)
+    for distance in sorted(range(1, panels), key=lambda d: -abs(2 * d - panels)):
         route = [(s, (s + distance) % panels) for s in range(panels)]
-        summed = summed + lax.ppermute(term, "panel", route).astype(F32)
-    summed = summed + product(z)
-    return solution_rows[None], rhs_tall.astype(F32) - summed[None]
+        moved = lax.ppermute(part(lax.rem(z + distance, panels)), "panel", route)
+        summed = summed + moved.astype(F32)
+
+    def in_order(own, other):
+        lead, rows = own.shape[:-2], own.shape[-1]
+        own = own.reshape(*lead, -1, 1, share, rows)
+        other = other.reshape(*lead, -1, 1, share, rows)
+        sides = lax.broadcasted_iota(jnp.int32, (2, 1, 1), 0)
+        whole_row = jnp.where(sides == core, own, other).reshape(*lead, columns, rows)
+        return jnp.swapaxes(whole_row, -1, -2)
+
+    def rows_of(index):
+        rows = lax.dynamic_slice_in_dim(mine, index * slice_rows, slice_rows, 2)
+        return rows.reshape(batches, -1, slice_rows)
+
+    other_rows = swap(rows_of(rows_index + 1 - 2 * core))
+    solution_rows = in_order(rows_of(rows_index), other_rows).astype(F32)
+
+    tall_sum = in_order(summed[:, :tall_rows], swap(summed[:, tall_rows:]))
+    return solution_rows[None], rhs_tall.astype(F32) - tall_sum[None]
 
 
 def solution(mesh):

time: 219 us -> 218 us (level)
  blocking collectives: 20.3 us -> 0 us
  waiting for transfers between devices: 81.3 us -> 95.8 us
  starting transfers between devices: 50.2 us -> 58.2 us
  local copies, waits for them, and re-layouts: 17.4 us -> 11.2 us
  other arithmetic: 2.41 us -> 7.78 us
    all_to_all x1 -> x0, blocking collectives: 20.3 us -> none  [per_device(): lax.all_to_all(jnp.broadcast_to(solved[None], (chips, share, width)), 'ch...]
    all_to_all x0 -> x1, waiting for transfers between devices: none -> 15.1 us  [per_device(): lax.all_to_all(jnp.broadcast_to(solved[None], (chips, share, width)), 'ch...]
    unnamed x21 -> x7, local copies, waits for them, and re-layouts: 12.5 us -> 3.93 us
    ppermute x8 -> x10, starting transfers between devices: 16.8 us -> 24.9 us  [the longest x7 15.8 us: per_device(): moved = lax.ppermute(part(lax.rem(z + distance, panels)), 'panel', route)]
    all_gather x1, waiting for transfers between devices: 61.4 us -> 55.9 us  [per_device(): whole = lax.all_gather(coupling[0], ROWS).reshape(panels, width, width)]
    ppermute x8 -> x10, waiting for transfers between devices: 7.85 us -> 12.7 us  [the longest x7 12.4 us: per_device(): moved = lax.ppermute(part(lax.rem(z + distance, panels)), 'panel', route)]
    all_to_all x0 -> x1, starting transfers between devices: none -> 4.8 us  [per_device(): lax.all_to_all(jnp.broadcast_to(solved[None], (chips, share, width)), 'ch...]
    all_to_all x1, starting transfers between devices: 8.59 us -> 5.52 us  [per_device(): pieces = lax.all_to_all(pieces, ROWS, 0, 0, tiled=True)]
  transfers between devices with their start and end apart: 31 -> 36, of which waited for: 7 -> 9; matrix products, arithmetic and copies ran while one was open for 13% -> 13% of each run, Pallas kernels for 4% -> 3%
where the time goes in v4:
time: 218 us; the launch traced here: 217 us
  waiting for transfers between devices  95.8 us (44%)
  starting transfers between devices  58.2 us (27%)
  matrix products  21.7 us (10%)
  between operations  14.8 us (7%)
  local copies, waits for them, and re-layouts  11.2 us (5%)
  other arithmetic  7.78 us (4%)
  Pallas kernels  7.48 us (3%)
    all_gather x1, waiting for transfers between devices, per_device(): whole = lax.all_gather(coupling[0], ROWS).reshape(panels, width, width)  55.9 us
    ppermute x23, starting transfers between devices, send(): moved = lax.ppermute(value, 'panel', [(s, s + distance) for s in senders])  22.9 us
    dot_general x27, matrix products, times(): lax.dot_general(left, weight, (((1,), (1,)), ((), ())), preferred_element...  21.7 us
    ppermute x7, starting transfers between devices, per_device(): moved = lax.ppermute(part(lax.rem(z + distance, panels)), 'panel', route)  15.8 us
    all_to_all x1, waiting for transfers between devices, per_device(): lax.all_to_all(jnp.broadcast_to(solved[None], (chips, share, width)), 'ch...  15.1 us
    ppermute x7, waiting for transfers between devices, per_device(): moved = lax.ppermute(part(lax.rem(z + distance, panels)), 'panel', route)  12.4 us
    all_to_all x1, waiting for transfers between devices, per_device(): pieces = lax.all_to_all(pieces, ROWS, 0, 0, tiled=True)  11.4 us
    ppermute x3, starting transfers between devices, swap(): return lax.ppermute(value, 'core', [(0, 1), (1, 0)])  9.1 us
  transfers between devices with their start and end apart: 36, of which 9 were waited for; matrix products, arithmetic and copies ran while one was open for 13% of the time, Pallas kernels for 3%

profile of v4, /device:TPU:1, one launch (start us, length us, event | category | flops | bytes accessed | tf_op | source)
XLA Modules:
  0.0 217.0 jit_solution(16711637546343910128)
XLA Ops:
  7.2 0.7 all-gather.2.cloned.1.call-update
  8.6 1.4 bitcast_multiply_fusion
  10.0 3.3 %collective-permute-start = (bf16[512,1024]{1,0:T(8,128)(2,1)S(1)}, bf16[512,1024]{1,0:T(8,128)(2,1)}, u32[]{:S(2)}, u32[]{:S(2)}) collective-permute-start(bf16[512,1024]{1,0:T(8,128)(2,1)S(1)} %bitcast_multiply_fusion), channel_id=1, source_target_pairs={{0,1},{1,0},{2,3},{3,2},{4,5},{5,4},{6,7},{7,6},{8,9},{9,8},{10,11... | collective-permute-start | bytes 3145736 | tf_op jit(solution)/shard_map/ppermute | solution.py:107
  13.3 2.1 copy.22
  15.4 5.5 %all-to-all-start = ((bf16[32,32,256]{2,1,0:T(8,128)(2,1)}), bf16[32,32,256]{2,1,0:T(8,128)(2,1)}, u32[]{:S(2)}, u32[]{:S(2)}) async-start(bf16[32,32,256]{2,1,0:T(8,128)(2,1)} %bitcast.166), calls=%async_computation | async-start | bytes 1048576 | tf_op jit(solution)/shard_map/all_to_all | solution.py:102
  21.1 11.4 %all-to-all-done = bf16[32,32,256]{2,1,0:T(8,128)(2,1)} async-done(((bf16[32,32,256]{2,1,0:T(8,128)(2,1)}), bf16[32,32,256]{2,1,0:T(8,128)(2,1)}, u32[]{:S(2)}, u32[]{:S(2)}) %all-to-all-start) | async-done | bytes 524320 | tf_op jit(solution)/shard_map/all_to_all | solution.py:102
  32.5 0.8 convert_bitcast_fusion.1
  33.4 2.7 %pad_maximum_fusion = bf16[1024,1024]{1,0:T(8,128)(2,1)} fusion(bf16[512,1024]{1,0:T(8,128)(2,1)} %collective-permute-done, bf16[512,1024]{1,0:T(8,128)(2,1)S(1)} %bitcast_multiply_fusion), kind=kLoop, calls=%fused_computation | loop fusion | flops 4194304 | bytes 4194304 | tf_op jit(solution)/shard_map/concatenate | solution.py:112
  36.2 0.7 fusion.16.solved_ref
  36.9 55.9 %all-gather.2.cloned.1.call-done = bf16[32,256,1024]{2,1,0:T(8,128)(2,1)} async-done(((bf16[1,256,1024]{2,1,0:T(8,128)(2,1)}), bf16[32,256,1024]{2,1,0:T(8,128)(2,1)}) %all-gather.2.cloned.1.call-update) | async-done | bytes 16777232 | tf_op jit(solution)/shard_map/all_gather | solution.py:98
  92.8 3.6 %dynamic-slice_bitcast_fusion = (bf16[1024,1024]{1,0:T(8,128)(2,1)S(1)}, bf16[1024,1024]{1,0:T(8,128)(2,1)S(1)}, bf16[1024,1024]{1,0:T(8,128)(2,1)S(1)}) fusion(bf16[8,1024,1024]{2,1,0:T(8,128)(2,1)} %bitcast.153, s32[]{:T(128)S(6)} %select_n.108, s32[]{:T(128)S(6)} %select_n.107, s32[]{:T(128)S(6)} %select_n.106), kind=kLoop, calls=%fused_computation.17 | loop fusion | bytes 12582924 | tf_op jit(solution)/shard_map/jit(dynamic_index_in_dim)/squeeze | solution.py:118
  96.4 0.7 convolution_convert_fusion.18
  97.1 3.2 %collective-permute-start.2 = (bf16[32,1024]{1,0:T(8,128)(2,1)S(1)}, bf16[32,1024]{1,0:T(8,128)(2,1)S(1)}, u32[]{:S(2)}, u32[]{:S(2)}) collective-permute-start(bf16[32,1024]{1,0:T(8,128)(2,1)S(1)} %convolution_convert_fusion.18), channel_id=1, source_target_pairs={{0,32},{1,33},{2,34},{3,35},{4,36},{5,37},{6,38},{7,39},{8,40},{9,... | collective-permute-start | bytes 196616 | tf_op jit(solution)/shard_map/ppermute | solution.py:127
  100.3 0.7 convolution_convert_fusion.14
  101.0 1.7 collective-permute-start.4
  102.7 0.7 convolution_convert_fusion.17
  103.4 1.7 collective-permute-start.1
  105.1 0.7 fusion.19.solved_ref
  105.8 0.7 convolution_convert_fusion.16
  107.2 0.7 convolution_convert_fusion.15
  107.9 0.7 convolution_convert_fusion.12
  110.0 5.4 %later_products.4.kept_ref = bf16[4,32,1024]{2,1,0:T(8,128)(2,1)S(1)} custom-call(s32[2]{0:T(128)S(1)} %get-tuple-element.81.place_ref, bf16[32,1024]{1,0:T(8,128)(2,1)S(1)} %fusion.16.solved_ref, bf16[8,1024,1024]{2,1,0:T(8,128)(2,1)} %bitcast.154, bf16[4,32,1024]{2,1,0:T(8,128)(2,1)S(1)} %broadcast_in_dim.93.kept_ref), custom_call_target="tpu_custom_call", output_to_operand_aliasing={{}: (3, {})} | custom-call | flops 268435456 | bytes 8388608 | tf_op jit(solution)/shard_map/later_products/pallas_call | solution.py:54
  115.5 0.7 fusion.22.solved_ref
  116.2 0.7 convolution_convert_fusion.13
  116.9 0.7 convolution_convert_fusion.11
  117.7 0.7 convolution_convert_fusion.7
  119.7 1.3 collective-permute-start.10
  122.4 0.7 fusion.25.solved_ref
  123.1 0.7 convolution_convert_fusion.10
  123.8 0.7 convolution_convert_fusion.6
  124.6 0.7 convolution_convert_fusion.3
  126.0 0.8 later_products.6.kept_ref
  126.8 1.3 collective-permute-start.7
  129.5 0.7 fusion.28
  130.2 0.7 convolution_convert_fusion.9
  130.9 0.7 convolution_convert_fusion.2
  131.7 0.7 convolution_convert_fusion.8
  133.8 1.3 collective-permute-start.14
  136.4 0.7 fusion.31
  137.1 0.7 convolution_convert_fusion.5
  138.6 0.7 convolution_convert_fusion.4
  139.3 1.8 collective-permute-start.19
  142.5 0.7 fusion.34
  143.3 0.7 convolution_convert_fusion.1
  144.7 0.7 fusion.40
  145.5 1.1 broadcast_in_dim.95
  146.6 4.8 %all-to-all-start.1 = ((bf16[16,32,1024]{2,1,0:T(8,128)(2,1)}), bf16[16,32,1024]{2,1,0:T(8,128)(2,1)S(1)}, u32[]{:S(2)}, u32[]{:S(2)}) async-start(bf16[16,32,1024]{2,1,0:T(8,128)(2,1)} %broadcast_in_dim.95), calls=%async_computation.1 | async-start | bytes 2097152 | tf_op jit(solution)/shard_map/all_to_all | solution.py:151
  151.5 15.1 %all-to-all-done.1 = bf16[16,32,1024]{2,1,0:T(8,128)(2,1)S(1)} async-done(((bf16[16,32,1024]{2,1,0:T(8,128)(2,1)}), bf16[16,32,1024]{2,1,0:T(8,128)(2,1)S(1)}, u32[]{:S(2)}, u32[]{:S(2)}) %all-to-all-start.1) | async-done | bytes 1048608 | tf_op jit(solution)/shard_map/all_to_all | solution.py:151
  166.5 2.9 %convolution_convert_fusion = bf16[512,1024]{1,0:T(8,128)(2,1)S(1)} fusion(bf16[512,1024]{1,0:T(8,128)(2,1)S(1)} %bitcast.167, bf16[1024,1024]{1,0:T(8,128)(2,1)} %pad_maximum_fusion), kind=kOutput, calls=%fused_computation.20 | convolution fusion | flops 1074266112 | bytes 4194304 | tf_op jit(solution)/shard_map/dot_general | solution.py:21
  169.4 1.0 dynamic-slice_bitcast_fusion.9
  170.4 5.3 %collective-permute-start.31 = (bf16[64,1024]{1,0:T(8,128)(2,1)}, bf16[64,1024]{1,0:T(8,128)(2,1)}, u32[]{:S(2)}, u32[]{:S(2)}) collective-permute-start(bf16[64,1024]{1,0:T(8,128)(2,1)} %get-tuple-element.66), channel_id=1, source_target_pairs={{0,128},{32,160},{64,192},{96,224},{128,0},{160,32},{192,64},{224,... | collective-permute-start | bytes 393224 | tf_op jit(solution)/shard_map/ppermute | solution.py:163
  175.7 0.9 collective-permute-start.30
  176.9 4.8 %collective-permute-start.24 = (bf16[8,64,32]{1,0,2:T(8,128)(2,1)S(1)}, bf16[8,64,32]{1,0,2:T(8,128)(2,1)S(1)}, u32[]{:S(2)}, u32[]{:S(2)}) collective-permute-start(bf16[8,64,32]{1,0,2:T(8,128)(2,1)S(1)} %copy.29), channel_id=1, source_target_pairs={{0,1},{1,0},{2,3},{3,2},{4,5},{5,4},{6,7},{7,6},{8,9},{9,8},{10,11... | collective-permute-start | bytes 98312 | tf_op jit(solution)/shard_map/ppermute | solution.py:107
  181.6 4.6 %collective-permute-start.29 = (bf16[64,1024]{1,0:T(8,128)(2,1)}, bf16[64,1024]{1,0:T(8,128)(2,1)S(1)}, u32[]{:S(2)}, u32[]{:S(2)}) collective-permute-start(bf16[64,1024]{1,0:T(8,128)(2,1)} %get-tuple-element.68), channel_id=1, source_target_pairs={{0,96},{32,128},{64,160},{96,192},{128,224},{160,0},{192,32},{224,... | collective-permute-start | bytes 393224 | tf_op jit(solution)/shard_map/ppermute | solution.py:163
  186.2 2.7 %collective-permute-start.28 = (bf16[64,1024]{1,0:T(8,128)(2,1)}, bf16[64,1024]{1,0:T(8,128)(2,1)S(1)}, u32[]{:S(2)}, u32[]{:S(2)}) collective-permute-start(bf16[64,1024]{1,0:T(8,128)(2,1)} %get-tuple-element.69), channel_id=1, source_target_pairs={{0,192},{32,224},{64,0},{96,32},{128,64},{160,96},{192,128},{224,1... | collective-permute-start | bytes 393224 | tf_op jit(solution)/shard_map/ppermute | solution.py:163
  189.5 1.8 collective-permute-start.26
  191.7 1.0 copy.27
  193.7 2.4 %collective-permute-done.29 = bf16[64,1024]{1,0:T(8,128)(2,1)S(1)} collective-permute-done((bf16[64,1024]{1,0:T(8,128)(2,1)}, bf16[64,1024]{1,0:T(8,128)(2,1)S(1)}, u32[]{:S(2)}, u32[]{:S(2)}) %collective-permute-start.29) | collective-permute-done | bytes 131104 | tf_op jit(solution)/shard_map/ppermute | solution.py:163
  196.2 1.1 collective-permute-done.28
  197.3 6.2 %collective-permute-done.27 = bf16[64,1024]{1,0:T(8,128)(2,1)S(1)} collective-permute-done((bf16[64,1024]{1,0:T(8,128)(2,1)}, bf16[64,1024]{1,0:T(8,128)(2,1)S(1)}, u32[]{:S(2)}, u32[]{:S(2)}) %collective-permute-start.27) | collective-permute-done | bytes 131104 | tf_op jit(solution)/shard_map/ppermute | solution.py:163
  203.5 2.4 %collective-permute-done.25 = bf16[64,1024]{1,0:T(8,128)(2,1)} collective-permute-done((bf16[64,1024]{1,0:T(8,128)(2,1)S(1)}, bf16[64,1024]{1,0:T(8,128)(2,1)}, u32[]{:S(2)}, u32[]{:S(2)}) %collective-permute-start.25) | collective-permute-done | bytes 131104 | tf_op jit(solution)/shard_map/ppermute | solution.py:163
  205.9 1.3 fusion.48
  207.2 1.0 collective-permute-start.32
  209.3 0.8 copy.28
  (78 shorter events, 16.4 us)
Async XLA Ops:
  7.2 29.0 %copy-start = (bf16[1,1024,1024]{2,1,0:T(8,128)(2,1)S(1)}, bf16[1,1024,1024]{2,1,0:T(8,128)(2,1)}, u32[]{:S(2)}) copy-start(bf16[1,1024,1024]{2,1,0:T(8,128)(2,1)} %param.8) | copy-start | bytes 6291460
  7.2 85.6 %all-gather.2.cloned.1.call-start = ((), (), s32[]{:S(2)}) async-start(), calls=%async_computation.2 | async-start | bytes 17301504 | tf_op jit(solution)/shard_map/all_gather | solution.py:98
  10.0 23.4 %collective-permute-start = (bf16[512,1024]{1,0:T(8,128)(2,1)S(1)}, bf16[512,1024]{1,0:T(8,128)(2,1)}, u32[]{:S(2)}, u32[]{:S(2)}) collective-permute-start(bf16[512,1024]{1,0:T(8,128)(2,1)S(1)} %bitcast_multiply_fusion), channel_id=1, source_target_pairs={{0,1},{1,0},{2,3},{3,2},{4,5},{5,4},{6,7},{7,6},{8,9},{9,8},{10,11... | collective-permute-start | bytes 3145736 | tf_op jit(solution)/shard_map/ppermute | solution.py:107
  15.4 17.1 %all-to-all-start = ((bf16[32,32,256]{2,1,0:T(8,128)(2,1)}), bf16[32,32,256]{2,1,0:T(8,128)(2,1)}, u32[]{:S(2)}, u32[]{:S(2)}) async-start(bf16[32,32,256]{2,1,0:T(8,128)(2,1)} %bitcast.166), calls=%async_computation | async-start | bytes 1048576 | tf_op jit(solution)/shard_map/all_to_all | solution.py:102
  97.1 8.0 %collective-permute-start.2 = (bf16[32,1024]{1,0:T(8,128)(2,1)S(1)}, bf16[32,1024]{1,0:T(8,128)(2,1)S(1)}, u32[]{:S(2)}, u32[]{:S(2)}) collective-permute-start(bf16[32,1024]{1,0:T(8,128)(2,1)S(1)} %convolution_convert_fusion.18), channel_id=1, source_target_pairs={{0,32},{1,33},{2,34},{3,35},{4,36},{5,37},{6,38},{7,39},{8,40},{9,... | collective-permute-start | bytes 196616 | tf_op jit(solution)/shard_map/ppermute | solution.py:127
  101.0 14.5 %collective-permute-start.4 = (bf16[32,1024]{1,0:T(8,128)(2,1)S(1)}, bf16[32,1024]{1,0:T(8,128)(2,1)S(1)}, u32[]{:S(2)}, u32[]{:S(2)}) collective-permute-start(bf16[32,1024]{1,0:T(8,128)(2,1)S(1)} %convolution_convert_fusion.14), channel_id=1, source_target_pairs={{0,64},{1,65},{2,66},{3,67},{4,68},{5,69},{6,70},{7,71},{8,72},{9,... | collective-permute-start | bytes 196616 | tf_op jit(solution)/shard_map/ppermute | solution.py:127
  103.4 17.6 %collective-permute-start.1 = (bf16[32,1024]{1,0:T(8,128)(2,1)S(1)}, bf16[32,1024]{1,0:T(8,128)(2,1)S(1)}, u32[]{:S(2)}, u32[]{:S(2)}) collective-permute-start(bf16[32,1024]{1,0:T(8,128)(2,1)S(1)} %convolution_convert_fusion.17), channel_id=1, source_target_pairs={{0,96},{1,97},{2,98},{3,99},{4,100},{5,101},{6,102},{7,103},{8,104... | collective-permute-start | bytes 196616 | tf_op jit(solution)/shard_map/ppermute | solution.py:127
  106.5 9.0 %collective-permute-start.5 = (bf16[32,1024]{1,0:T(8,128)(2,1)S(1)}, bf16[32,1024]{1,0:T(8,128)(2,1)S(1)}, u32[]{:S(2)}, u32[]{:S(2)}) collective-permute-start(bf16[32,1024]{1,0:T(8,128)(2,1)S(1)} %convolution_convert_fusion.16), channel_id=1, source_target_pairs={{32,64},{33,65},{34,66},{35,67},{36,68},{37,69},{38,70},{39,71},{4... | collective-permute-start | bytes 196616 | tf_op jit(solution)/shard_map/ppermute | solution.py:127
  108.6 13.1 %collective-permute-start.3 = (bf16[32,1024]{1,0:T(8,128)(2,1)S(1)}, bf16[32,1024]{1,0:T(8,128)(2,1)S(1)}, u32[]{:S(2)}, u32[]{:S(2)}) collective-permute-start(bf16[32,1024]{1,0:T(8,128)(2,1)S(1)} %convolution_convert_fusion.15), channel_id=1, source_target_pairs={{32,96},{33,97},{34,98},{35,99},{36,100},{37,101},{38,102},{39,103... | collective-permute-start | bytes 196616 | tf_op jit(solution)/shard_map/ppermute | solution.py:127
  109.3 17.5 %collective-permute-start.8 = (bf16[32,1024]{1,0:T(8,128)(2,1)S(1)}, bf16[32,1024]{1,0:T(8,128)(2,1)S(1)}, u32[]{:S(2)}, u32[]{:S(2)}) collective-permute-start(bf16[32,1024]{1,0:T(8,128)(2,1)S(1)} %convolution_convert_fusion.12), channel_id=1, source_target_pairs={{32,128},{33,129},{34,130},{35,131},{36,132},{37,133},{38,134},{39... | collective-permute-start | bytes 196616 | tf_op jit(solution)/shard_map/ppermute | solution.py:127
  118.4 4.0 %collective-permute-start.6 = (bf16[32,1024]{1,0:T(8,128)(2,1)S(1)}, bf16[32,1024]{1,0:T(8,128)(2,1)S(1)}, u32[]{:S(2)}, u32[]{:S(2)}) collective-permute-start(bf16[32,1024]{1,0:T(8,128)(2,1)S(1)} %convolution_convert_fusion.13), channel_id=1, source_target_pairs={{64,96},{65,97},{66,98},{67,99},{68,100},{69,101},{70,102},{71,103... | collective-permute-start | bytes 196616 | tf_op jit(solution)/shard_map/ppermute | solution.py:127
  119.7 8.4 %collective-permute-start.10 = (bf16[32,1024]{1,0:T(8,128)(2,1)S(1)}, bf16[32,1024]{1,0:T(8,128)(2,1)S(1)}, u32[]{:S(2)}, u32[]{:S(2)}) collective-permute-start(bf16[32,1024]{1,0:T(8,128)(2,1)S(1)} %slice_bitcast_fusion.3), channel_id=1, source_target_pairs={{0,128},{32,160},{1,129},{33,161},{2,130},{34,162},{3,131},{35,163... | collective-permute-start | bytes 196616 | tf_op jit(solution)/shard_map/ppermute | solution.py:127
  121.0 7.8 %collective-permute-start.9 = (bf16[32,1024]{1,0:T(8,128)(2,1)S(1)}, bf16[32,1024]{1,0:T(8,128)(2,1)S(1)}, u32[]{:S(2)}, u32[]{:S(2)}) collective-permute-start(bf16[32,1024]{1,0:T(8,128)(2,1)S(1)} %convolution_convert_fusion.11), channel_id=1, source_target_pairs={{64,128},{65,129},{66,130},{67,131},{68,132},{69,133},{70,134},{71... | collective-permute-start | bytes 196616 | tf_op jit(solution)/shard_map/ppermute | solution.py:127
  121.7 12.0 %collective-permute-start.15 = (bf16[32,1024]{1,0:T(8,128)(2,1)S(1)}, bf16[32,1024]{1,0:T(8,128)(2,1)S(1)}, u32[]{:S(2)}, u32[]{:S(2)}) collective-permute-start(bf16[32,1024]{1,0:T(8,128)(2,1)S(1)} %convolution_convert_fusion.7), channel_id=1, source_target_pairs={{64,160},{65,161},{66,162},{67,163},{68,164},{69,165},{70,166},{71... | collective-permute-start | bytes 196616 | tf_op jit(solution)/shard_map/ppermute | solution.py:127
  125.3 4.2 %collective-permute-start.11 = (bf16[32,1024]{1,0:T(8,128)(2,1)S(1)}, bf16[32,1024]{1,0:T(8,128)(2,1)S(1)}, u32[]{:S(2)}, u32[]{:S(2)}) collective-permute-start(bf16[32,1024]{1,0:T(8,128)(2,1)S(1)} %convolution_convert_fusion.10), channel_id=1, source_target_pairs={{96,128},{97,129},{98,130},{99,131},{100,132},{101,133},{102,134},... | collective-permute-start | bytes 196616 | tf_op jit(solution)/shard_map/ppermute | solution.py:127
  126.8 8.2 %collective-permute-start.7 = (bf16[32,1024]{1,0:T(8,128)(2,1)S(1)}, bf16[32,1024]{1,0:T(8,128)(2,1)S(1)}, u32[]{:S(2)}, u32[]{:S(2)}) collective-permute-start(bf16[32,1024]{1,0:T(8,128)(2,1)S(1)} %slice_bitcast_fusion.4), channel_id=1, source_target_pairs={{0,160},{32,192},{64,224},{1,161},{33,193},{65,225},{2,162},{34,19... | collective-permute-start | bytes 196616 | tf_op jit(solution)/shard_map/ppermute | solution.py:127
  128.1 7.6 %collective-permute-start.16 = (bf16[32,1024]{1,0:T(8,128)(2,1)S(1)}, bf16[32,1024]{1,0:T(8,128)(2,1)S(1)}, u32[]{:S(2)}, u32[]{:S(2)}) collective-permute-start(bf16[32,1024]{1,0:T(8,128)(2,1)S(1)} %convolution_convert_fusion.6), channel_id=1, source_target_pairs={{96,160},{97,161},{98,162},{99,163},{100,164},{101,165},{102,166},... | collective-permute-start | bytes 196616 | tf_op jit(solution)/shard_map/ppermute | solution.py:127
  128.8 10.5 %collective-permute-start.20 = (bf16[32,1024]{1,0:T(8,128)(2,1)S(1)}, bf16[32,1024]{1,0:T(8,128)(2,1)S(1)}, u32[]{:S(2)}, u32[]{:S(2)}) collective-permute-start(bf16[32,1024]{1,0:T(8,128)(2,1)S(1)} %convolution_convert_fusion.3), channel_id=1, source_target_pairs={{96,192},{97,193},{98,194},{99,195},{100,196},{101,197},{102,198},... | collective-permute-start | bytes 196616 | tf_op jit(solution)/shard_map/ppermute | solution.py:127
  132.4 4.0 %collective-permute-start.17 = (bf16[32,1024]{1,0:T(8,128)(2,1)S(1)}, bf16[32,1024]{1,0:T(8,128)(2,1)S(1)}, u32[]{:S(2)}, u32[]{:S(2)}) collective-permute-start(bf16[32,1024]{1,0:T(8,128)(2,1)S(1)} %convolution_convert_fusion.9), channel_id=1, source_target_pairs={{128,160},{129,161},{130,162},{131,163},{132,164},{133,165},{134,1... | collective-permute-start | bytes 196616 | tf_op jit(solution)/shard_map/ppermute | solution.py:127
  133.8 7.4 %collective-permute-start.14 = (bf16[32,1024]{1,0:T(8,128)(2,1)S(1)}, bf16[32,1024]{1,0:T(8,128)(2,1)S(1)}, u32[]{:S(2)}, u32[]{:S(2)}) collective-permute-start(bf16[32,1024]{1,0:T(8,128)(2,1)S(1)} %get-tuple-element.77), channel_id=1, source_target_pairs={{0,192},{32,224},{1,193},{33,225},{2,194},{34,226},{3,195},{35,227... | collective-permute-start | bytes 196616 | tf_op jit(solution)/shard_map/ppermute | solution.py:127
  135.1 6.8 %collective-permute-start.13 = (bf16[32,1024]{1,0:T(8,128)(2,1)S(1)}, bf16[32,1024]{1,0:T(8,128)(2,1)S(1)}, u32[]{:S(2)}, u32[]{:S(2)}) collective-permute-start(bf16[32,1024]{1,0:T(8,128)(2,1)S(1)} %get-tuple-element.78), channel_id=1, source_target_pairs={{64,192},{96,224},{65,193},{97,225},{66,194},{98,226},{67,195},{99... | collective-permute-start | bytes 196616 | tf_op jit(solution)/shard_map/ppermute | solution.py:127
  135.7 6.8 %collective-permute-start.21 = (bf16[32,1024]{1,0:T(8,128)(2,1)S(1)}, bf16[32,1024]{1,0:T(8,128)(2,1)S(1)}, u32[]{:S(2)}, u32[]{:S(2)}) collective-permute-start(bf16[32,1024]{1,0:T(8,128)(2,1)S(1)} %convolution_convert_fusion.2), channel_id=1, source_target_pairs={{128,192},{129,193},{130,194},{131,195},{132,196},{133,197},{134,1... | collective-permute-start | bytes 196616 | tf_op jit(solution)/shard_map/ppermute | solution.py:127
  137.9 4.6 %collective-permute-start.22 = (bf16[32,1024]{1,0:T(8,128)(2,1)S(1)}, bf16[32,1024]{1,0:T(8,128)(2,1)S(1)}, u32[]{:S(2)}, u32[]{:S(2)}) collective-permute-start(bf16[32,1024]{1,0:T(8,128)(2,1)S(1)} %convolution_convert_fusion.5), channel_id=1, source_target_pairs={{160,192},{161,193},{162,194},{163,195},{164,196},{165,197},{166,1... | collective-permute-start | bytes 196616 | tf_op jit(solution)/shard_map/ppermute | solution.py:127
  139.3 5.4 %collective-permute-start.19 = (bf16[32,1024]{1,0:T(8,128)(2,1)S(1)}, bf16[32,1024]{1,0:T(8,128)(2,1)S(1)}, u32[]{:S(2)}, u32[]{:S(2)}) collective-permute-start(bf16[32,1024]{1,0:T(8,128)(2,1)S(1)} %get-tuple-element.76), channel_id=1, source_target_pairs={{0,224},{1,225},{2,226},{3,227},{4,228},{5,229},{6,230},{7,231},{8... | collective-permute-start | bytes 196616 | tf_op jit(solution)/shard_map/ppermute | solution.py:127
  141.2 3.5 %collective-permute-start.12 = (bf16[32,1024]{1,0:T(8,128)(2,1)S(1)}, bf16[32,1024]{1,0:T(8,128)(2,1)S(1)}, u32[]{:S(2)}, u32[]{:S(2)}) collective-permute-start(bf16[32,1024]{1,0:T(8,128)(2,1)S(1)} %convolution_convert_fusion.8), channel_id=1, source_target_pairs={{128,224},{129,225},{130,226},{131,227},{132,228},{133,229},{134,2... | collective-permute-start | bytes 196616 | tf_op jit(solution)/shard_map/ppermute | solution.py:127
  141.8 2.9 %collective-permute-start.18 = (bf16[32,1024]{1,0:T(8,128)(2,1)S(1)}, bf16[32,1024]{1,0:T(8,128)(2,1)S(1)}, u32[]{:S(2)}, u32[]{:S(2)}) collective-permute-start(bf16[32,1024]{1,0:T(8,128)(2,1)S(1)} %convolution_convert_fusion.4), channel_id=1, source_target_pairs={{160,224},{161,225},{162,226},{163,227},{164,228},{165,229},{166,2... | collective-permute-start | bytes 196616 | tf_op jit(solution)/shard_map/ppermute | solution.py:127
  144.0 0.7 collective-permute-start.23
  146.6 19.9 %all-to-all-start.1 = ((bf16[16,32,1024]{2,1,0:T(8,128)(2,1)}), bf16[16,32,1024]{2,1,0:T(8,128)(2,1)S(1)}, u32[]{:S(2)}, u32[]{:S(2)}) async-start(bf16[16,32,1024]{2,1,0:T(8,128)(2,1)} %broadcast_in_dim.95), calls=%async_computation.1 | async-start | bytes 2097152 | tf_op jit(solution)/shard_map/all_to_all | solution.py:151
  169.4 7.3 %copy-start.1 = (bf16[512,1024]{1,0:T(8,128)(2,1)}, bf16[512,1024]{1,0:T(8,128)(2,1)S(1)}, u32[]{:S(2)}) copy-start(bf16[512,1024]{1,0:T(8,128)(2,1)S(1)} %convolution_convert_fusion) | copy-start | bytes 3145732
  170.4 19.1 %collective-permute-start.31 = (bf16[64,1024]{1,0:T(8,128)(2,1)}, bf16[64,1024]{1,0:T(8,128)(2,1)}, u32[]{:S(2)}, u32[]{:S(2)}) collective-permute-start(bf16[64,1024]{1,0:T(8,128)(2,1)} %get-tuple-element.66), channel_id=1, source_target_pairs={{0,128},{32,160},{64,192},{96,224},{128,0},{160,32},{192,64},{224,... | collective-permute-start | bytes 393224 | tf_op jit(solution)/shard_map/ppermute | solution.py:163
  175.7 15.8 %collective-permute-start.30 = (bf16[64,1024]{1,0:T(8,128)(2,1)}, bf16[64,1024]{1,0:T(8,128)(2,1)}, u32[]{:S(2)}, u32[]{:S(2)}) collective-permute-start(bf16[64,1024]{1,0:T(8,128)(2,1)} %get-tuple-element.67), channel_id=1, source_target_pairs={{0,160},{32,192},{64,224},{96,0},{128,32},{160,64},{192,96},{224,1... | collective-permute-start | bytes 393224 | tf_op jit(solution)/shard_map/ppermute | solution.py:163
  176.9 12.0 %collective-permute-start.24 = (bf16[8,64,32]{1,0,2:T(8,128)(2,1)S(1)}, bf16[8,64,32]{1,0,2:T(8,128)(2,1)S(1)}, u32[]{:S(2)}, u32[]{:S(2)}) collective-permute-start(bf16[8,64,32]{1,0,2:T(8,128)(2,1)S(1)} %copy.29), channel_id=1, source_target_pairs={{0,1},{1,0},{2,3},{3,2},{4,5},{5,4},{6,7},{7,6},{8,9},{9,8},{10,11... | collective-permute-start | bytes 98312 | tf_op jit(solution)/shard_map/ppermute | solution.py:107
  181.6 14.5 %collective-permute-start.29 = (bf16[64,1024]{1,0:T(8,128)(2,1)}, bf16[64,1024]{1,0:T(8,128)(2,1)S(1)}, u32[]{:S(2)}, u32[]{:S(2)}) collective-permute-start(bf16[64,1024]{1,0:T(8,128)(2,1)} %get-tuple-element.68), channel_id=1, source_target_pairs={{0,96},{32,128},{64,160},{96,192},{128,224},{160,0},{192,32},{224,... | collective-permute-start | bytes 393224 | tf_op jit(solution)/shard_map/ppermute | solution.py:163
  186.2 11.1 %collective-permute-start.28 = (bf16[64,1024]{1,0:T(8,128)(2,1)}, bf16[64,1024]{1,0:T(8,128)(2,1)S(1)}, u32[]{:S(2)}, u32[]{:S(2)}) collective-permute-start(bf16[64,1024]{1,0:T(8,128)(2,1)} %get-tuple-element.69), channel_id=1, source_target_pairs={{0,192},{32,224},{64,0},{96,32},{128,64},{160,96},{192,128},{224,1... | collective-permute-start | bytes 393224 | tf_op jit(solution)/shard_map/ppermute | solution.py:163
  188.9 14.7 %collective-permute-start.27 = (bf16[64,1024]{1,0:T(8,128)(2,1)}, bf16[64,1024]{1,0:T(8,128)(2,1)S(1)}, u32[]{:S(2)}, u32[]{:S(2)}) collective-permute-start(bf16[64,1024]{1,0:T(8,128)(2,1)} %get-tuple-element.70), channel_id=1, source_target_pairs={{0,64},{32,96},{64,128},{96,160},{128,192},{160,224},{192,0},{224,... | collective-permute-start | bytes 393224 | tf_op jit(solution)/shard_map/ppermute | solution.py:163
  189.5 14.0 %collective-permute-start.26 = (bf16[64,1024]{1,0:T(8,128)(2,1)}, bf16[64,1024]{1,0:T(8,128)(2,1)S(1)}, u32[]{:S(2)}, u32[]{:S(2)}) collective-permute-start(bf16[64,1024]{1,0:T(8,128)(2,1)} %get-tuple-element.71), channel_id=1, source_target_pairs={{0,224},{32,0},{64,32},{96,64},{128,96},{160,128},{192,160},{224,1... | collective-permute-start | bytes 393224 | tf_op jit(solution)/shard_map/ppermute | solution.py:163
  191.5 14.4 %collective-permute-start.25 = (bf16[64,1024]{1,0:T(8,128)(2,1)S(1)}, bf16[64,1024]{1,0:T(8,128)(2,1)}, u32[]{:S(2)}, u32[]{:S(2)}) collective-permute-start(bf16[64,1024]{1,0:T(8,128)(2,1)S(1)} %get-tuple-element.65), channel_id=1, source_target_pairs={{0,32},{32,64},{64,96},{96,128},{128,160},{160,192},{192,224},{224... | collective-permute-start | bytes 393224 | tf_op jit(solution)/shard_map/ppermute | solution.py:163
  207.2 2.0 collective-permute-start.32
Sparse Core Ops, SparseCore 0:
  10.6 82.1 all-gather.1

commit v5 on v4

--- a/solution.py
+++ b/solution.py
@@ -81,6 +81,50 @@
     )(jnp.stack([z, turn.astype(jnp.int32)]), solved, whole, kept)
 
 
+def next_body(place_ref, solved_ref, whole_ref, *refs):
+    *outs, weights, loaded = refs
+    z, panels = place_ref[0], whole_ref.shape[0]
+
+    def load(i):
+        return pltpu.make_async_copy(whole_ref.at[z + 2 + i], weights.at[i], loaded.at[i])
+
+    @pl.when(place_ref[1] == 1)
+    def _():
+        for i in range(len(outs)):
+
+            @pl.when(z + 2 + i < panels)
+            def _():
+                load(i).start()
+
+        for i in range(len(outs)):
+
+            @pl.when(z + 2 + i < panels)
+            def _():
+                load(i).wait()
+                outs[i][...] = times(solved_ref[...], weights[i]).astype(BF16)
+
+
+def next_products(z, turn, solved, whole):
+    share, width = solved.shape
+    one = pl.BlockSpec((share, width), lambda i, p: (0, 0))
+    return pl.pallas_call(
+        next_body,
+        grid_spec=pltpu.PrefetchScalarGridSpec(
+            num_scalar_prefetch=1,
+            grid=(1,),
+            in_specs=[one, pl.BlockSpec(memory_space=pl.ANY)],
+            out_specs=[one, one],
+            scratch_shapes=[
+                pltpu.VMEM((2, width, width), BF16),
+                pltpu.SemaphoreType.DMA((2,)),
+            ],
+        ),
+        out_shape=[jax.ShapeDtypeStruct((share, width), BF16)] * 2,
+        compiler_params=pltpu.CompilerParams(vmem_limit_bytes=48 * 2**20),
+        name="next_products",
+    )(jnp.stack([z, turn.astype(jnp.int32)]), solved, whole)
+
+
 def per_device(rhs_diag, rhs_tall, diag_inverse, coupling, tall_blocks, sparsity):
     z = lax.axis_index("panel")
     rows_index = lax.axis_index(ROWS)
@@ -117,7 +161,7 @@
         index = jnp.minimum(z + distance, panels - 1)
         return lax.dynamic_index_in_dim(whole, index, 0, keepdims=False)
 
-    following, second, third = lax.optimization_barrier((ahead(1), ahead(2), ahead(3)))
+    following = lax.optimization_barrier(ahead(1))
 
     solved = jnp.zeros((share, width), BF16)
     kept = jnp.zeros((panels - 4, share, width), BF16)
@@ -140,9 +184,10 @@
         near, fresh = lax.optimization_barrier((near, fresh))
         send(near, [k], 1)
         if k < panels - 2:
-            send(times(fresh, second).astype(BF16), [k], 2)
+            after = next_products(z, z == k, fresh, whole)
+            send(after[0], [k], 2)
         if k < panels - 3:
-            send(times(fresh, third).astype(BF16), [k], 3)
+            send(after[1], [k], 3)
         if 0 < k < panels - 3:
             kept = later_products(z, z == k - 1, previous, whole, kept)
         previous = fresh

time: 218 us -> 216 us (level)
  matrix products: 21.7 us -> 13.7 us
  Pallas kernels: 7.48 us -> 14.6 us
    dot_general x27 -> x16, matrix products: 21.7 us -> 13.7 us  [times(): lax.dot_general(left, weight, (((1,), (1,)), ((), ())), preferred_element...]
    pallas_call x0 -> x6, Pallas kernels: none -> 7.08 us  [next_products(): pl.pallas_call(next_body, grid_spec=pltpu.PrefetchScalarGridSpec(num_scal...]
  transfers between devices with their start and end apart: 36 -> 36, of which waited for: 9 -> 8; matrix products, arithmetic and copies ran while one was open for 13% -> 10% of each run, Pallas kernels for 3% -> 7%
where the time goes in v5:
time: 216 us; the launch traced here: 215 us
  waiting for transfers between devices  96.2 us (45%)
  starting transfers between devices  57.5 us (27%)
  between operations  14.8 us (7%)
  Pallas kernels  14.6 us (7%)
  matrix products  13.7 us (6%)
  local copies, waits for them, and re-layouts  9.36 us (4%)
  other arithmetic  8.87 us (4%)
    all_gather x1, waiting for transfers between devices, per_device(): whole = lax.all_gather(coupling[0], ROWS).reshape(panels, width, width)  55.9 us
    ppermute x23, starting transfers between devices, send(): moved = lax.ppermute(value, 'panel', [(s, s + distance) for s in senders])  23 us
    ppermute x7, starting transfers between devices, per_device(): moved = lax.ppermute(part(lax.rem(z + distance, panels)), 'panel', route)  15.4 us
    all_to_all x1, waiting for transfers between devices, per_device(): lax.all_to_all(jnp.broadcast_to(solved[None], (chips, share, width)), 'ch...  14.9 us
    dot_general x16, matrix products, times(): lax.dot_general(left, weight, (((1,), (1,)), ((), ())), preferred_element...  13.7 us
    ppermute x7, waiting for transfers between devices, per_device(): moved = lax.ppermute(part(lax.rem(z + distance, panels)), 'panel', route)  12.9 us
    all_to_all x1, waiting for transfers between devices, per_device(): pieces = lax.all_to_all(pieces, ROWS, 0, 0, tiled=True)  11.5 us
    ppermute x3, starting transfers between devices, swap(): return lax.ppermute(value, 'core', [(0, 1), (1, 0)])  8.83 us
  transfers between devices with their start and end apart: 36, of which 8 were waited for; matrix products, arithmetic and copies ran while one was open for 10% of the time, Pallas kernels for 7%

profile of v5, /device:TPU:1, one launch (start us, length us, event | category | flops | bytes accessed | tf_op | source)
XLA Modules:
  0.0 215.0 jit_solution(2581163801952046422)
XLA Ops:
  7.2 0.7 all-gather.2.cloned.1.call-update
  8.6 2.3 %bitcast_multiply_fusion = bf16[512,1024]{1,0:T(8,128)(2,1)} fusion(bf16[1,4,128,1024]{3,2,1,0:T(8,128)(2,1)} %param.10, bf16[512]{0:T(512)(128)(2,1)S(1)} %broadcast_bitcast_fusion), kind=kLoop, calls=%fused_computation.35 | loop fusion | flops 524288 | bytes 2098176 | tf_op jit(solution)/shard_map/mul | solution.py:153
  11.0 3.2 %collective-permute-start = (bf16[512,1024]{1,0:T(8,128)(2,1)}, bf16[512,1024]{1,0:T(8,128)(2,1)S(1)}, u32[]{:S(2)}, u32[]{:S(2)}) collective-permute-start(bf16[512,1024]{1,0:T(8,128)(2,1)} %bitcast_multiply_fusion), channel_id=1, source_target_pairs={{0,1},{1,0},{2,3},{3,2},{4,5},{5,4},{6,7},{7,6},{8,9},{9,8},{10,11... | collective-permute-start | bytes 3145736 | tf_op jit(solution)/shard_map/ppermute | solution.py:151
  14.2 2.0 copy.22
  16.3 5.5 %all-to-all-start = ((bf16[32,32,256]{2,1,0:T(8,128)(2,1)}), bf16[32,32,256]{2,1,0:T(8,128)(2,1)}, u32[]{:S(2)}, u32[]{:S(2)}) async-start(bf16[32,32,256]{2,1,0:T(8,128)(2,1)} %bitcast.2), calls=%async_computation | async-start | bytes 1048576 | tf_op jit(solution)/shard_map/all_to_all | solution.py:146
  21.9 11.5 %all-to-all-done = bf16[32,32,256]{2,1,0:T(8,128)(2,1)} async-done(((bf16[32,32,256]{2,1,0:T(8,128)(2,1)}), bf16[32,32,256]{2,1,0:T(8,128)(2,1)}, u32[]{:S(2)}, u32[]{:S(2)}) %all-to-all-start) | async-done | bytes 524320 | tf_op jit(solution)/shard_map/all_to_all | solution.py:146
  33.4 0.9 convert_bitcast_fusion.1
  34.3 2.8 %pad_maximum_fusion = bf16[1024,1024]{1,0:T(8,128)(2,1)} fusion(bf16[512,1024]{1,0:T(8,128)(2,1)S(1)} %collective-permute-done, bf16[512,1024]{1,0:T(8,128)(2,1)} %bitcast_multiply_fusion), kind=kLoop, calls=%fused_computation | loop fusion | flops 4194304 | bytes 4194304 | tf_op jit(solution)/shard_map/concatenate | solution.py:156
  37.1 0.7 fusion.16.solved_ref
  37.8 55.9 %all-gather.2.cloned.1.call-done = bf16[32,256,1024]{2,1,0:T(8,128)(2,1)} async-done(((bf16[1,256,1024]{2,1,0:T(8,128)(2,1)}), bf16[32,256,1024]{2,1,0:T(8,128)(2,1)}) %all-gather.2.cloned.1.call-update) | async-done | bytes 16777232 | tf_op jit(solution)/shard_map/all_gather | solution.py:142
  93.6 1.8 dynamic-slice_bitcast_fusion
  95.4 0.7 convolution_convert_fusion.7
  96.1 3.2 %collective-permute-start.2 = (bf16[32,1024]{1,0:T(8,128)(2,1)S(1)}, bf16[32,1024]{1,0:T(8,128)(2,1)S(1)}, u32[]{:S(2)}, u32[]{:S(2)}) collective-permute-start(bf16[32,1024]{1,0:T(8,128)(2,1)S(1)} %convolution_convert_fusion.7), channel_id=1, source_target_pairs={{0,32},{1,33},{2,34},{3,35},{4,36},{5,37},{6,38},{7,39},{8,40},{9,... | collective-permute-start | bytes 196616 | tf_op jit(solution)/shard_map/ppermute | solution.py:171
  99.4 3.6 %next_products.6 = (bf16[32,1024]{1,0:T(8,128)(2,1)S(1)}, bf16[32,1024]{1,0:T(8,128)(2,1)S(1)}) custom-call(s32[2]{0:T(128)S(1)} %get-tuple-element.93.place_ref, bf16[32,1024]{1,0:T(8,128)(2,1)S(1)} %fusion.16.solved_ref, bf16[8,1024,1024]{2,1,0:T(8,128)(2,1)} %bitcast.130), custom_call_target="tpu_custom_call" | custom-call | tf_op jit(solution)/shard_map/next_products/pallas_call | solution.py:110
  103.0 1.3 collective-permute-start.4
  104.3 0.7 fusion.19.solved_ref
  105.0 0.7 convolution_convert_fusion.6
  105.8 0.7 collective-permute-start.5
  106.5 1.3 collective-permute-start.1
  108.4 0.7 collective-permute-start.3
  109.1 0.7 collective-permute-start.8
  109.8 5.4 %later_products.4.kept_ref = bf16[4,32,1024]{2,1,0:T(8,128)(2,1)S(1)} custom-call(s32[2]{0:T(128)S(1)} %get-tuple-element.93.place_ref, bf16[32,1024]{1,0:T(8,128)(2,1)S(1)} %fusion.16.solved_ref, bf16[8,1024,1024]{2,1,0:T(8,128)(2,1)} %bitcast.132, bf16[4,32,1024]{2,1,0:T(8,128)(2,1)S(1)} %broadcast_in_dim.93.kept_ref), custom_call_target="tpu_custom_call", output_to_operand_aliasing={{}: (3, {})} | custom-call | flops 268435456 | bytes 8388608 | tf_op jit(solution)/shard_map/later_products/pallas_call | solution.py:54
  115.2 0.7 fusion.22.solved_ref
  115.9 0.7 convolution_convert_fusion.5
  116.7 0.7 collective-permute-start.6
  118.0 1.3 collective-permute-start.10
  119.9 0.7 collective-permute-start.9
  120.6 0.7 collective-permute-start.15
  121.2 0.7 fusion.25.solved_ref
  122.6 0.7 convolution_convert_fusion.4
  123.3 0.7 collective-permute-start.11
  124.6 1.3 collective-permute-start.7
  125.9 0.7 collective-permute-start.16
  127.3 0.7 fusion.28.solved_ref
  128.0 0.8 later_products.7
  128.8 0.7 convolution_convert_fusion.3
  129.5 0.7 collective-permute-start.17
  130.8 1.3 collective-permute-start.14
  133.5 0.7 fusion.31.solved_ref
  134.2 0.7 convolution_convert_fusion.2
  135.0 0.7 collective-permute-start.22
  135.6 1.2 next_products.11
  136.9 2.6 %collective-permute-start.19 = (bf16[32,1024]{1,0:T(8,128)(2,1)S(1)}, bf16[32,1024]{1,0:T(8,128)(2,1)S(1)}, u32[]{:S(2)}, u32[]{:S(2)}) collective-permute-start(bf16[32,1024]{1,0:T(8,128)(2,1)S(1)} %get-tuple-element.89), channel_id=1, source_target_pairs={{0,224},{1,225},{2,226},{3,227},{4,228},{5,229},{6,230},{7,231},{8... | collective-permute-start | bytes 196616 | tf_op jit(solution)/shard_map/ppermute | solution.py:171
  140.9 0.7 fusion.34
  141.6 0.7 convolution_convert_fusion.1
  142.4 0.7 collective-permute-start.23
  143.1 0.7 fusion.40
  143.8 1.1 broadcast_in_dim.95
  145.0 4.8 %all-to-all-start.1 = ((bf16[16,32,1024]{2,1,0:T(8,128)(2,1)}), bf16[16,32,1024]{2,1,0:T(8,128)(2,1)S(1)}, u32[]{:S(2)}, u32[]{:S(2)}) async-start(bf16[16,32,1024]{2,1,0:T(8,128)(2,1)} %broadcast_in_dim.95), calls=%async_computation.1 | async-start | bytes 2097152 | tf_op jit(solution)/shard_map/all_to_all | solution.py:196
  149.8 14.9 %all-to-all-done.1 = bf16[16,32,1024]{2,1,0:T(8,128)(2,1)S(1)} async-done(((bf16[16,32,1024]{2,1,0:T(8,128)(2,1)}), bf16[16,32,1024]{2,1,0:T(8,128)(2,1)S(1)}, u32[]{:S(2)}, u32[]{:S(2)}) %all-to-all-start.1) | async-done | bytes 1048608 | tf_op jit(solution)/shard_map/all_to_all | solution.py:196
  164.7 2.9 %convolution_convert_fusion = bf16[512,1024]{1,0:T(8,128)(2,1)S(1)} fusion(bf16[512,1024]{1,0:T(8,128)(2,1)S(1)} %bitcast.148, bf16[1024,1024]{1,0:T(8,128)(2,1)} %pad_maximum_fusion), kind=kOutput, calls=%fused_computation.18 | convolution fusion | flops 1074266112 | bytes 4194304 | tf_op jit(solution)/shard_map/dot_general | solution.py:21
  167.6 1.0 dynamic-slice_bitcast_fusion.7
  168.6 5.1 %collective-permute-start.31 = (bf16[64,1024]{1,0:T(8,128)(2,1)}, bf16[64,1024]{1,0:T(8,128)(2,1)}, u32[]{:S(2)}, u32[]{:S(2)}) collective-permute-start(bf16[64,1024]{1,0:T(8,128)(2,1)} %get-tuple-element.79), channel_id=1, source_target_pairs={{0,128},{32,160},{64,192},{96,224},{128,0},{160,32},{192,64},{224,... | collective-permute-start | bytes 393224 | tf_op jit(solution)/shard_map/ppermute | solution.py:208
  174.0 5.0 %collective-permute-start.24 = (bf16[8,64,32]{1,0,2:T(8,128)(2,1)S(1)}, bf16[8,64,32]{1,0,2:T(8,128)(2,1)S(1)}, u32[]{:S(2)}, u32[]{:S(2)}) collective-permute-start(bf16[8,64,32]{1,0,2:T(8,128)(2,1)S(1)} %copy.29), channel_id=1, source_target_pairs={{0,1},{1,0},{2,3},{3,2},{4,5},{5,4},{6,7},{7,6},{8,9},{9,8},{10,11... | collective-permute-start | bytes 98312 | tf_op jit(solution)/shard_map/ppermute | solution.py:151
  179.0 5.1 %collective-permute-start.29 = (bf16[64,1024]{1,0:T(8,128)(2,1)}, bf16[64,1024]{1,0:T(8,128)(2,1)S(1)}, u32[]{:S(2)}, u32[]{:S(2)}) collective-permute-start(bf16[64,1024]{1,0:T(8,128)(2,1)} %get-tuple-element.81), channel_id=1, source_target_pairs={{0,96},{32,128},{64,160},{96,192},{128,224},{160,0},{192,32},{224,... | collective-permute-start | bytes 393224 | tf_op jit(solution)/shard_map/ppermute | solution.py:208
  184.1 2.7 %collective-permute-start.28 = (bf16[64,1024]{1,0:T(8,128)(2,1)}, bf16[64,1024]{1,0:T(8,128)(2,1)S(1)}, u32[]{:S(2)}, u32[]{:S(2)}) collective-permute-start(bf16[64,1024]{1,0:T(8,128)(2,1)} %get-tuple-element.82), channel_id=1, source_target_pairs={{0,192},{32,224},{64,0},{96,32},{128,64},{160,96},{192,128},{224,1... | collective-permute-start | bytes 393224 | tf_op jit(solution)/shard_map/ppermute | solution.py:208
  187.2 2.0 collective-permute-start.26
  189.4 1.0 copy.27
  191.5 2.0 collective-permute-done.29
  193.6 7.8 %collective-permute-done.27 = bf16[64,1024]{1,0:T(8,128)(2,1)S(1)} collective-permute-done((bf16[64,1024]{1,0:T(8,128)(2,1)}, bf16[64,1024]{1,0:T(8,128)(2,1)S(1)}, u32[]{:S(2)}, u32[]{:S(2)}) %collective-permute-start.27) | collective-permute-done | bytes 131104 | tf_op jit(solution)/shard_map/ppermute | solution.py:208
  201.5 2.9 %collective-permute-done.25 = bf16[64,1024]{1,0:T(8,128)(2,1)} collective-permute-done((bf16[64,1024]{1,0:T(8,128)(2,1)S(1)}, bf16[64,1024]{1,0:T(8,128)(2,1)}, u32[]{:S(2)}, u32[]{:S(2)}) %collective-permute-start.25) | collective-permute-done | bytes 131104 | tf_op jit(solution)/shard_map/ppermute | solution.py:208
  204.4 1.3 fusion.48
  206.3 0.7 convert_bitcast_fusion
  207.4 0.8 copy.28
  (74 shorter events, 11.1 us)
Async XLA Ops:
  7.2 29.9 %copy-start = (bf16[1,1024,1024]{2,1,0:T(8,128)(2,1)S(1)}, bf16[1,1024,1024]{2,1,0:T(8,128)(2,1)}, u32[]{:S(2)}) copy-start(bf16[1,1024,1024]{2,1,0:T(8,128)(2,1)} %param.8) | copy-start | bytes 6291460
  7.2 86.4 %all-gather.2.cloned.1.call-start = ((), (), s32[]{:S(2)}) async-start(), calls=%async_computation.2 | async-start | bytes 17301504 | tf_op jit(solution)/shard_map/all_gather | solution.py:142
  11.0 23.3 %collective-permute-start = (bf16[512,1024]{1,0:T(8,128)(2,1)}, bf16[512,1024]{1,0:T(8,128)(2,1)S(1)}, u32[]{:S(2)}, u32[]{:S(2)}) collective-permute-start(bf16[512,1024]{1,0:T(8,128)(2,1)} %bitcast_multiply_fusion), channel_id=1, source_target_pairs={{0,1},{1,0},{2,3},{3,2},{4,5},{5,4},{6,7},{7,6},{8,9},{9,8},{10,11... | collective-permute-start | bytes 3145736 | tf_op jit(solution)/shard_map/ppermute | solution.py:151
  16.3 17.1 %all-to-all-start = ((bf16[32,32,256]{2,1,0:T(8,128)(2,1)}), bf16[32,32,256]{2,1,0:T(8,128)(2,1)}, u32[]{:S(2)}, u32[]{:S(2)}) async-start(bf16[32,32,256]{2,1,0:T(8,128)(2,1)} %bitcast.2), calls=%async_computation | async-start | bytes 1048576 | tf_op jit(solution)/shard_map/all_to_all | solution.py:146
  96.1 8.2 %collective-permute-start.2 = (bf16[32,1024]{1,0:T(8,128)(2,1)S(1)}, bf16[32,1024]{1,0:T(8,128)(2,1)S(1)}, u32[]{:S(2)}, u32[]{:S(2)}) collective-permute-start(bf16[32,1024]{1,0:T(8,128)(2,1)S(1)} %convolution_convert_fusion.7), channel_id=1, source_target_pairs={{0,32},{1,33},{2,34},{3,35},{4,36},{5,37},{6,38},{7,39},{8,40},{9,... | collective-permute-start | bytes 196616 | tf_op jit(solution)/shard_map/ppermute | solution.py:171
  103.0 12.2 %collective-permute-start.4 = (bf16[32,1024]{1,0:T(8,128)(2,1)S(1)}, bf16[32,1024]{1,0:T(8,128)(2,1)S(1)}, u32[]{:S(2)}, u32[]{:S(2)}) collective-permute-start(bf16[32,1024]{1,0:T(8,128)(2,1)S(1)} %get-tuple-element.45), channel_id=1, source_target_pairs={{0,64},{1,65},{2,66},{3,67},{4,68},{5,69},{6,70},{7,71},{8,72},{9,... | collective-permute-start | bytes 196616 | tf_op jit(solution)/shard_map/ppermute | solution.py:171
  105.8 9.5 %collective-permute-start.5 = (bf16[32,1024]{1,0:T(8,128)(2,1)S(1)}, bf16[32,1024]{1,0:T(8,128)(2,1)S(1)}, u32[]{:S(2)}, u32[]{:S(2)}) collective-permute-start(bf16[32,1024]{1,0:T(8,128)(2,1)S(1)} %convolution_convert_fusion.6), channel_id=1, source_target_pairs={{32,64},{33,65},{34,66},{35,67},{36,68},{37,69},{38,70},{39,71},{4... | collective-permute-start | bytes 196616 | tf_op jit(solution)/shard_map/ppermute | solution.py:171
  106.5 13.4 %collective-permute-start.1 = (bf16[32,1024]{1,0:T(8,128)(2,1)S(1)}, bf16[32,1024]{1,0:T(8,128)(2,1)S(1)}, u32[]{:S(2)}, u32[]{:S(2)}) collective-permute-start(bf16[32,1024]{1,0:T(8,128)(2,1)S(1)} %get-tuple-element.40), channel_id=1, source_target_pairs={{0,96},{1,97},{2,98},{3,99},{4,100},{5,101},{6,102},{7,103},{8,104... | collective-permute-start | bytes 196616 | tf_op jit(solution)/shard_map/ppermute | solution.py:171
  108.4 12.2 %collective-permute-start.3 = (bf16[32,1024]{1,0:T(8,128)(2,1)S(1)}, bf16[32,1024]{1,0:T(8,128)(2,1)S(1)}, u32[]{:S(2)}, u32[]{:S(2)}) collective-permute-start(bf16[32,1024]{1,0:T(8,128)(2,1)S(1)} %get-tuple-element.44), channel_id=1, source_target_pairs={{32,96},{33,97},{34,98},{35,99},{36,100},{37,101},{38,102},{39,103... | collective-permute-start | bytes 196616 | tf_op jit(solution)/shard_map/ppermute | solution.py:171
  109.1 15.5 %collective-permute-start.8 = (bf16[32,1024]{1,0:T(8,128)(2,1)S(1)}, bf16[32,1024]{1,0:T(8,128)(2,1)S(1)}, u32[]{:S(2)}, u32[]{:S(2)}) collective-permute-start(bf16[32,1024]{1,0:T(8,128)(2,1)S(1)} %get-tuple-element.53), channel_id=1, source_target_pairs={{32,128},{33,129},{34,130},{35,131},{36,132},{37,133},{38,134},{39... | collective-permute-start | bytes 196616 | tf_op jit(solution)/shard_map/ppermute | solution.py:171
  116.7 4.6 %collective-permute-start.6 = (bf16[32,1024]{1,0:T(8,128)(2,1)S(1)}, bf16[32,1024]{1,0:T(8,128)(2,1)S(1)}, u32[]{:S(2)}, u32[]{:S(2)}) collective-permute-start(bf16[32,1024]{1,0:T(8,128)(2,1)S(1)} %convolution_convert_fusion.5), channel_id=1, source_target_pairs={{64,96},{65,97},{66,98},{67,99},{68,100},{69,101},{70,102},{71,103... | collective-permute-start | bytes 196616 | tf_op jit(solution)/shard_map/ppermute | solution.py:171
  118.0 7.9 %collective-permute-start.10 = (bf16[32,1024]{1,0:T(8,128)(2,1)S(1)}, bf16[32,1024]{1,0:T(8,128)(2,1)S(1)}, u32[]{:S(2)}, u32[]{:S(2)}) collective-permute-start(bf16[32,1024]{1,0:T(8,128)(2,1)S(1)} %slice_bitcast_fusion.3), channel_id=1, source_target_pairs={{0,128},{32,160},{1,129},{33,161},{2,130},{34,162},{3,131},{35,163... | collective-permute-start | bytes 196616 | tf_op jit(solution)/shard_map/ppermute | solution.py:171
  119.9 6.7 %collective-permute-start.9 = (bf16[32,1024]{1,0:T(8,128)(2,1)S(1)}, bf16[32,1024]{1,0:T(8,128)(2,1)S(1)}, u32[]{:S(2)}, u32[]{:S(2)}) collective-permute-start(bf16[32,1024]{1,0:T(8,128)(2,1)S(1)} %get-tuple-element.54), channel_id=1, source_target_pairs={{64,128},{65,129},{66,130},{67,131},{68,132},{69,133},{70,134},{71... | collective-permute-start | bytes 196616 | tf_op jit(solution)/shard_map/ppermute | solution.py:171
  120.6 10.3 %collective-permute-start.15 = (bf16[32,1024]{1,0:T(8,128)(2,1)S(1)}, bf16[32,1024]{1,0:T(8,128)(2,1)S(1)}, u32[]{:S(2)}, u32[]{:S(2)}) collective-permute-start(bf16[32,1024]{1,0:T(8,128)(2,1)S(1)} %get-tuple-element.62), channel_id=1, source_target_pairs={{64,160},{65,161},{66,162},{67,163},{68,164},{69,165},{70,166},{71... | collective-permute-start | bytes 196616 | tf_op jit(solution)/shard_map/ppermute | solution.py:171
  123.3 4.0 %collective-permute-start.11 = (bf16[32,1024]{1,0:T(8,128)(2,1)S(1)}, bf16[32,1024]{1,0:T(8,128)(2,1)S(1)}, u32[]{:S(2)}, u32[]{:S(2)}) collective-permute-start(bf16[32,1024]{1,0:T(8,128)(2,1)S(1)} %convolution_convert_fusion.4), channel_id=1, source_target_pairs={{96,128},{97,129},{98,130},{99,131},{100,132},{101,133},{102,134},... | collective-permute-start | bytes 196616 | tf_op jit(solution)/shard_map/ppermute | solution.py:171
  124.6 7.5 %collective-permute-start.7 = (bf16[32,1024]{1,0:T(8,128)(2,1)S(1)}, bf16[32,1024]{1,0:T(8,128)(2,1)S(1)}, u32[]{:S(2)}, u32[]{:S(2)}) collective-permute-start(bf16[32,1024]{1,0:T(8,128)(2,1)S(1)} %slice_bitcast_fusion.4), channel_id=1, source_target_pairs={{0,160},{32,192},{64,224},{1,161},{33,193},{65,225},{2,162},{34,19... | collective-permute-start | bytes 196616 | tf_op jit(solution)/shard_map/ppermute | solution.py:171
  125.9 6.9 %collective-permute-start.16 = (bf16[32,1024]{1,0:T(8,128)(2,1)S(1)}, bf16[32,1024]{1,0:T(8,128)(2,1)S(1)}, u32[]{:S(2)}, u32[]{:S(2)}) collective-permute-start(bf16[32,1024]{1,0:T(8,128)(2,1)S(1)} %get-tuple-element.63), channel_id=1, source_target_pairs={{96,160},{97,161},{98,162},{99,163},{100,164},{101,165},{102,166},... | collective-permute-start | bytes 196616 | tf_op jit(solution)/shard_map/ppermute | solution.py:171
  126.6 10.3 %collective-permute-start.20 = (bf16[32,1024]{1,0:T(8,128)(2,1)S(1)}, bf16[32,1024]{1,0:T(8,128)(2,1)S(1)}, u32[]{:S(2)}, u32[]{:S(2)}) collective-permute-start(bf16[32,1024]{1,0:T(8,128)(2,1)S(1)} %get-tuple-element.68), channel_id=1, source_target_pairs={{96,192},{97,193},{98,194},{99,195},{100,196},{101,197},{102,198},... | collective-permute-start | bytes 196616 | tf_op jit(solution)/shard_map/ppermute | solution.py:171
  129.5 4.0 %collective-permute-start.17 = (bf16[32,1024]{1,0:T(8,128)(2,1)S(1)}, bf16[32,1024]{1,0:T(8,128)(2,1)S(1)}, u32[]{:S(2)}, u32[]{:S(2)}) collective-permute-start(bf16[32,1024]{1,0:T(8,128)(2,1)S(1)} %convolution_convert_fusion.3), channel_id=1, source_target_pairs={{128,160},{129,161},{130,162},{131,163},{132,164},{133,165},{134,1... | collective-permute-start | bytes 196616 | tf_op jit(solution)/shard_map/ppermute | solution.py:171
  130.8 8.7 %collective-permute-start.14 = (bf16[32,1024]{1,0:T(8,128)(2,1)S(1)}, bf16[32,1024]{1,0:T(8,128)(2,1)S(1)}, u32[]{:S(2)}, u32[]{:S(2)}) collective-permute-start(bf16[32,1024]{1,0:T(8,128)(2,1)S(1)} %get-tuple-element.90), channel_id=1, source_target_pairs={{0,192},{32,224},{1,193},{33,225},{2,194},{34,226},{3,195},{35,227... | collective-permute-start | bytes 196616 | tf_op jit(solution)/shard_map/ppermute | solution.py:171
  132.1 8.1 %collective-permute-start.13 = (bf16[32,1024]{1,0:T(8,128)(2,1)S(1)}, bf16[32,1024]{1,0:T(8,128)(2,1)S(1)}, u32[]{:S(2)}, u32[]{:S(2)}) collective-permute-start(bf16[32,1024]{1,0:T(8,128)(2,1)S(1)} %get-tuple-element.91), channel_id=1, source_target_pairs={{64,192},{96,224},{65,193},{97,225},{66,194},{98,226},{67,195},{99... | collective-permute-start | bytes 196616 | tf_op jit(solution)/shard_map/ppermute | solution.py:171
  132.8 8.1 %collective-permute-start.21 = (bf16[32,1024]{1,0:T(8,128)(2,1)S(1)}, bf16[32,1024]{1,0:T(8,128)(2,1)S(1)}, u32[]{:S(2)}, u32[]{:S(2)}) collective-permute-start(bf16[32,1024]{1,0:T(8,128)(2,1)S(1)} %get-tuple-element.69), channel_id=1, source_target_pairs={{128,192},{129,193},{130,194},{131,195},{132,196},{133,197},{134,1... | collective-permute-start | bytes 196616 | tf_op jit(solution)/shard_map/ppermute | solution.py:171
  135.0 5.9 %collective-permute-start.22 = (bf16[32,1024]{1,0:T(8,128)(2,1)S(1)}, bf16[32,1024]{1,0:T(8,128)(2,1)S(1)}, u32[]{:S(2)}, u32[]{:S(2)}) collective-permute-start(bf16[32,1024]{1,0:T(8,128)(2,1)S(1)} %convolution_convert_fusion.2), channel_id=1, source_target_pairs={{160,192},{161,193},{162,194},{163,195},{164,196},{165,197},{166,1... | collective-permute-start | bytes 196616 | tf_op jit(solution)/shard_map/ppermute | solution.py:171
  136.9 6.2 %collective-permute-start.19 = (bf16[32,1024]{1,0:T(8,128)(2,1)S(1)}, bf16[32,1024]{1,0:T(8,128)(2,1)S(1)}, u32[]{:S(2)}, u32[]{:S(2)}) collective-permute-start(bf16[32,1024]{1,0:T(8,128)(2,1)S(1)} %get-tuple-element.89), channel_id=1, source_target_pairs={{0,224},{1,225},{2,226},{3,227},{4,228},{5,229},{6,230},{7,231},{8... | collective-permute-start | bytes 196616 | tf_op jit(solution)/shard_map/ppermute | solution.py:171
  139.5 3.5 %collective-permute-start.12 = (bf16[32,1024]{1,0:T(8,128)(2,1)S(1)}, bf16[32,1024]{1,0:T(8,128)(2,1)S(1)}, u32[]{:S(2)}, u32[]{:S(2)}) collective-permute-start(bf16[32,1024]{1,0:T(8,128)(2,1)S(1)} %get-tuple-element.60), channel_id=1, source_target_pairs={{128,224},{129,225},{130,226},{131,227},{132,228},{133,229},{134,2... | collective-permute-start | bytes 196616 | tf_op jit(solution)/shard_map/ppermute | solution.py:171
  140.2 2.9 %collective-permute-start.18 = (bf16[32,1024]{1,0:T(8,128)(2,1)S(1)}, bf16[32,1024]{1,0:T(8,128)(2,1)S(1)}, u32[]{:S(2)}, u32[]{:S(2)}) collective-permute-start(bf16[32,1024]{1,0:T(8,128)(2,1)S(1)} %get-tuple-element.67), channel_id=1, source_target_pairs={{160,224},{161,225},{162,226},{163,227},{164,228},{165,229},{166,2... | collective-permute-start | bytes 196616 | tf_op jit(solution)/shard_map/ppermute | solution.py:171
  142.4 0.7 collective-permute-start.23
  145.0 19.8 %all-to-all-start.1 = ((bf16[16,32,1024]{2,1,0:T(8,128)(2,1)}), bf16[16,32,1024]{2,1,0:T(8,128)(2,1)S(1)}, u32[]{:S(2)}, u32[]{:S(2)}) async-start(bf16[16,32,1024]{2,1,0:T(8,128)(2,1)} %broadcast_in_dim.95), calls=%async_computation.1 | async-start | bytes 2097152 | tf_op jit(solution)/shard_map/all_to_all | solution.py:196
  167.6 6.3 %copy-start.1 = (bf16[512,1024]{1,0:T(8,128)(2,1)}, bf16[512,1024]{1,0:T(8,128)(2,1)S(1)}, u32[]{:S(2)}) copy-start(bf16[512,1024]{1,0:T(8,128)(2,1)S(1)} %convolution_convert_fusion) | copy-start | bytes 3145732
  168.6 18.6 %collective-permute-start.31 = (bf16[64,1024]{1,0:T(8,128)(2,1)}, bf16[64,1024]{1,0:T(8,128)(2,1)}, u32[]{:S(2)}, u32[]{:S(2)}) collective-permute-start(bf16[64,1024]{1,0:T(8,128)(2,1)} %get-tuple-element.79), channel_id=1, source_target_pairs={{0,128},{32,160},{64,192},{96,224},{128,0},{160,32},{192,64},{224,... | collective-permute-start | bytes 393224 | tf_op jit(solution)/shard_map/ppermute | solution.py:208
  173.7 15.5 %collective-permute-start.30 = (bf16[64,1024]{1,0:T(8,128)(2,1)}, bf16[64,1024]{1,0:T(8,128)(2,1)}, u32[]{:S(2)}, u32[]{:S(2)}) collective-permute-start(bf16[64,1024]{1,0:T(8,128)(2,1)} %get-tuple-element.80), channel_id=1, source_target_pairs={{0,160},{32,192},{64,224},{96,0},{128,32},{160,64},{192,96},{224,1... | collective-permute-start | bytes 393224 | tf_op jit(solution)/shard_map/ppermute | solution.py:208
  174.0 12.8 %collective-permute-start.24 = (bf16[8,64,32]{1,0,2:T(8,128)(2,1)S(1)}, bf16[8,64,32]{1,0,2:T(8,128)(2,1)S(1)}, u32[]{:S(2)}, u32[]{:S(2)}) collective-permute-start(bf16[8,64,32]{1,0,2:T(8,128)(2,1)S(1)} %copy.29), channel_id=1, source_target_pairs={{0,1},{1,0},{2,3},{3,2},{4,5},{5,4},{6,7},{7,6},{8,9},{9,8},{10,11... | collective-permute-start | bytes 98312 | tf_op jit(solution)/shard_map/ppermute | solution.py:151
  179.0 14.5 %collective-permute-start.29 = (bf16[64,1024]{1,0:T(8,128)(2,1)}, bf16[64,1024]{1,0:T(8,128)(2,1)S(1)}, u32[]{:S(2)}, u32[]{:S(2)}) collective-permute-start(bf16[64,1024]{1,0:T(8,128)(2,1)} %get-tuple-element.81), channel_id=1, source_target_pairs={{0,96},{32,128},{64,160},{96,192},{128,224},{160,0},{192,32},{224,... | collective-permute-start | bytes 393224 | tf_op jit(solution)/shard_map/ppermute | solution.py:208
  184.1 9.5 %collective-permute-start.28 = (bf16[64,1024]{1,0:T(8,128)(2,1)}, bf16[64,1024]{1,0:T(8,128)(2,1)S(1)}, u32[]{:S(2)}, u32[]{:S(2)}) collective-permute-start(bf16[64,1024]{1,0:T(8,128)(2,1)} %get-tuple-element.82), channel_id=1, source_target_pairs={{0,192},{32,224},{64,0},{96,32},{128,64},{160,96},{192,128},{224,1... | collective-permute-start | bytes 393224 | tf_op jit(solution)/shard_map/ppermute | solution.py:208
  186.8 14.7 %collective-permute-start.27 = (bf16[64,1024]{1,0:T(8,128)(2,1)}, bf16[64,1024]{1,0:T(8,128)(2,1)S(1)}, u32[]{:S(2)}, u32[]{:S(2)}) collective-permute-start(bf16[64,1024]{1,0:T(8,128)(2,1)} %get-tuple-element.83), channel_id=1, source_target_pairs={{0,64},{32,96},{64,128},{96,160},{128,192},{160,224},{192,0},{224,... | collective-permute-start | bytes 393224 | tf_op jit(solution)/shard_map/ppermute | solution.py:208
  187.2 14.3 %collective-permute-start.26 = (bf16[64,1024]{1,0:T(8,128)(2,1)}, bf16[64,1024]{1,0:T(8,128)(2,1)S(1)}, u32[]{:S(2)}, u32[]{:S(2)}) collective-permute-start(bf16[64,1024]{1,0:T(8,128)(2,1)} %get-tuple-element.84), channel_id=1, source_target_pairs={{0,224},{32,0},{64,32},{96,64},{128,96},{160,128},{192,160},{224,1... | collective-permute-start | bytes 393224 | tf_op jit(solution)/shard_map/ppermute | solution.py:208
  189.2 15.2 %collective-permute-start.25 = (bf16[64,1024]{1,0:T(8,128)(2,1)S(1)}, bf16[64,1024]{1,0:T(8,128)(2,1)}, u32[]{:S(2)}, u32[]{:S(2)}) collective-permute-start(bf16[64,1024]{1,0:T(8,128)(2,1)S(1)} %get-tuple-element.78), channel_id=1, source_target_pairs={{0,32},{32,64},{64,96},{96,128},{128,160},{160,192},{192,224},{224... | collective-permute-start | bytes 393224 | tf_op jit(solution)/shard_map/ppermute | solution.py:208
  205.7 1.6 collective-permute-start.32
Sparse Core Ops, SparseCore 0:
  10.6 83.0 all-gather.1

commit v6 on v4

--- a/solution.py
+++ b/solution.py
@@ -49,36 +49,62 @@
         lax.fori_loop(0, valid, lambda i, _: store(i).wait(), None)
 
 
-def later_products(z, turn, solved, whole, kept):
+def next_body(place_ref, solved_ref, whole_ref, *refs):
+    *outs, weights, loaded = refs
+    z, panels = place_ref[0], whole_ref.shape[0]
+
+    def load(i):
+        return pltpu.make_async_copy(whole_ref.at[z + 2 + i], weights.at[i], loaded.at[i])
+
+    @pl.when(place_ref[2] == 1)
+    def _():
+        for i in range(len(outs)):
+
+            @pl.when(z + 2 + i < panels)
+            def _():
+                load(i).start()
+
+        for i in range(len(outs)):
+
+            @pl.when(z + 2 + i < panels)
+            def _():
+                load(i).wait()
+                outs[i][...] = times(solved_ref[...], weights[i]).astype(BF16)
+
+
+def stage_body(place_ref, fresh_ref, previous_ref, whole_ref, kept_ref, *refs):
+    next_a, next_b, out_ref, weights, products, loaded, stored, near_loaded = refs
+    next_body(place_ref, fresh_ref, whole_ref, next_a, next_b, weights, near_loaded)
+    later_body(
+        place_ref, previous_ref, whole_ref, kept_ref, out_ref, weights, products, loaded, stored
+    )
+
+
+def stage_products(z, stage, fresh, previous, whole, kept):
     count, share, width = kept.shape
+    one = pl.BlockSpec((share, width), lambda i, p: (0, 0))
+    place = jnp.stack([z, z == stage - 1, z == stage]).astype(jnp.int32)
+    part = jax.ShapeDtypeStruct((share, width), BF16)
     return pl.pallas_call(
-        later_body,
+        stage_body,
         grid_spec=pltpu.PrefetchScalarGridSpec(
             num_scalar_prefetch=1,
             grid=(1,),
-            in_specs=[
-                pl.BlockSpec((share, width), lambda i, p: (0, 0)),
-                pl.BlockSpec(memory_space=pl.ANY),
-                pl.BlockSpec(memory_space=pl.ANY),
-            ],
-            out_specs=pl.BlockSpec(memory_space=pl.ANY),
+            in_specs=[one, one] + [pl.BlockSpec(memory_space=pl.ANY)] * 2,
+            out_specs=[one, one, pl.BlockSpec(memory_space=pl.ANY)],
             scratch_shapes=[
                 pltpu.VMEM((count, width, width), BF16),
                 pltpu.VMEM((count, share, width), BF16),
                 pltpu.SemaphoreType.DMA((count,)),
                 pltpu.SemaphoreType.DMA((count,)),
+                pltpu.SemaphoreType.DMA((2,)),
             ],
         ),
-        out_shape=jax.ShapeDtypeStruct(kept.shape, BF16),
-        input_output_aliases={3: 0},
+        out_shape=[part, part, jax.ShapeDtypeStruct(kept.shape, BF16)],
+        input_output_aliases={4: 2},
         compiler_params=pltpu.CompilerParams(vmem_limit_bytes=48 * 2**20),
-        cost_estimate=pl.CostEstimate(
-            flops=2 * count * share * width * width,
-            bytes_accessed=2 * count * width * width,
-            transcendentals=0,
-        ),
-        name="later_products",
-    )(jnp.stack([z, turn.astype(jnp.int32)]), solved, whole, kept)
+        name="stage_products",
+    )(place, fresh, previous, whole, kept)
 
 
 def per_device(rhs_diag, rhs_tall, diag_inverse, coupling, tall_blocks, sparsity):
@@ -117,9 +143,10 @@
         index = jnp.minimum(z + distance, panels - 1)
         return lax.dynamic_index_in_dim(whole, index, 0, keepdims=False)
 
-    following, second, third = lax.optimization_barrier((ahead(1), ahead(2), ahead(3)))
+    following = lax.optimization_barrier(ahead(1))
 
     solved = jnp.zeros((share, width), BF16)
+    previous = jnp.zeros((share, width), BF16)
     kept = jnp.zeros((panels - 4, share, width), BF16)
     arrivals = [[] for _ in range(panels)]
 
@@ -140,11 +167,10 @@
         near, fresh = lax.optimization_barrier((near, fresh))
         send(near, [k], 1)
         if k < panels - 2:
-            send(times(fresh, second).astype(BF16), [k], 2)
+            *after, kept = stage_products(z, k, fresh, previous, whole, kept)
+            send(after[0], [k], 2)
         if k < panels - 3:
-            send(times(fresh, third).astype(BF16), [k], 3)
-        if 0 < k < panels - 3:
-            kept = later_products(z, z == k - 1, previous, whole, kept)
+            send(after[1], [k], 3)
         previous = fresh
         for distance, senders in FAR_SENDS.get(k, ()):
             send(kept[distance - 4], senders, distance)

time: 218 us -> 215 us (0.986)
  matrix products: 21.7 us -> 13.7 us
  Pallas kernels: 7.48 us -> 12.4 us
    dot_general x27 -> x16, matrix products: 21.7 us -> 13.7 us  [times(): lax.dot_general(left, weight, (((1,), (1,)), ((), ())), preferred_element...]
    pallas_call x4 -> x6, Pallas kernels: 7.48 us -> 12.4 us  [stage_products(): pl.pallas_call(stage_body, grid_spec=pltpu.PrefetchScalarGridSpec(num_sca...]
  transfers between devices with their start and end apart: 36 -> 36, of which waited for: 9 -> 8; matrix products, arithmetic and copies ran while one was open for 13% -> 10% of each run, Pallas kernels for 3% -> 6%
where the time goes in v6:
time: 215 us; the launch traced here: 214 us
  waiting for transfers between devices  96.1 us (45%)
  starting transfers between devices  58.5 us (27%)
  between operations  14.8 us (7%)
  matrix products  13.7 us (6%)
  Pallas kernels  12.4 us (6%)
  local copies, waits for them, and re-layouts  9.37 us (4%)
  other arithmetic  8.98 us (4%)
    all_gather x1, waiting for transfers between devices, per_device(): whole = lax.all_gather(coupling[0], ROWS).reshape(panels, width, width)  55.8 us
    ppermute x23, starting transfers between devices, send(): moved = lax.ppermute(value, 'panel', [(s, s + distance) for s in senders])  24.5 us
    ppermute x7, starting transfers between devices, per_device(): moved = lax.ppermute(part(lax.rem(z + distance, panels)), 'panel', route)  14.9 us
    all_to_all x1, waiting for transfers between devices, per_device(): lax.all_to_all(jnp.broadcast_to(solved[None], (chips, share, width)), 'ch...  14.9 us
    dot_general x16, matrix products, times(): lax.dot_general(left, weight, (((1,), (1,)), ((), ())), preferred_element...  13.7 us
    ppermute x7, waiting for transfers between devices, per_device(): moved = lax.ppermute(part(lax.rem(z + distance, panels)), 'panel', route)  12.9 us
    pallas_call x6, Pallas kernels, stage_products(): pl.pallas_call(stage_body, grid_spec=pltpu.PrefetchScalarGridSpec(num_sca...  12.4 us
    all_to_all x1, waiting for transfers between devices, per_device(): pieces = lax.all_to_all(pieces, ROWS, 0, 0, tiled=True)  11.5 us
  transfers between devices with their start and end apart: 36, of which 8 were waited for; matrix products, arithmetic and copies ran while one was open for 10% of the time, Pallas kernels for 6%

profile of v6, /device:TPU:1, one launch (start us, length us, event | category | flops | bytes accessed | tf_op | source)
XLA Modules:
  0.0 213.7 jit_solution(12500568021588695109)
XLA Ops:
  7.2 0.7 all-gather.2.cloned.1.call-update
  8.6 2.3 %bitcast_multiply_fusion = bf16[512,1024]{1,0:T(8,128)(2,1)} fusion(bf16[1,4,128,1024]{3,2,1,0:T(8,128)(2,1)} %param.10, bf16[512]{0:T(512)(128)(2,1)S(1)} %broadcast_bitcast_fusion), kind=kLoop, calls=%fused_computation.35 | loop fusion | flops 524288 | bytes 2098176 | tf_op jit(solution)/shard_map/mul | solution.py:135
  11.0 3.2 %collective-permute-start = (bf16[512,1024]{1,0:T(8,128)(2,1)}, bf16[512,1024]{1,0:T(8,128)(2,1)S(1)}, u32[]{:S(2)}, u32[]{:S(2)}) collective-permute-start(bf16[512,1024]{1,0:T(8,128)(2,1)} %bitcast_multiply_fusion), channel_id=1, source_target_pairs={{0,1},{1,0},{2,3},{3,2},{4,5},{5,4},{6,7},{7,6},{8,9},{9,8},{10,11... | collective-permute-start | bytes 3145736 | tf_op jit(solution)/shard_map/ppermute | solution.py:133
  14.2 2.0 copy.24
  16.3 5.5 %all-to-all-start = ((bf16[32,32,256]{2,1,0:T(8,128)(2,1)}), bf16[32,32,256]{2,1,0:T(8,128)(2,1)}, u32[]{:S(2)}, u32[]{:S(2)}) async-start(bf16[32,32,256]{2,1,0:T(8,128)(2,1)} %bitcast.2), calls=%async_computation | async-start | bytes 1048576 | tf_op jit(solution)/shard_map/all_to_all | solution.py:128
  21.9 11.5 %all-to-all-done = bf16[32,32,256]{2,1,0:T(8,128)(2,1)} async-done(((bf16[32,32,256]{2,1,0:T(8,128)(2,1)}), bf16[32,32,256]{2,1,0:T(8,128)(2,1)}, u32[]{:S(2)}, u32[]{:S(2)}) %all-to-all-start) | async-done | bytes 524320 | tf_op jit(solution)/shard_map/all_to_all | solution.py:128
  33.4 0.9 convert_bitcast_fusion.1
  34.3 2.9 %pad_maximum_fusion = bf16[1024,1024]{1,0:T(8,128)(2,1)} fusion(bf16[512,1024]{1,0:T(8,128)(2,1)S(1)} %collective-permute-done, bf16[512,1024]{1,0:T(8,128)(2,1)} %bitcast_multiply_fusion), kind=kLoop, calls=%fused_computation | loop fusion | flops 4194304 | bytes 4194304 | tf_op jit(solution)/shard_map/concatenate | solution.py:138
  37.2 0.7 fusion.16.fresh_ref.previous_ref
  37.9 55.8 %all-gather.2.cloned.1.call-done = bf16[32,256,1024]{2,1,0:T(8,128)(2,1)} async-done(((bf16[1,256,1024]{2,1,0:T(8,128)(2,1)}), bf16[32,256,1024]{2,1,0:T(8,128)(2,1)}) %all-gather.2.cloned.1.call-update) | async-done | bytes 16777232 | tf_op jit(solution)/shard_map/all_gather | solution.py:124
  93.6 1.8 dynamic-slice_bitcast_fusion
  95.4 0.7 convolution_convert_fusion.7
  96.1 3.2 %collective-permute-start.2 = (bf16[32,1024]{1,0:T(8,128)(2,1)S(1)}, bf16[32,1024]{1,0:T(8,128)(2,1)S(1)}, u32[]{:S(2)}, u32[]{:S(2)}) collective-permute-start(bf16[32,1024]{1,0:T(8,128)(2,1)S(1)} %convolution_convert_fusion.7), channel_id=1, source_target_pairs={{0,32},{1,33},{2,34},{3,35},{4,36},{5,37},{6,38},{7,39},{8,40},{9,... | collective-permute-start | bytes 196616 | tf_op jit(solution)/shard_map/ppermute | solution.py:154
  99.4 3.7 %stage_products.6 = (bf16[32,1024]{1,0:T(8,128)(2,1)S(1)}, bf16[32,1024]{1,0:T(8,128)(2,1)S(1)}, bf16[4,32,1024]{2,1,0:T(8,128)(2,1)S(1)}) custom-call(s32[3]{0:T(128)S(1)} %get-tuple-element.106.place_ref, bf16[32,1024]{1,0:T(8,128)(2,1)S(1)} %fusion.16.fresh_ref.previous_ref, ...), custom_call_target="tpu_custom_call", output_to_operand_aliasing={{2}: (4, {})} | custom-call | tf_op jit(solution)/shard_map/stage_products/pallas_call | solution.py:88
  103.1 1.3 collective-permute-start.4
  104.4 0.7 fusion.19.fresh_ref.previous_ref
  105.1 0.7 convolution_convert_fusion.6
  105.9 0.7 collective-permute-start.5
  106.6 1.3 collective-permute-start.1
  107.9 5.5 %stage_products.7 = (bf16[32,1024]{1,0:T(8,128)(2,1)S(1)}, bf16[32,1024]{1,0:T(8,128)(2,1)S(1)}, bf16[4,32,1024]{2,1,0:T(8,128)(2,1)S(1)}) custom-call(s32[3]{0:T(128)S(1)} %get-tuple-element.107.place_ref, bf16[32,1024]{1,0:T(8,128)(2,1)S(1)} %fusion.19.fresh_ref.previous_ref, ...), custom_call_target="tpu_custom_call", output_to_operand_aliasing={{2}: (4, {})} | custom-call | tf_op jit(solution)/shard_map/stage_products/pallas_call | solution.py:88
  114.1 0.7 collective-permute-start.8
  114.8 0.7 fusion.22.fresh_ref.previous_ref
  115.5 0.7 convolution_convert_fusion.5
  116.2 0.7 collective-permute-start.6
  117.6 1.3 collective-permute-start.10
  118.9 0.7 collective-permute-start.9
  119.6 0.7 collective-permute-start.15
  120.2 0.7 fusion.25.fresh_ref.previous_ref
  121.0 0.7 convolution_convert_fusion.4
  121.7 0.7 collective-permute-start.11
  123.0 1.3 collective-permute-start.7
  124.4 0.7 collective-permute-start.16
  125.0 0.8 collective-permute-start.20
  125.9 0.7 fusion.28.fresh_ref.previous_ref
  126.6 0.7 convolution_convert_fusion.3
  127.4 0.7 collective-permute-start.17
  128.7 1.3 collective-permute-start.14
  130.0 0.7 collective-permute-start.13
  131.4 0.7 fusion.31.fresh_ref
  132.1 0.7 convolution_convert_fusion.2
  132.9 0.7 collective-permute-start.22
  133.5 1.3 stage_products.11
  135.5 4.0 %collective-permute-start.19 = (bf16[32,1024]{1,0:T(8,128)(2,1)S(1)}, bf16[32,1024]{1,0:T(8,128)(2,1)S(1)}, u32[]{:S(2)}, u32[]{:S(2)}) collective-permute-start(bf16[32,1024]{1,0:T(8,128)(2,1)S(1)} %slice_bitcast_fusion), channel_id=1, source_target_pairs={{0,224},{1,225},{2,226},{3,227},{4,228},{5,229},{6,230},{7,231},{8... | collective-permute-start | bytes 196616 | tf_op jit(solution)/shard_map/ppermute | solution.py:154
  140.2 0.7 fusion.34
  140.9 0.7 convolution_convert_fusion.1
  141.7 0.7 collective-permute-start.23
  142.4 0.7 fusion.40
  143.1 1.1 broadcast_in_dim.91
  144.3 4.8 %all-to-all-start.1 = ((bf16[16,32,1024]{2,1,0:T(8,128)(2,1)}), bf16[16,32,1024]{2,1,0:T(8,128)(2,1)S(1)}, u32[]{:S(2)}, u32[]{:S(2)}) async-start(bf16[16,32,1024]{2,1,0:T(8,128)(2,1)} %broadcast_in_dim.91), calls=%async_computation.1 | async-start | bytes 2097152 | tf_op jit(solution)/shard_map/all_to_all | solution.py:177
  149.1 14.9 %all-to-all-done.1 = bf16[16,32,1024]{2,1,0:T(8,128)(2,1)S(1)} async-done(((bf16[16,32,1024]{2,1,0:T(8,128)(2,1)}), bf16[16,32,1024]{2,1,0:T(8,128)(2,1)S(1)}, u32[]{:S(2)}, u32[]{:S(2)}) %all-to-all-start.1) | async-done | bytes 1048608 | tf_op jit(solution)/shard_map/all_to_all | solution.py:177
  164.0 2.9 %convolution_convert_fusion = bf16[512,1024]{1,0:T(8,128)(2,1)S(1)} fusion(bf16[512,1024]{1,0:T(8,128)(2,1)S(1)} %bitcast.145, bf16[1024,1024]{1,0:T(8,128)(2,1)} %pad_maximum_fusion), kind=kOutput, calls=%fused_computation.18 | convolution fusion | flops 1074266112 | bytes 4194304 | tf_op jit(solution)/shard_map/dot_general | solution.py:21
  166.9 1.0 dynamic-slice_bitcast_fusion.7
  167.9 4.8 %collective-permute-start.31 = (bf16[64,1024]{1,0:T(8,128)(2,1)}, bf16[64,1024]{1,0:T(8,128)(2,1)}, u32[]{:S(2)}, u32[]{:S(2)}) collective-permute-start(bf16[64,1024]{1,0:T(8,128)(2,1)} %get-tuple-element.93), channel_id=1, source_target_pairs={{0,128},{32,160},{64,192},{96,224},{128,0},{160,32},{192,64},{224,... | collective-permute-start | bytes 393224 | tf_op jit(solution)/shard_map/ppermute | solution.py:189
  173.0 4.9 %collective-permute-start.24 = (bf16[8,64,32]{1,0,2:T(8,128)(2,1)S(1)}, bf16[8,64,32]{1,0,2:T(8,128)(2,1)S(1)}, u32[]{:S(2)}, u32[]{:S(2)}) collective-permute-start(bf16[8,64,32]{1,0,2:T(8,128)(2,1)S(1)} %copy.31), channel_id=1, source_target_pairs={{0,1},{1,0},{2,3},{3,2},{4,5},{5,4},{6,7},{7,6},{8,9},{9,8},{10,11... | collective-permute-start | bytes 98312 | tf_op jit(solution)/shard_map/ppermute | solution.py:133
  177.9 5.0 %collective-permute-start.29 = (bf16[64,1024]{1,0:T(8,128)(2,1)}, bf16[64,1024]{1,0:T(8,128)(2,1)S(1)}, u32[]{:S(2)}, u32[]{:S(2)}) collective-permute-start(bf16[64,1024]{1,0:T(8,128)(2,1)} %get-tuple-element.95), channel_id=1, source_target_pairs={{0,96},{32,128},{64,160},{96,192},{128,224},{160,0},{192,32},{224,... | collective-permute-start | bytes 393224 | tf_op jit(solution)/shard_map/ppermute | solution.py:189
  182.8 2.7 %collective-permute-start.28 = (bf16[64,1024]{1,0:T(8,128)(2,1)}, bf16[64,1024]{1,0:T(8,128)(2,1)S(1)}, u32[]{:S(2)}, u32[]{:S(2)}) collective-permute-start(bf16[64,1024]{1,0:T(8,128)(2,1)} %get-tuple-element.96), channel_id=1, source_target_pairs={{0,192},{32,224},{64,0},{96,32},{128,64},{160,96},{192,128},{224,1... | collective-permute-start | bytes 393224 | tf_op jit(solution)/shard_map/ppermute | solution.py:189
  186.0 1.9 collective-permute-start.26
  188.1 1.0 copy.29
  190.2 2.1 collective-permute-done.29
  192.9 7.2 %collective-permute-done.27 = bf16[64,1024]{1,0:T(8,128)(2,1)S(1)} collective-permute-done((bf16[64,1024]{1,0:T(8,128)(2,1)}, bf16[64,1024]{1,0:T(8,128)(2,1)S(1)}, u32[]{:S(2)}, u32[]{:S(2)}) %collective-permute-start.27) | collective-permute-done | bytes 131104 | tf_op jit(solution)/shard_map/ppermute | solution.py:189
  200.1 2.9 %collective-permute-done.25 = bf16[64,1024]{1,0:T(8,128)(2,1)} collective-permute-done((bf16[64,1024]{1,0:T(8,128)(2,1)S(1)}, bf16[64,1024]{1,0:T(8,128)(2,1)}, u32[]{:S(2)}, u32[]{:S(2)}) %collective-permute-start.25) | collective-permute-done | bytes 131104 | tf_op jit(solution)/shard_map/ppermute | solution.py:189
  203.1 1.3 fusion.48
  205.0 0.7 convert_bitcast_fusion
  206.1 0.8 copy.30
  (72 shorter events, 9.4 us)
Async XLA Ops:
  7.2 30.0 %copy-start = (bf16[1,1024,1024]{2,1,0:T(8,128)(2,1)S(1)}, bf16[1,1024,1024]{2,1,0:T(8,128)(2,1)}, u32[]{:S(2)}) copy-start(bf16[1,1024,1024]{2,1,0:T(8,128)(2,1)} %param.8) | copy-start | bytes 6291460
  7.2 86.5 %all-gather.2.cloned.1.call-start = ((), (), s32[]{:S(2)}) async-start(), calls=%async_computation.2 | async-start | bytes 17301504 | tf_op jit(solution)/shard_map/all_gather | solution.py:124
  11.0 23.3 %collective-permute-start = (bf16[512,1024]{1,0:T(8,128)(2,1)}, bf16[512,1024]{1,0:T(8,128)(2,1)S(1)}, u32[]{:S(2)}, u32[]{:S(2)}) collective-permute-start(bf16[512,1024]{1,0:T(8,128)(2,1)} %bitcast_multiply_fusion), channel_id=1, source_target_pairs={{0,1},{1,0},{2,3},{3,2},{4,5},{5,4},{6,7},{7,6},{8,9},{9,8},{10,11... | collective-permute-start | bytes 3145736 | tf_op jit(solution)/shard_map/ppermute | solution.py:133
  16.3 17.1 %all-to-all-start = ((bf16[32,32,256]{2,1,0:T(8,128)(2,1)}), bf16[32,32,256]{2,1,0:T(8,128)(2,1)}, u32[]{:S(2)}, u32[]{:S(2)}) async-start(bf16[32,32,256]{2,1,0:T(8,128)(2,1)} %bitcast.2), calls=%async_computation | async-start | bytes 1048576 | tf_op jit(solution)/shard_map/all_to_all | solution.py:128
  96.1 8.3 %collective-permute-start.2 = (bf16[32,1024]{1,0:T(8,128)(2,1)S(1)}, bf16[32,1024]{1,0:T(8,128)(2,1)S(1)}, u32[]{:S(2)}, u32[]{:S(2)}) collective-permute-start(bf16[32,1024]{1,0:T(8,128)(2,1)S(1)} %convolution_convert_fusion.7), channel_id=1, source_target_pairs={{0,32},{1,33},{2,34},{3,35},{4,36},{5,37},{6,38},{7,39},{8,40},{9,... | collective-permute-start | bytes 196616 | tf_op jit(solution)/shard_map/ppermute | solution.py:154
  103.1 11.6 %collective-permute-start.4 = (bf16[32,1024]{1,0:T(8,128)(2,1)S(1)}, bf16[32,1024]{1,0:T(8,128)(2,1)S(1)}, u32[]{:S(2)}, u32[]{:S(2)}) collective-permute-start(bf16[32,1024]{1,0:T(8,128)(2,1)S(1)} %get-tuple-element.54), channel_id=1, source_target_pairs={{0,64},{1,65},{2,66},{3,67},{4,68},{5,69},{6,70},{7,71},{8,72},{9,... | collective-permute-start | bytes 196616 | tf_op jit(solution)/shard_map/ppermute | solution.py:154
  105.9 8.9 %collective-permute-start.5 = (bf16[32,1024]{1,0:T(8,128)(2,1)S(1)}, bf16[32,1024]{1,0:T(8,128)(2,1)S(1)}, u32[]{:S(2)}, u32[]{:S(2)}) collective-permute-start(bf16[32,1024]{1,0:T(8,128)(2,1)S(1)} %convolution_convert_fusion.6), channel_id=1, source_target_pairs={{32,64},{33,65},{34,66},{35,67},{36,68},{37,69},{38,70},{39,71},{4... | collective-permute-start | bytes 196616 | tf_op jit(solution)/shard_map/ppermute | solution.py:154
  106.6 12.2 %collective-permute-start.1 = (bf16[32,1024]{1,0:T(8,128)(2,1)S(1)}, bf16[32,1024]{1,0:T(8,128)(2,1)S(1)}, u32[]{:S(2)}, u32[]{:S(2)}) collective-permute-start(bf16[32,1024]{1,0:T(8,128)(2,1)S(1)} %get-tuple-element.47), channel_id=1, source_target_pairs={{0,96},{1,97},{2,98},{3,99},{4,100},{5,101},{6,102},{7,103},{8,104... | collective-permute-start | bytes 196616 | tf_op jit(solution)/shard_map/ppermute | solution.py:154
  113.4 6.2 %collective-permute-start.3 = (bf16[32,1024]{1,0:T(8,128)(2,1)S(1)}, bf16[32,1024]{1,0:T(8,128)(2,1)S(1)}, u32[]{:S(2)}, u32[]{:S(2)}) collective-permute-start(bf16[32,1024]{1,0:T(8,128)(2,1)S(1)} %get-tuple-element.53), channel_id=1, source_target_pairs={{32,96},{33,97},{34,98},{35,99},{36,100},{37,101},{38,102},{39,103... | collective-permute-start | bytes 196616 | tf_op jit(solution)/shard_map/ppermute | solution.py:154
  114.1 9.0 %collective-permute-start.8 = (bf16[32,1024]{1,0:T(8,128)(2,1)S(1)}, bf16[32,1024]{1,0:T(8,128)(2,1)S(1)}, u32[]{:S(2)}, u32[]{:S(2)}) collective-permute-start(bf16[32,1024]{1,0:T(8,128)(2,1)S(1)} %get-tuple-element.66), channel_id=1, source_target_pairs={{32,128},{33,129},{34,130},{35,131},{36,132},{37,133},{38,134},{39... | collective-permute-start | bytes 196616 | tf_op jit(solution)/shard_map/ppermute | solution.py:154
  116.2 4.0 %collective-permute-start.6 = (bf16[32,1024]{1,0:T(8,128)(2,1)S(1)}, bf16[32,1024]{1,0:T(8,128)(2,1)S(1)}, u32[]{:S(2)}, u32[]{:S(2)}) collective-permute-start(bf16[32,1024]{1,0:T(8,128)(2,1)S(1)} %convolution_convert_fusion.5), channel_id=1, source_target_pairs={{64,96},{65,97},{66,98},{67,99},{68,100},{69,101},{70,102},{71,103... | collective-permute-start | bytes 196616 | tf_op jit(solution)/shard_map/ppermute | solution.py:154
  117.6 6.8 %collective-permute-start.10 = (bf16[32,1024]{1,0:T(8,128)(2,1)S(1)}, bf16[32,1024]{1,0:T(8,128)(2,1)S(1)}, u32[]{:S(2)}, u32[]{:S(2)}) collective-permute-start(bf16[32,1024]{1,0:T(8,128)(2,1)S(1)} %slice_bitcast_fusion.3), channel_id=1, source_target_pairs={{0,128},{32,160},{1,129},{33,161},{2,130},{34,162},{3,131},{35,163... | collective-permute-start | bytes 196616 | tf_op jit(solution)/shard_map/ppermute | solution.py:154
  118.9 6.2 %collective-permute-start.9 = (bf16[32,1024]{1,0:T(8,128)(2,1)S(1)}, bf16[32,1024]{1,0:T(8,128)(2,1)S(1)}, u32[]{:S(2)}, u32[]{:S(2)}) collective-permute-start(bf16[32,1024]{1,0:T(8,128)(2,1)S(1)} %get-tuple-element.67), channel_id=1, source_target_pairs={{64,128},{65,129},{66,130},{67,131},{68,132},{69,133},{70,134},{71... | collective-permute-start | bytes 196616 | tf_op jit(solution)/shard_map/ppermute | solution.py:154
  119.6 9.2 %collective-permute-start.15 = (bf16[32,1024]{1,0:T(8,128)(2,1)S(1)}, bf16[32,1024]{1,0:T(8,128)(2,1)S(1)}, u32[]{:S(2)}, u32[]{:S(2)}) collective-permute-start(bf16[32,1024]{1,0:T(8,128)(2,1)S(1)} %get-tuple-element.74), channel_id=1, source_target_pairs={{64,160},{65,161},{66,162},{67,163},{68,164},{69,165},{70,166},{71... | collective-permute-start | bytes 196616 | tf_op jit(solution)/shard_map/ppermute | solution.py:154
  121.7 4.2 %collective-permute-start.11 = (bf16[32,1024]{1,0:T(8,128)(2,1)S(1)}, bf16[32,1024]{1,0:T(8,128)(2,1)S(1)}, u32[]{:S(2)}, u32[]{:S(2)}) collective-permute-start(bf16[32,1024]{1,0:T(8,128)(2,1)S(1)} %convolution_convert_fusion.4), channel_id=1, source_target_pairs={{96,128},{97,129},{98,130},{99,131},{100,132},{101,133},{102,134},... | collective-permute-start | bytes 196616 | tf_op jit(solution)/shard_map/ppermute | solution.py:154
  123.0 7.0 %collective-permute-start.7 = (bf16[32,1024]{1,0:T(8,128)(2,1)S(1)}, bf16[32,1024]{1,0:T(8,128)(2,1)S(1)}, u32[]{:S(2)}, u32[]{:S(2)}) collective-permute-start(bf16[32,1024]{1,0:T(8,128)(2,1)S(1)} %slice_bitcast_fusion.4), channel_id=1, source_target_pairs={{0,160},{32,192},{64,224},{1,161},{33,193},{65,225},{2,162},{34,19... | collective-permute-start | bytes 196616 | tf_op jit(solution)/shard_map/ppermute | solution.py:154
  124.4 6.4 %collective-permute-start.16 = (bf16[32,1024]{1,0:T(8,128)(2,1)S(1)}, bf16[32,1024]{1,0:T(8,128)(2,1)S(1)}, u32[]{:S(2)}, u32[]{:S(2)}) collective-permute-start(bf16[32,1024]{1,0:T(8,128)(2,1)S(1)} %get-tuple-element.75), channel_id=1, source_target_pairs={{96,160},{97,161},{98,162},{99,163},{100,164},{101,165},{102,166},... | collective-permute-start | bytes 196616 | tf_op jit(solution)/shard_map/ppermute | solution.py:154
  125.0 9.8 %collective-permute-start.20 = (bf16[32,1024]{1,0:T(8,128)(2,1)S(1)}, bf16[32,1024]{1,0:T(8,128)(2,1)S(1)}, u32[]{:S(2)}, u32[]{:S(2)}) collective-permute-start(bf16[32,1024]{1,0:T(8,128)(2,1)S(1)} %get-tuple-element.82), channel_id=1, source_target_pairs={{96,192},{97,193},{98,194},{99,195},{100,196},{101,197},{102,198},... | collective-permute-start | bytes 196616 | tf_op jit(solution)/shard_map/ppermute | solution.py:154
  127.4 4.0 %collective-permute-start.17 = (bf16[32,1024]{1,0:T(8,128)(2,1)S(1)}, bf16[32,1024]{1,0:T(8,128)(2,1)S(1)}, u32[]{:S(2)}, u32[]{:S(2)}) collective-permute-start(bf16[32,1024]{1,0:T(8,128)(2,1)S(1)} %convolution_convert_fusion.3), channel_id=1, source_target_pairs={{128,160},{129,161},{130,162},{131,163},{132,164},{133,165},{134,1... | collective-permute-start | bytes 196616 | tf_op jit(solution)/shard_map/ppermute | solution.py:154
  128.7 6.8 %collective-permute-start.14 = (bf16[32,1024]{1,0:T(8,128)(2,1)S(1)}, bf16[32,1024]{1,0:T(8,128)(2,1)S(1)}, u32[]{:S(2)}, u32[]{:S(2)}) collective-permute-start(bf16[32,1024]{1,0:T(8,128)(2,1)S(1)} %get-tuple-element.104), channel_id=1, source_target_pairs={{0,192},{32,224},{1,193},{33,225},{2,194},{34,226},{3,195},{35,227... | collective-permute-start | bytes 196616 | tf_op jit(solution)/shard_map/ppermute | solution.py:154
  130.0 9.5 %collective-permute-start.13 = (bf16[32,1024]{1,0:T(8,128)(2,1)S(1)}, bf16[32,1024]{1,0:T(8,128)(2,1)S(1)}, u32[]{:S(2)}, u32[]{:S(2)}) collective-permute-start(bf16[32,1024]{1,0:T(8,128)(2,1)S(1)} %get-tuple-element.103), channel_id=1, source_target_pairs={{64,192},{96,224},{65,193},{97,225},{66,194},{98,226},{67,195},{99... | collective-permute-start | bytes 196616 | tf_op jit(solution)/shard_map/ppermute | solution.py:154
  130.7 9.5 %collective-permute-start.21 = (bf16[32,1024]{1,0:T(8,128)(2,1)S(1)}, bf16[32,1024]{1,0:T(8,128)(2,1)S(1)}, u32[]{:S(2)}, u32[]{:S(2)}) collective-permute-start(bf16[32,1024]{1,0:T(8,128)(2,1)S(1)} %get-tuple-element.83), channel_id=1, source_target_pairs={{128,192},{129,193},{130,194},{131,195},{132,196},{133,197},{134,1... | collective-permute-start | bytes 196616 | tf_op jit(solution)/shard_map/ppermute | solution.py:154
  132.9 7.4 %collective-permute-start.22 = (bf16[32,1024]{1,0:T(8,128)(2,1)S(1)}, bf16[32,1024]{1,0:T(8,128)(2,1)S(1)}, u32[]{:S(2)}, u32[]{:S(2)}) collective-permute-start(bf16[32,1024]{1,0:T(8,128)(2,1)S(1)} %convolution_convert_fusion.2), channel_id=1, source_target_pairs={{160,192},{161,193},{162,194},{163,195},{164,196},{165,197},{166,1... | collective-permute-start | bytes 196616 | tf_op jit(solution)/shard_map/ppermute | solution.py:154
  134.8 7.5 %collective-permute-start.12 = (bf16[32,1024]{1,0:T(8,128)(2,1)S(1)}, bf16[32,1024]{1,0:T(8,128)(2,1)S(1)}, u32[]{:S(2)}, u32[]{:S(2)}) collective-permute-start(bf16[32,1024]{1,0:T(8,128)(2,1)S(1)} %get-tuple-element.72), channel_id=1, source_target_pairs={{128,224},{129,225},{130,226},{131,227},{132,228},{133,229},{134,2... | collective-permute-start | bytes 196616 | tf_op jit(solution)/shard_map/ppermute | solution.py:154
  135.5 6.8 %collective-permute-start.19 = (bf16[32,1024]{1,0:T(8,128)(2,1)S(1)}, bf16[32,1024]{1,0:T(8,128)(2,1)S(1)}, u32[]{:S(2)}, u32[]{:S(2)}) collective-permute-start(bf16[32,1024]{1,0:T(8,128)(2,1)S(1)} %slice_bitcast_fusion), channel_id=1, source_target_pairs={{0,224},{1,225},{2,226},{3,227},{4,228},{5,229},{6,230},{7,231},{8... | collective-permute-start | bytes 196616 | tf_op jit(solution)/shard_map/ppermute | solution.py:154
  139.5 2.9 %collective-permute-start.18 = (bf16[32,1024]{1,0:T(8,128)(2,1)S(1)}, bf16[32,1024]{1,0:T(8,128)(2,1)S(1)}, u32[]{:S(2)}, u32[]{:S(2)}) collective-permute-start(bf16[32,1024]{1,0:T(8,128)(2,1)S(1)} %get-tuple-element.80), channel_id=1, source_target_pairs={{160,224},{161,225},{162,226},{163,227},{164,228},{165,229},{166,2... | collective-permute-start | bytes 196616 | tf_op jit(solution)/shard_map/ppermute | solution.py:154
  141.7 0.7 collective-permute-start.23
  144.3 19.8 %all-to-all-start.1 = ((bf16[16,32,1024]{2,1,0:T(8,128)(2,1)}), bf16[16,32,1024]{2,1,0:T(8,128)(2,1)S(1)}, u32[]{:S(2)}, u32[]{:S(2)}) async-start(bf16[16,32,1024]{2,1,0:T(8,128)(2,1)} %broadcast_in_dim.91), calls=%async_computation.1 | async-start | bytes 2097152 | tf_op jit(solution)/shard_map/all_to_all | solution.py:177
  166.9 5.9 %copy-start.1 = (bf16[512,1024]{1,0:T(8,128)(2,1)}, bf16[512,1024]{1,0:T(8,128)(2,1)S(1)}, u32[]{:S(2)}) copy-start(bf16[512,1024]{1,0:T(8,128)(2,1)S(1)} %convolution_convert_fusion) | copy-start | bytes 3145732
  167.9 18.1 %collective-permute-start.31 = (bf16[64,1024]{1,0:T(8,128)(2,1)}, bf16[64,1024]{1,0:T(8,128)(2,1)}, u32[]{:S(2)}, u32[]{:S(2)}) collective-permute-start(bf16[64,1024]{1,0:T(8,128)(2,1)} %get-tuple-element.93), channel_id=1, source_target_pairs={{0,128},{32,160},{64,192},{96,224},{128,0},{160,32},{192,64},{224,... | collective-permute-start | bytes 393224 | tf_op jit(solution)/shard_map/ppermute | solution.py:189
  172.7 15.2 %collective-permute-start.30 = (bf16[64,1024]{1,0:T(8,128)(2,1)}, bf16[64,1024]{1,0:T(8,128)(2,1)}, u32[]{:S(2)}, u32[]{:S(2)}) collective-permute-start(bf16[64,1024]{1,0:T(8,128)(2,1)} %get-tuple-element.94), channel_id=1, source_target_pairs={{0,160},{32,192},{64,224},{96,0},{128,32},{160,64},{192,96},{224,1... | collective-permute-start | bytes 393224 | tf_op jit(solution)/shard_map/ppermute | solution.py:189
  173.0 12.5 %collective-permute-start.24 = (bf16[8,64,32]{1,0,2:T(8,128)(2,1)S(1)}, bf16[8,64,32]{1,0,2:T(8,128)(2,1)S(1)}, u32[]{:S(2)}, u32[]{:S(2)}) collective-permute-start(bf16[8,64,32]{1,0,2:T(8,128)(2,1)S(1)} %copy.31), channel_id=1, source_target_pairs={{0,1},{1,0},{2,3},{3,2},{4,5},{5,4},{6,7},{7,6},{8,9},{9,8},{10,11... | collective-permute-start | bytes 98312 | tf_op jit(solution)/shard_map/ppermute | solution.py:133
  177.9 14.4 %collective-permute-start.29 = (bf16[64,1024]{1,0:T(8,128)(2,1)}, bf16[64,1024]{1,0:T(8,128)(2,1)S(1)}, u32[]{:S(2)}, u32[]{:S(2)}) collective-permute-start(bf16[64,1024]{1,0:T(8,128)(2,1)} %get-tuple-element.95), channel_id=1, source_target_pairs={{0,96},{32,128},{64,160},{96,192},{128,224},{160,0},{192,32},{224,... | collective-permute-start | bytes 393224 | tf_op jit(solution)/shard_map/ppermute | solution.py:189
  182.8 10.1 %collective-permute-start.28 = (bf16[64,1024]{1,0:T(8,128)(2,1)}, bf16[64,1024]{1,0:T(8,128)(2,1)S(1)}, u32[]{:S(2)}, u32[]{:S(2)}) collective-permute-start(bf16[64,1024]{1,0:T(8,128)(2,1)} %get-tuple-element.96), channel_id=1, source_target_pairs={{0,192},{32,224},{64,0},{96,32},{128,64},{160,96},{192,128},{224,1... | collective-permute-start | bytes 393224 | tf_op jit(solution)/shard_map/ppermute | solution.py:189
  185.5 14.7 %collective-permute-start.27 = (bf16[64,1024]{1,0:T(8,128)(2,1)}, bf16[64,1024]{1,0:T(8,128)(2,1)S(1)}, u32[]{:S(2)}, u32[]{:S(2)}) collective-permute-start(bf16[64,1024]{1,0:T(8,128)(2,1)} %get-tuple-element.97), channel_id=1, source_target_pairs={{0,64},{32,96},{64,128},{96,160},{128,192},{160,224},{192,0},{224,... | collective-permute-start | bytes 393224 | tf_op jit(solution)/shard_map/ppermute | solution.py:189
  186.0 14.2 %collective-permute-start.26 = (bf16[64,1024]{1,0:T(8,128)(2,1)}, bf16[64,1024]{1,0:T(8,128)(2,1)S(1)}, u32[]{:S(2)}, u32[]{:S(2)}) collective-permute-start(bf16[64,1024]{1,0:T(8,128)(2,1)} %get-tuple-element.98), channel_id=1, source_target_pairs={{0,224},{32,0},{64,32},{96,64},{128,96},{160,128},{192,160},{224,1... | collective-permute-start | bytes 393224 | tf_op jit(solution)/shard_map/ppermute | solution.py:189
  187.9 15.2 %collective-permute-start.25 = (bf16[64,1024]{1,0:T(8,128)(2,1)S(1)}, bf16[64,1024]{1,0:T(8,128)(2,1)}, u32[]{:S(2)}, u32[]{:S(2)}) collective-permute-start(bf16[64,1024]{1,0:T(8,128)(2,1)S(1)} %get-tuple-element.92), channel_id=1, source_target_pairs={{0,32},{32,64},{64,96},{96,128},{128,160},{160,192},{192,224},{224... | collective-permute-start | bytes 393224 | tf_op jit(solution)/shard_map/ppermute | solution.py:189
  204.4 1.6 collective-permute-start.32
Sparse Core Ops, SparseCore 0:
  10.6 83.0 all-gather.1
